TPU v7x, 128 devices: a whole 4x4x4 slice. The times are simulated.
128 devices in a mesh: wave: 16 (over x, z_hi, core), lev: 8 (over y, z_lo).
Axes of the slice: x: 4, y: 4, z: 4 (z_hi: 2, z_lo: 2; z = z_hi * 2 + z_lo), core: 2. Of those that a mesh axis runs over, the one named last changes fastest.
Arguments:
- spectra: bfloat16 [1280, 1280, 2, 32], P(('wave', 'lev')), may hold values from -0.125 to 0.125
- legendre: bfloat16 [1280, 640, 1280], P(('wave', 'lev')), may hold values from -0.15625 to 0.15625
- gauss_weights: float32 [640], replicated, may hold values from 0.25 to 1.75
- phys_matrix: float32 [32, 32], replicated, may hold values from -1 to 1
- phys_bias: float32 [32], replicated, may hold values from -3 to 3
- tracers: float32 [8, 64, 320, 640], P(None, None, 'wave', 'lev'), may hold values from 0.2 to 5
- reaction: float32 [64, 64], replicated, may hold values from -0.375 to 0.375
- heat_coeff: float32 [64], replicated, may hold values from -0.625 to 0.625
Outputs:
- spectral_tend: bfloat16 [1280, 1280, 2, 32], P(('wave', 'lev'))
- mixing: float32 [8, 64, 320, 640], P(None, None, 'wave', 'lev')
All inputs are finite; a program needn't handle non-finite values.
Results may differ from a plain program's by a relative error of at most 0.007.
Values may be sent and summed in bfloat16 or wider, within the bound.
No kernel may reach another device: no remote copies, remote signals or barrier semaphores. Data moves between devices by JAX's collectives and lax.ppermute only.
A program may use at most 192 MiB of HBM per device.

v0:
```python
import functools
import math

import jax
import jax.numpy as jnp
from jax import lax
from jax.experimental import pallas as pl
from jax.experimental.pallas import tpu as pltpu
from jax.sharding import PartitionSpec as P

TRUNC = 1280
NLON = 2560
SUBSTEPS = 2
COURANT = 0.6
LANES = 128
PIECE_ROWS = 64
HALO = 2
BF, F32 = jnp.bfloat16, jnp.float32


TABLE_ROWS = 160


def table_kernel(cos_ref, sin_ref, sign_ref, a_ref, b_ref, inverse_ref, direct_ref):
    rows = cos_ref.shape[0]
    cos, sin, sign = cos_ref[...], sin_ref[...], sign_ref[...]
    first = (lax.broadcasted_iota(jnp.int32, cos.shape, 0) == 0) & (pl.program_id(0) == 0)
    factor = jnp.where(first, 1.0, 2.0)
    scale = 1.0 / math.sqrt(NLON)
    for block in range(NLON // LANES):
        part = slice(block * LANES, (block + 1) * LANES)
        value = cos * a_ref[:, part] - sin * b_ref[:, part]
        if block % 2:
            value = value * sign
        inverse_ref[:, part] = (value * factor).astype(BF)
        direct_ref[:, part] = (value * scale).astype(BF)


def fourier_tables(owners, m_count):
    unit = 2.0 * math.pi / NLON
    owner = jnp.arange(owners, dtype=jnp.int32)
    lane = jnp.arange(LANES, dtype=jnp.int32)
    coarse = (m_count * owner[:, None] * lane[None, :] % NLON).astype(F32) * unit
    sign = jnp.where(owner % 2 == 1, -1.0, 1.0).astype(F32)[:, None]
    rows = 2 * m_count
    per_row = lambda value: jnp.broadcast_to(value[:, None, :], (owners, rows, LANES)).reshape(-1, LANES)
    inner = jnp.arange(m_count, dtype=jnp.int32)[:, None]
    fine = (inner * jnp.arange(NLON, dtype=jnp.int32)[None, :] % NLON).astype(F32) * unit
    cos, sin = jnp.cos(fine), jnp.sin(fine)
    repeat = TABLE_ROWS // rows
    a = jnp.tile(jnp.concatenate([cos, -sin]), (repeat, 1))
    b = jnp.tile(jnp.concatenate([sin, cos]), (repeat, 1))
    row_spec = pl.BlockSpec((TABLE_ROWS, LANES), lambda i: (i, 0))
    all_spec = pl.BlockSpec((TABLE_ROWS, NLON), lambda i: (0, 0))
    out_spec = pl.BlockSpec((TABLE_ROWS, NLON), lambda i: (i, 0))
    shape = jax.ShapeDtypeStruct((owners * rows, NLON), BF)
    return pl.pallas_call(
        table_kernel,
        grid=(owners * rows // TABLE_ROWS,),
        in_specs=[row_spec] * 3 + [all_spec] * 2,
        out_specs=[out_spec] * 2,
        out_shape=[shape] * 2,
        cost_estimate=pl.CostEstimate(flops=12 * TRUNC * NLON, bytes_accessed=8 * TRUNC * NLON, transcendentals=0),
        name="fourier_tables",
    )(per_row(jnp.cos(coarse)), per_row(jnp.sin(coarse)), per_row(jnp.broadcast_to(sign, coarse.shape)), a, b)


def swapped(x):
    shape = x.shape
    x = x.reshape(-1, 8, LANES)
    row = lax.broadcasted_iota(jnp.int32, x.shape, 1)
    block = lax.broadcasted_iota(jnp.int32, x.shape, 2) // 32
    for bit in (2, 1):
        span = 32 * bit
        low, high = (row & bit) == 0, (block & bit) == 0
        from_below = pltpu.roll(pltpu.roll(x, 8 - bit, 1), span, 2)
        from_above = pltpu.roll(pltpu.roll(x, bit, 1), LANES - span, 2)
        x = jnp.where(low == high, x, jnp.where(low, from_below, from_above))
    return x.reshape(shape)


def kept(m, shape, part_rows):
    row = lax.broadcasted_iota(jnp.int32, shape, 0)
    k = lax.broadcasted_iota(jnp.int32, shape, 1)
    return (k < TRUNC - m) & ((row < part_rows) | (m > 0)), k % 2 == 0


def inverse_kernel(geometry, first_ref, spec_ref, leg_ref, out_ref, z_ref, q_ref):
    waves, levs, groups, bands, band_groups, m_count = geometry
    half_rows = leg_ref.shape[1]
    step = pl.program_id(0)
    spec = spec_ref[0].astype(F32)
    keep, even = kept(first_ref[0] + step, spec.shape, spec.shape[0] // 2)
    spec = jnp.where(keep, spec, 0.0)
    stacked = jnp.concatenate([spec, jnp.where(even, spec, -spec)], axis=0).astype(BF)
    values = lax.dot_general(leg_ref[0], stacked, (((1,), (1,)), ((), ())), preferred_element_type=F32)
    z_ref[pl.ds(step * half_rows, half_rows), :] = swapped(values)

    @pl.when(step == m_count - 1)
    def _():
        q_ref[...] = jnp.zeros_like(q_ref)

        def of_wave(wave, carry):
            south = (wave >= bands).astype(jnp.int32)
            band = jnp.where(wave >= bands, waves - 1 - wave, wave)
            for lev in range(levs):
                for g in range(groups):
                    at = band * band_groups + (lev * groups + g - HALO)
                    over = at >= bands * band_groups
                    line = jnp.where(over, 2 * bands * band_groups - 1 - at, jnp.maximum(at, 0))
                    base = line * 4 + jnp.where(over, 1 - south, south) * 2
                    for c in range(2):
                        row = (g * 2 + c) * m_count
                        q_ref[lev, row : row + m_count] = z_ref[pl.ds(base + c, m_count, stride=half_rows), :]
                out_ref[wave * levs + lev] = q_ref[lev].astype(BF)
            return carry

        lax.fori_loop(0, waves, of_wave, 0)


def direct_kernel(geometry, first_ref, values_ref, weights_ref, leg_ref, out_ref, z_ref, q_ref):
    waves, levs, groups, bands, band_groups, m_count = geometry
    half_rows = leg_ref.shape[1]
    step = pl.program_id(0)

    @pl.when(step == 0)
    def _():
        def of_wave(wave, carry):
            south = (wave >= bands).astype(jnp.int32)
            band = jnp.where(wave >= bands, waves - 1 - wave, wave)
            for lev in range(levs):
                q_ref[lev] = values_ref[wave * levs + lev].astype(F32)
                for g in range(groups):
                    inside = lev * groups + g - HALO
                    if 0 <= inside < band_groups:
                        base = (band * band_groups + inside) * 4 + south * 2
                        for c in range(2):
                            row = (g * 2 + c) * m_count
                            z_ref[pl.ds(base + c, m_count, stride=half_rows), :] = q_ref[lev, row : row + m_count]
            return carry

        lax.fori_loop(0, waves, of_wave, 0)

    x = swapped(z_ref[pl.ds(step * half_rows, half_rows), :])
    y = pltpu.roll(x, LANES // 2, 1)
    north = lane_ids(x.shape) < LANES // 2
    paired = (weights_ref[...] * jnp.where(north, x + y, y - x)).astype(BF)
    folded = lax.dot_general(paired, leg_ref[0], (((0,), (0,)), ((), ())), preferred_element_type=F32)
    half = folded.shape[0] // 2
    keep, even = kept(first_ref[0] + step, (half, folded.shape[1]), half // 2)
    chosen = jnp.where(even, folded[:half], folded[half:])
    out_ref[0] = jnp.where(keep, chosen, 0.0).astype(BF)


def legendre_call(kernel, name, first, operands, in_specs, out_spec, out_shape, geometry, legendre):
    m_count, half_rows, k_count = legendre.shape
    levs = geometry[1]
    return pl.pallas_call(
        functools.partial(kernel, geometry),
        grid=(m_count,),
        in_specs=[pl.BlockSpec(memory_space=pltpu.SMEM)]
        + in_specs
        + [pl.BlockSpec((1, half_rows, k_count), lambda m: (m, 0, 0))],
        out_specs=out_spec,
        out_shape=out_shape,
        scratch_shapes=[
            pltpu.VMEM((m_count * half_rows, LANES), F32),
            pltpu.VMEM((levs, PIECE_ROWS, LANES), F32),
        ],
        cost_estimate=pl.CostEstimate(
            flops=2 * legendre.size * LANES, bytes_accessed=2 * legendre.size + 5 * 10**6, transcendentals=0
        ),
        name=name,
    )(first.reshape(1), *operands, legendre)


def lane_ids(shape):
    return lax.broadcasted_iota(jnp.int32, shape, len(shape) - 1)


def edge_columns_kernel(tr_ref, head_ref, tail_ref, pad):
    rows, count, cols = tr_ref.shape[1:]
    lanes = lane_ids((count, LANES))
    head = jnp.zeros((count, LANES), F32)
    tail = head
    pad[:, :, :cols] = tr_ref[0]
    for r in range(rows):
        line = pad[r]
        here = (lanes >> 1) == r
        head = jnp.where(here, pltpu.roll(line, 2 * r, 1), head)
        tail = jnp.where(here, pltpu.roll(line, (2 * r - cols + 2) % LANES, 1), tail)
    head_ref[0] = head
    tail_ref[0] = tail


def with_columns(line, r, west, east, cols, lanes):
    line = jnp.where((lanes >> 1) == cols // 2, pltpu.roll(east, (cols - 2 * r) % LANES, 1), line)
    return jnp.where((lanes >> 1) == LANES // 2 - 1, pltpu.roll(west, (LANES - 2 - 2 * r) % LANES, 1), line)


def edge_rows_kernel(rows, first_ref, last_ref, west_ref, east_ref, top_ref, low_ref):
    count, cols = first_ref.shape[2:]
    lanes = lane_ids((count, LANES))
    west, east = west_ref[0], east_ref[0]
    for at in range(HALO):
        for src, out, r in ((first_ref, top_ref, at), (last_ref, low_ref, rows - HALO + at)):
            out[0, at, :, :cols] = src[0, at]
            out[0, at] = with_columns(out[0, at], r, west, east, cols, lanes)


def chemistry_kernel(
    total_rows, first_ref, tr_ref, north_ref, south_ref, west_ref, east_ref, u_ref, v_ref, react_ref, heat_ref,
    mix_ref, heating_ref, x_ref, y_ref, coef_ref,
):
    rows, tracers, cols = tr_ref.shape[1:]
    deep = rows + 2 * HALO
    lanes = lane_ids((tracers, LANES))
    west, east = west_ref[0], east_ref[0]
    for at in range(HALO):
        x_ref[at] = north_ref[0, at]
        x_ref[rows + HALO + at] = south_ref[0, at]
    x_ref[HALO : HALO + rows, :, :cols] = tr_ref[0]
    for r in range(rows):
        x_ref[HALO + r] = with_columns(x_ref[HALO + r], r, west, east, cols, lanes)
    u, v = u_ref[0], v_ref[0]
    face_u = 0.5 * (u + pltpu.roll(u, LANES - 1, 1))
    east_up, east_down = COURANT * jnp.maximum(face_u, 0.0), COURANT * jnp.minimum(face_u, 0.0)
    face_v = 0.5 * (v + pltpu.roll(v, deep - 1, 0))
    row = first_ref[0] - HALO + lax.broadcasted_iota(jnp.int32, face_v.shape, 0)
    face_v = jnp.where((row >= 0) & (row + 1 <= total_rows - 1), face_v, 0.0)
    south_up, south_down = COURANT * jnp.maximum(face_v, 0.0), COURANT * jnp.minimum(face_v, 0.0)
    coef_ref[0] = 1.0 - east_up + pltpu.roll(east_down, 1, 1) - south_up + pltpu.roll(south_down, 1, 0)
    coef_ref[1] = -east_down
    coef_ref[2] = pltpu.roll(east_up, 1, 1)
    coef_ref[3] = -south_down
    coef_ref[4] = pltpu.roll(south_up, 1, 0)
    react = react_ref[...]

    def moved(src, r):
        q = src[r]
        return (
            coef_ref[0, r : r + 1] * q
            + coef_ref[1, r : r + 1] * pltpu.roll(q, LANES - 1, 1)
            + coef_ref[2, r : r + 1] * pltpu.roll(q, 1, 1)
            + coef_ref[3, r : r + 1] * src[r + 1]
            + coef_ref[4, r : r + 1] * src[r - 1]
        )

    def step(src, r):
        both = jnp.concatenate([moved(src, r), moved(src, r + 1)], axis=1)
        high = both.astype(BF)
        low = (both - high.astype(F32)).astype(BF)
        return both + jnp.dot(react, jnp.concatenate([high, high, low], axis=0), preferred_element_type=F32)

    for r in range(1, deep - 1, 2):
        both = step(x_ref, r)
        y_ref[r] = both[:, :LANES]
        y_ref[r + 1] = both[:, LANES:]
    heat = heat_ref[...]
    heating_ref[0] = jnp.zeros_like(heating_ref[0])
    for r in range(HALO, rows + HALO, 2):
        both = step(y_ref, r)
        for at in range(2):
            one = both[:, at * LANES : (at + 1) * LANES]
            mix_ref[0, r - HALO + at] = one[:, :cols]
            heating_ref[0, r + at : r + at + 1] = jnp.sum(heat * one, axis=0, keepdims=True)


def shift(value, axis, by):
    count = lax.axis_size(axis)
    return lax.ppermute(value, axis, [(i, (i + by) % count) for i in range(count)])


def tracer_halos(tracers):
    levels, rows, count, cols = tracers.shape
    tr_spec = pl.BlockSpec((1, rows, count, cols), lambda l: (l, 0, 0, 0))
    col_spec = pl.BlockSpec((1, count, LANES), lambda l: (l, 0, 0))
    row_spec = pl.BlockSpec((1, HALO, count, LANES), lambda l: (l, 0, 0, 0))
    col_shape = jax.ShapeDtypeStruct((levels, count, LANES), F32)
    row_shape = jax.ShapeDtypeStruct((levels, HALO, count, LANES), F32)
    head, tail = pl.pallas_call(
        edge_columns_kernel,
        grid=(levels,),
        in_specs=[tr_spec],
        out_specs=[col_spec] * 2,
        out_shape=[col_shape] * 2,
        scratch_shapes=[pltpu.VMEM((rows, count, LANES), F32)],
        cost_estimate=pl.CostEstimate(flops=10**7, bytes_accessed=7 * 10**6, transcendentals=0),
        name="edge_columns",
    )(tracers)
    west = shift(tail, "lev", 1)
    east = shift(head, "lev", -1)
    top, low = pl.pallas_call(
        functools.partial(edge_rows_kernel, rows),
        grid=(levels,),
        in_specs=[
            pl.BlockSpec((1, HALO, count, cols), lambda l: (l, 0, 0, 0)),
            pl.BlockSpec((1, HALO, count, cols), lambda l: (l, rows // HALO - 1, 0, 0)),
            col_spec,
            col_spec,
        ],
        out_specs=[row_spec] * 2,
        out_shape=[row_shape] * 2,
        cost_estimate=pl.CostEstimate(flops=10**6, bytes_accessed=2 * 10**6, transcendentals=0),
        name="edge_rows",
    )(tracers, tracers, west, east)
    return shift(low, "wave", 1), shift(top, "wave", -1), west, east


def chemistry(tracers, halos, winds, reaction, heat_coeff, row_first, total_rows):
    levels, rows, count, cols = tracers.shape
    deep = rows + 2 * HALO
    high = reaction.astype(BF)
    low = (reaction - high.astype(F32)).astype(BF)
    react = jnp.concatenate([high, low, high], axis=1)
    heat = jnp.broadcast_to(heat_coeff[:, None], (count, LANES))
    tr_spec = pl.BlockSpec((1, rows, count, cols), lambda l: (l, 0, 0, 0))
    col_spec = pl.BlockSpec((1, count, LANES), lambda l: (l, 0, 0))
    row_spec = pl.BlockSpec((1, HALO, count, LANES), lambda l: (l, 0, 0, 0))
    whole = lambda shape: pl.BlockSpec(shape, lambda l: (0,) * len(shape))
    return pl.pallas_call(
        functools.partial(chemistry_kernel, total_rows),
        grid=(levels,),
        in_specs=[
            pl.BlockSpec(memory_space=pltpu.SMEM),
            tr_spec,
            row_spec,
            row_spec,
            col_spec,
            col_spec,
            pl.BlockSpec((1, deep, LANES), lambda l: (l, 0, 0)),
            pl.BlockSpec((1, deep, LANES), lambda l: (l + levels, 0, 0)),
            whole(react.shape),
            whole(heat.shape),
        ],
        out_specs=[tr_spec, pl.BlockSpec((1, deep, LANES), lambda l: (l, 0, 0))],
        out_shape=[
            jax.ShapeDtypeStruct(tracers.shape, F32),
            jax.ShapeDtypeStruct((levels, deep, LANES), F32),
        ],
        scratch_shapes=[
            pltpu.VMEM((deep, count, LANES), F32),
            pltpu.VMEM((deep, count, LANES), F32),
            pltpu.VMEM((5, deep, LANES), F32),
        ],
        cost_estimate=pl.CostEstimate(flops=10**9, bytes_accessed=16 * 10**6, transcendentals=0),
        name="chemistry",
    )(row_first.reshape(1), tracers, *halos, winds, winds, react, heat)


def body(spectra, legendre, gauss_weights, phys_matrix, phys_bias, tracers, reaction, heat_coeff):
    waves = lax.axis_size("wave")
    levs = lax.axis_size("lev")
    both = ("wave", "lev")
    wave, lev = lax.axis_index("wave"), lax.axis_index("lev")
    m_count, k_count, _, fields = spectra.shape
    half_rows = legendre.shape[1]
    levels, _, chem_rows, chem_cols = tracers.shape
    ratio = NLON // (chem_cols * levs)
    bands = waves // 2
    groups = (chem_rows + 2 * HALO) // levs
    south = wave >= bands
    width = 2 * fields

    owners = waves * levs
    geometry = (waves, levs, groups, bands, chem_rows, m_count)
    first_m = (wave * levs + lev) * m_count
    piece_shape = (owners, PIECE_ROWS, LANES)
    piece_spec = pl.BlockSpec(piece_shape, lambda m: (0, 0, 0))
    spec_spec = pl.BlockSpec((1, width, k_count), lambda m: (m, 0, 0))
    used = groups * 2 * m_count
    tracers = tracers.transpose(0, 2, 1, 3)

    pieces = legendre_call(
        inverse_kernel,
        "to_latitude",
        first_m,
        [spectra.transpose(0, 2, 3, 1).reshape(m_count, width, k_count)],
        [spec_spec],
        piece_spec,
        jax.ShapeDtypeStruct(piece_shape, BF),
        geometry,
        legendre,
    )
    spread = lax.all_to_all(pieces, both, split_axis=0, concat_axis=0, tiled=True)
    halos = tracer_halos(tracers)
    inverse, direct = fourier_tables(owners, m_count)
    spread = spread[:, :used].reshape(owners, groups, 2 * m_count, LANES).transpose(0, 2, 1, 3)
    spread = spread.reshape(2 * TRUNC, groups * LANES)

    grid = lax.dot_general(spread, inverse, (((0,), (0,)), ((), ())), preferred_element_type=F32).astype(BF)
    grid = grid.reshape(groups, ratio, fields, NLON)

    lane = jnp.arange(LANES, dtype=jnp.int32)
    column = jnp.where(lane < LANES - HALO, lane, lane - LANES)
    column = (column[None, :] + chem_cols * jnp.arange(levs, dtype=jnp.int32)[:, None]) % (chem_cols * levs)
    held = (lane < chem_cols + HALO) | (lane >= LANES - HALO)
    column = jnp.where(held[None, :], column, -1).reshape(levs * LANES)
    cell = jnp.arange(NLON, dtype=jnp.int32) // ratio
    mean = jnp.where(cell[:, None] == column[None, :], 1.0 / ratio**2, 0.0).astype(BF)
    winds = jnp.einsum("gqfj,jx->gfx", grid[:, :, : 2 * levels], mean, preferred_element_type=F32)
    winds = winds.reshape(groups * 2 * levels, levs, LANES).transpose(1, 0, 2)
    winds = lax.all_to_all(winds, "lev", split_axis=0, concat_axis=0, tiled=True)
    winds = winds.reshape(levs * groups, 2 * levels, LANES)
    winds = jnp.where(south, jnp.flip(winds, axis=0), winds).transpose(1, 0, 2)

    mixing, heating = chemistry(
        tracers, halos, winds, reaction, heat_coeff, wave * chem_rows, chem_rows * waves
    )
    heating = heating.transpose(1, 0, 2)
    heating = jnp.where(south, jnp.flip(heating, axis=0), heating).reshape(levs, groups * levels, LANES)
    heating = lax.all_to_all(heating, "lev", split_axis=0, concat_axis=0, tiled=True)
    heating = heating.reshape(levs, groups, levels, LANES)[..., :chem_cols].transpose(1, 2, 0, 3)
    heating = jnp.repeat(heating.reshape(groups, 1, levels, levs * chem_cols), ratio, axis=3)

    physics = jnp.tanh(
        jnp.einsum("ef,gqfj->gqej", phys_matrix, grid.astype(F32), precision=lax.Precision.HIGHEST)
        + phys_bias[:, None]
    )
    tendency = jnp.concatenate(
        [physics[:, :, : 2 * levels], physics[:, :, 2 * levels : 3 * levels] + heating, physics[:, :, 3 * levels :]],
        axis=2,
    ).astype(BF)

    tendency = tendency.reshape(groups * ratio * fields, NLON)
    coeffs = lax.dot_general(direct, tendency, (((1,), (1,)), ((), ())), preferred_element_type=F32).astype(BF)
    coeffs = coeffs.reshape(owners, 2 * m_count, groups, LANES).transpose(0, 2, 1, 3).reshape(owners, used, LANES)
    coeffs = jnp.pad(coeffs, ((0, 0), (0, PIECE_ROWS - used), (0, 0)))
    values = lax.all_to_all(coeffs, both, split_axis=0, concat_axis=0, tiled=True)

    result = legendre_call(
        direct_kernel,
        "to_spectral",
        first_m,
        [values, jnp.broadcast_to(gauss_weights[:, None], (half_rows, LANES))],
        [piece_spec, pl.BlockSpec((half_rows, LANES), lambda m: (0, 0))],
        spec_spec,
        jax.ShapeDtypeStruct((m_count, width, k_count), BF),
        geometry,
        legendre,
    )
    result = result.reshape(m_count, 2, fields, k_count).transpose(0, 3, 1, 2)
    mixing = mixing.transpose(0, 2, 1, 3)
    return (result, mixing)


def solution(mesh):
    return jax.shard_map(
        body,
        mesh=mesh,
        in_specs=(
            P(("wave", "lev"), None, None, None),
            P(("wave", "lev"), None, None),
            P(),
            P(),
            P(),
            P(None, None, "wave", "lev"),
            P(),
            P(),
        ),
        out_specs=(P(("wave", "lev"), None, None, None), P(None, None, "wave", "lev")),
        check_vma=False,
    )
```

profile of v0, /device:TPU:1, one launch (start us, length us, event | category | flops | bytes accessed | tf_op | source)
XLA Modules:
  0.0 223.6 jit_solution(6035407184282347215)
XLA Ops:
  0.7 17.9 %to_latitude.1 = bf16[128,64,128]{2,1,0:T(8,128)(2,1)} custom-call(s32[1]{0:T(128)} %bitcast.first_ref, bf16[10,64,1280]{2,1,0:T(8,128)(2,1)} %bitcast.70, bf16[10,640,1280]{2,1,0:T(8,128)(2,1)} %leg_ref.3), custom_call_target="tpu_custom_call" | custom-call | flops 2097152000 | bytes 21384000 | tf_op jit(solution)/shard_map/to_latitude/pallas_call | solution.py:158
  18.5 11.5 %all-to-all-start = ((bf16[128,64,128]{2,1,0:T(8,128)(2,1)}), bf16[128,64,128]{2,1,0:T(8,128)(2,1)S(1)}, u32[]{:S(2)}, u32[]{:S(2)}) async-start(bf16[128,64,128]{2,1,0:T(8,128)(2,1)} %to_latitude.1), calls=%async_computation | async-start | bytes 4194304 | tf_op jit(solution)/shard_map/all_to_all | solution.py:385
  30.0 7.4 %edge_columns.1 = (f32[8,64,128]{2,1,0:T(8,128)}, f32[8,64,128]{2,1,0:T(8,128)}) custom-call(f32[8,20,64,80]{3,2,1,0:T(8,128)} %bitcast.54), custom_call_target="tpu_custom_call" | custom-call | flops 10000000 | bytes 7000000 | tf_op jit(solution)/shard_map/edge_columns/pallas_call | solution.py:281
  37.4 1.5 collective-permute-start
  38.9 2.3 %collective-permute-start.1 = (f32[8,64,128]{2,1,0:T(8,128)}, f32[8,64,128]{2,1,0:T(8,128)S(1)}, u32[]{:S(2)}, u32[]{:S(2)}) collective-permute-start(f32[8,64,128]{2,1,0:T(8,128)} %get-tuple-element.13), channel_id=1, source_target_pairs={{0,7},{1,0},{2,1},{3,2},{4,3},{5,4},{6,5},{7,6},{8,15},{9,8},{10,9... | collective-permute-start | bytes 786440 | tf_op jit(solution)/shard_map/ppermute | solution.py:271
  41.2 0.3 fusion.23
  41.6 0.6 fusion.18
  42.2 0.7 fusion.15
  43.0 1.5 tile.20
  44.5 2.7 %tile.21.b_ref = f32[160,2560]{1,0:T(8,128)} reshape(f32[8,20,2560]{2,1,0:T(8,128)} %tile.20) | data formatting | bytes 3276800 | tf_op jit(solution)/shard_map/tile | solution.py:52
  47.2 1.5 tile.8
  48.7 2.7 %tile.9.a_ref = f32[160,2560]{1,0:T(8,128)} reshape(f32[8,20,2560]{2,1,0:T(8,128)} %tile.8) | data formatting | bytes 3276800 | tf_op jit(solution)/shard_map/tile | solution.py:51
  51.4 1.3 broadcast_in_dim.40
  52.6 2.4 %reshape.195.cos_ref = f32[2560,128]{1,0:T(8,128)} reshape(f32[128,20,128]{2,1,0:T(8,128)} %broadcast_in_dim.40) | data formatting | bytes 2621440 | tf_op jit(solution)/shard_map/reshape | solution.py:46
  55.1 1.3 broadcast_in_dim.41
  56.3 2.5 %reshape.196.sin_ref = f32[2560,128]{1,0:T(8,128)} reshape(f32[128,20,128]{2,1,0:T(8,128)} %broadcast_in_dim.41) | data formatting | bytes 2621440 | tf_op jit(solution)/shard_map/reshape | solution.py:46
  59.0 1.5 broadcast_in_dim_broadcast_in_dim_broadcast_in_dim.11.sign_ref
  60.4 18.9 %fourier_tables.1 = (bf16[2560,2560]{1,0:T(8,128)(2,1)}, bf16[2560,2560]{1,0:T(8,128)(2,1)}) custom-call(f32[2560,128]{1,0:T(8,128)} %reshape.195.cos_ref, f32[2560,128]{1,0:T(8,128)} %reshape.196.sin_ref, f32[2560,128]{1,0:T(8,128)} %broadcast_in_dim_broadcast_in_dim_broadcast_in_dim.11.sign_ref, f32[160,2560]{1,0:T(8,128)} %tile.9.a_ref, ...), custom_call_target="tpu_custom_call" | custom-call | flops 39321600 | bytes 26214400 | tf_op jit(solution)/shard_map/fourier_tables/pallas_call | solution.py:57
  79.5 0.7 copy-done.2
  80.2 0.7 copy-done.3
  80.9 5.5 %edge_rows.1 = (f32[8,2,64,128]{3,2,1,0:T(8,128)}, f32[8,2,64,128]{3,2,1,0:T(8,128)}) custom-call(f32[8,20,64,80]{3,2,1,0:T(8,128)} %bitcast.55, f32[8,20,64,80]{3,2,1,0:T(8,128)} %bitcast.56, f32[8,64,128]{2,1,0:T(8,128)} %copy-done.2, f32[8,64,128]{2,1,0:T(8,128)} %copy-done.3), custom_call_target="tpu_custom_call" | custom-call | flops 1000000 | bytes 2000000 | tf_op jit(solution)/shard_map/edge_rows/pallas_call | solution.py:293
  86.3 3.9 %collective-permute-start.2 = (f32[8,2,64,128]{3,2,1,0:T(8,128)}, f32[8,2,64,128]{3,2,1,0:T(8,128)S(1)}, u32[]{:S(2)}, u32[]{:S(2)}) collective-permute-start(f32[8,2,64,128]{3,2,1,0:T(8,128)} %get-tuple-element.14), channel_id=1, source_target_pairs={{0,8},{8,16},{16,24},{24,32},{32,40},{40,48},{48,56},{56,64},{64,7... | collective-permute-start | bytes 1572872 | tf_op jit(solution)/shard_map/ppermute | solution.py:271
  90.2 1.3 copy.19
  91.5 1.7 copy.20
  93.2 8.9 %convolution_convert_fusion = bf16[384,2560]{1,0:T(8,128)(2,1)S(1)} fusion(bf16[2560,2560]{1,0:T(8,128)(2,1)} %get-tuple-element.11, bf16[320,8,3,128]{3,2,1,0:T(4,128)(2,1)S(1)} %bitcast.66), kind=kOutput, calls=%fused_computation.9 | convolution fusion | flops 5034147840 | bytes 17039360 | tf_op jit(solution)/shard_map/dot_general | solution.py:391
  102.3 2.4 %fusion.9 = f32[8,48,128]{2,1,0:T(8,128)} fusion(bf16[48,2560,1]{1,0,2:T(8,128)(2,1)S(1)} %bitcast.74, s32[8,128]{1,0:T(8,128)S(1)} %fusion.30, s32[2560]{0:T(1024)S(1)} %add_select_fusion.2), kind=kOutput, calls=%fused_computation.15 | convolution fusion | flops 259522560 | bytes 456704 | tf_op jit(solution)/shard_map/gqfj,jx->gfx/dot_general | solution.py:401
  104.7 3.4 %all-to-all-start.1 = ((f32[8,48,128]{2,1,0:T(8,128)}), f32[8,48,128]{2,1,0:T(8,128)S(1)}, u32[]{:S(2)}, u32[]{:S(2)}) async-start(f32[8,48,128]{2,1,0:T(8,128)} %fusion.9), calls=%async_computation.1 | async-start | bytes 393216 | tf_op jit(solution)/shard_map/all_to_all | solution.py:403
  108.1 0.7 pad_maximum_fusion.3.react_ref
  108.8 4.7 %all-to-all-done.1 = f32[8,48,128]{2,1,0:T(8,128)S(1)} async-done(((f32[8,48,128]{2,1,0:T(8,128)}), f32[8,48,128]{2,1,0:T(8,128)S(1)}, u32[]{:S(2)}, u32[]{:S(2)}) %all-to-all-start.1) | async-done | bytes 196640 | tf_op jit(solution)/shard_map/all_to_all | solution.py:403
  113.6 0.7 select_bitcast_fusion.u_ref.v_ref
  114.4 0.8 broadcast_in_dim.74.heat_ref
  115.2 14.2 %chemistry.1 = (f32[8,20,64,80]{3,2,1,0:T(8,128)}, f32[8,24,128]{2,1,0:T(8,128)}) custom-call(s32[1]{0:T(128)} %bitcast.9.first_ref, f32[8,20,64,80]{3,2,1,0:T(8,128)} %bitcast.57, f32[8,2,64,128]{3,2,1,0:T(8,128)} %copy-done.4, f32[8,2,64,128]{3,2,1,0:T(8,128)} %collective-permute-done.3.south_ref, f32[8,64,128]{2,1,0:T(8,128)} %copy-done.2, ...), custom_call_target="tpu_custom_call" | custom-call | flops 1000000000 | bytes 16000000 | tf_op jit(solution)/shard_map/chemistry/pallas_call | solution.py:321
  129.3 0.9 rev.9
  130.2 0.9 broadcast_select_fusion
  131.1 0.7 copy.23
  131.8 3.6 %all-to-all-start.2 = ((f32[8,24,128]{2,1,0:T(8,128)}), f32[8,24,128]{2,1,0:T(8,128)S(1)}, u32[]{:S(2)}, u32[]{:S(2)}) async-start(f32[8,24,128]{2,1,0:T(8,128)} %bitcast.17), calls=%async_computation.2 | async-start | bytes 196608 | tf_op jit(solution)/shard_map/all_to_all | solution.py:412
  135.4 4.0 %fusion.36 = (bf16[3,4,32,2560]{3,2,1,0:T(8,128)(2,1)S(1)}, f32[3,4,32,2560]{3,2,1,0:T(8,128)}) fusion(f32[32]{0:T(128)S(1)} %copy-done.8, bf16[3,4,32,2560]{3,2,1,0:T(8,128)(2,1)S(1)} %bitcast.64, f32[32,32]{1,0:T(8,128)S(1)} %copy-done), kind=kOutput, calls=%fused_computation.66 | convolution fusion | flops 379453440 | bytes 7868544 | tf_op jit(solution)/shard_map/ef,gqfj->gqej/dot_general | solution.py:417
  139.6 0.7 all-to-all-done.2
  140.6 2.5 %broadcast_in_dim.75 = f32[3,8,640,4]{1,3,2,0:T(4,128)} broadcast(f32[3,8,640]{1,2,0:T(8,128)S(1)} %bitcast.65), dimensions={0,1,2} | broadcast | bytes 307200 | tf_op jit(solution)/shard_map/broadcast_in_dim | solution.py:414
  143.1 2.7 %copy.26 = f32[3,8,2560]{2,1,0:T(8,128)S(1)} copy(f32[3,8,2560]{1,2,0:T(8,128)} %bitcast.58) | data formatting | bytes 491520 | tf_op jit(solution)/shard_map/broadcast_in_dim | solution.py:414
  145.8 1.3 fusion.10
  147.3 11.0 %convolution_convert_fusion.1 = bf16[2560,384]{1,0:T(8,128)(2,1)} fusion(bf16[2560,2560]{1,0:T(8,128)(2,1)} %get-tuple-element.10, bf16[384,2560]{1,0:T(8,128)(2,1)S(1)} %bitcast.67), kind=kOutput, calls=%fused_computation.10 | convolution fusion | flops 5034147840 | bytes 17039360 | tf_op jit(solution)/shard_map/dot_general | solution.py:426
  158.3 4.9 %reshape.206 = bf16[128,20,3,128]{3,2,1,0:T(4,128)(2,1)S(1)} reshape(bf16[2560,384]{1,0:T(8,128)(2,1)} %convolution_convert_fusion.1) | data formatting | bytes 3932160 | tf_op jit(solution)/shard_map/reshape | solution.py:427
  163.2 0.6 copy.27
  163.8 1.3 copy.28
  165.3 40.2 %all_to_all.20.values_ref = bf16[128,64,128]{2,1,0:T(8,128)(2,1)} all-to-all(bf16[128,64,128]{2,1,0:T(8,128)(2,1)S(1)} %pad.4), channel_id=1, replica_groups=mesh['wave'=16,'lev'=8] {'wave','lev'}, dimensions={0} | all-to-all | bytes 4194304 | tf_op jit(solution)/shard_map/all_to_all | solution.py:429
  205.5 0.9 broadcast_in_dim.77.weights_ref
  206.4 17.2 %to_spectral.1 = bf16[10,64,1280]{2,1,0:T(8,128)(2,1)} custom-call(s32[1]{0:T(128)} %bitcast.first_ref, bf16[128,64,128]{2,1,0:T(8,128)(2,1)} %all_to_all.20.values_ref, f32[640,128]{1,0:T(8,128)} %broadcast_in_dim.77.weights_ref, bf16[10,640,1280]{2,1,0:T(8,128)(2,1)} %leg_ref.3), custom_call_target="tpu_custom_call" | custom-call | flops 2097152000 | bytes 21384000 | tf_op jit(solution)/shard_map/to_spectral/pallas_call | solution.py:158
  (42 shorter events, 1.5 us)
Async XLA Ops:
  0.6 134.8 %copy-start = (f32[32,32]{1,0:T(8,128)S(1)}, f32[32,32]{1,0:T(8,128)}, u32[]{:S(2)}) copy-start(f32[32,32]{1,0:T(8,128)} %param.11) | copy-start | bytes 12292
  18.5 71.7 %all-to-all-start = ((bf16[128,64,128]{2,1,0:T(8,128)(2,1)}), bf16[128,64,128]{2,1,0:T(8,128)(2,1)S(1)}, u32[]{:S(2)}, u32[]{:S(2)}) async-start(bf16[128,64,128]{2,1,0:T(8,128)(2,1)} %to_latitude.1), calls=%async_computation | async-start | bytes 4194304 | tf_op jit(solution)/shard_map/all_to_all | solution.py:385
  37.4 42.0 %collective-permute-start = (f32[8,64,128]{2,1,0:T(8,128)}, f32[8,64,128]{2,1,0:T(8,128)S(1)}, u32[]{:S(2)}, u32[]{:S(2)}) collective-permute-start(f32[8,64,128]{2,1,0:T(8,128)} %get-tuple-element.12), channel_id=1, source_target_pairs={{0,1},{1,2},{2,3},{3,4},{4,5},{5,6},{6,7},{7,0},{8,9},{9,10},{10,1... | collective-permute-start | bytes 786440 | tf_op jit(solution)/shard_map/ppermute | solution.py:271
  38.9 40.6 %collective-permute-start.1 = (f32[8,64,128]{2,1,0:T(8,128)}, f32[8,64,128]{2,1,0:T(8,128)S(1)}, u32[]{:S(2)}, u32[]{:S(2)}) collective-permute-start(f32[8,64,128]{2,1,0:T(8,128)} %get-tuple-element.13), channel_id=1, source_target_pairs={{0,7},{1,0},{2,1},{3,2},{4,3},{5,4},{6,5},{7,6},{8,15},{9,8},{10,9... | collective-permute-start | bytes 786440 | tf_op jit(solution)/shard_map/ppermute | solution.py:271
  79.4 0.7 copy-start.2
  80.1 0.7 copy-start.3
  86.3 28.0 %collective-permute-start.2 = (f32[8,2,64,128]{3,2,1,0:T(8,128)}, f32[8,2,64,128]{3,2,1,0:T(8,128)S(1)}, u32[]{:S(2)}, u32[]{:S(2)}) collective-permute-start(f32[8,2,64,128]{3,2,1,0:T(8,128)} %get-tuple-element.14), channel_id=1, source_target_pairs={{0,8},{8,16},{16,24},{24,32},{32,40},{40,48},{48,56},{56,64},{64,7... | collective-permute-start | bytes 1572872 | tf_op jit(solution)/shard_map/ppermute | solution.py:271
  90.2 24.2 %collective-permute-start.3 = (f32[8,2,64,128]{3,2,1,0:T(8,128)}, f32[8,2,64,128]{3,2,1,0:T(8,128)}, u32[]{:S(2)}, u32[]{:S(2)}) collective-permute-start(f32[8,2,64,128]{3,2,1,0:T(8,128)} %get-tuple-element.15), channel_id=1, source_target_pairs={{0,120},{8,0},{16,8},{24,16},{32,24},{40,32},{48,40},{56,48},{64,5... | collective-permute-start | bytes 1572872 | tf_op jit(solution)/shard_map/ppermute | solution.py:271
  102.2 5.8 %copy-start.5 = (f32[64,64]{1,0:T(8,128)S(1)}, f32[64,64]{1,0:T(8,128)}, u32[]{:S(2)}) copy-start(f32[64,64]{1,0:T(8,128)} %param.14) | copy-start | bytes 49156
  102.3 12.1 %copy-start.7 = (f32[64]{0:T(128)S(1)}, f32[64]{0:T(128)}, u32[]{:S(2)}) copy-start(f32[64]{0:T(128)} %param.15) | copy-start | bytes 772
  104.7 8.9 %all-to-all-start.1 = ((f32[8,48,128]{2,1,0:T(8,128)}), f32[8,48,128]{2,1,0:T(8,128)S(1)}, u32[]{:S(2)}, u32[]{:S(2)}) async-start(f32[8,48,128]{2,1,0:T(8,128)} %fusion.9), calls=%async_computation.1 | async-start | bytes 393216 | tf_op jit(solution)/shard_map/all_to_all | solution.py:403
  114.4 0.8 copy-start.4
  115.2 20.2 %copy-start.8 = (f32[32]{0:T(128)S(1)}, f32[32]{0:T(128)}, u32[]{:S(2)}) copy-start(f32[32]{0:T(128)} %param.12) | copy-start | bytes 388
  131.8 8.4 %all-to-all-start.2 = ((f32[8,24,128]{2,1,0:T(8,128)}), f32[8,24,128]{2,1,0:T(8,128)S(1)}, u32[]{:S(2)}, u32[]{:S(2)}) async-start(f32[8,24,128]{2,1,0:T(8,128)} %bitcast.17), calls=%async_computation.2 | async-start | bytes 196608 | tf_op jit(solution)/shard_map/all_to_all | solution.py:412
  165.3 40.2 %copy-start.6 = (f32[640]{0:T(1024)S(1)}, f32[640]{0:T(1024)}, u32[]{:S(2)}) copy-start(f32[640]{0:T(1024)} %param.10) | copy-start | bytes 7684
  206.4 17.2 %copy-start.1 = (f32[32,32]{1,0:T(8,128)S(1)}, f32[32,32]{1,0:T(8,128)}, u32[]{:S(2)}) copy-start(f32[32,32]{1,0:T(8,128)} %param.11) | copy-start | bytes 12292
where the time goes:
time: 226 us; the launch traced here: 224 us
  Pallas kernels  81 us (36%)
  blocking collectives  40.2 us (18%)
  local copies, waits for them, and re-layouts  37.8 us (17%)
  matrix products  26.4 us (12%)
  starting transfers between devices  26.1 us (12%)
  other arithmetic  5.74 us (3%)
  waiting for transfers between devices  5.43 us (2%)
    all_to_all x1, blocking collectives, body(): lax.all_to_all(coeffs, both, split_axis=0, concat_axis=0, tiled=True)  40.2 us
    pallas_call x2, Pallas kernels, legendre_call(): pl.pallas_call(functools.partial(kernel, geometry), grid=(m_count,), in_s...  35.1 us
    pallas_call x1, Pallas kernels, fourier_tables(): pl.pallas_call(table_kernel, grid=(owners * rows // TABLE_ROWS,), in_spec...  18.9 us
    pallas_call x1, Pallas kernels, chemistry(): pl.pallas_call(functools.partial(chemistry_kernel, total_rows), grid=(lev...  14.2 us
    all_to_all x1, starting transfers between devices, body(): lax.all_to_all(pieces, both, split_axis=0, concat_axis=0, tiled=True)  11.5 us
    dot_general x1, matrix products, body(): lax.dot_general(direct, tendency, (((1,), (1,)), ((), ())), preferred_ele...  11 us
    dot_general x1, matrix products, body(): lax.dot_general(spread, inverse, (((0,), (0,)), ((), ())), preferred_elem...  8.93 us
    ppermute x4, starting transfers between devices, shift(): lax.ppermute(value, axis, [(i, (i + by) % count) for i in range(count)])  7.67 us
  transfers between devices with their start and end apart: 7, of which 2 were waited for; matrix products, arithmetic and copies ran while one was open for 18% of the time, Pallas kernels for 14%

commit v1 on v0

--- a/solution.py
+++ b/solution.py
@@ -18,65 +18,60 @@
 BF, F32 = jnp.bfloat16, jnp.float32
 
 
-TABLE_ROWS = 160
-
-
-def table_kernel(cos_ref, sin_ref, sign_ref, a_ref, b_ref, inverse_ref, direct_ref):
-    rows = cos_ref.shape[0]
-    cos, sin, sign = cos_ref[...], sin_ref[...], sign_ref[...]
-    first = (lax.broadcasted_iota(jnp.int32, cos.shape, 0) == 0) & (pl.program_id(0) == 0)
-    factor = jnp.where(first, 1.0, 2.0)
+def table_kernel(cos_ref, sin_ref, turned_cos_ref, turned_sin_ref, a_ref, b_ref, inverse_ref, direct_ref):
+    step = pl.program_id(0)
     scale = 1.0 / math.sqrt(NLON)
     for block in range(NLON // LANES):
         part = slice(block * LANES, (block + 1) * LANES)
-        value = cos * a_ref[:, part] - sin * b_ref[:, part]
-        if block % 2:
-            value = value * sign
-        inverse_ref[:, part] = (value * factor).astype(BF)
+        cos, sin = (turned_cos_ref, turned_sin_ref) if block % 2 else (cos_ref, sin_ref)
+        value = cos[...] * a_ref[0, :, part] - sin[...] * b_ref[0, :, part]
+        inverse_ref[:, part] = (value + value).astype(BF)
         direct_ref[:, part] = (value * scale).astype(BF)
+
+    @pl.when(step == 0)
+    def _():
+        top = inverse_ref[:16, :].astype(F32)
+        first = lax.broadcasted_iota(jnp.int32, top.shape, 0) == 0
+        inverse_ref[:16, :] = jnp.where(first, 0.5 * top, top).astype(BF)
 
 
 def fourier_tables(owners, m_count):
     unit = 2.0 * math.pi / NLON
-    owner = jnp.arange(owners, dtype=jnp.int32)
-    lane = jnp.arange(LANES, dtype=jnp.int32)
-    coarse = (m_count * owner[:, None] * lane[None, :] % NLON).astype(F32) * unit
-    sign = jnp.where(owner % 2 == 1, -1.0, 1.0).astype(F32)[:, None]
-    rows = 2 * m_count
-    per_row = lambda value: jnp.broadcast_to(value[:, None, :], (owners, rows, LANES)).reshape(-1, LANES)
+    owner = jnp.arange(owners, dtype=jnp.int32)[:, None]
+    lane = jnp.arange(LANES, dtype=jnp.int32)[None, :]
+    coarse = (m_count * owner * lane % NLON).astype(F32) * unit
+    cos_c, sin_c = jnp.cos(coarse), jnp.sin(coarse)
+    turn = jnp.where(owner % 2 == 1, -1.0, 1.0).astype(F32)
     inner = jnp.arange(m_count, dtype=jnp.int32)[:, None]
     fine = (inner * jnp.arange(NLON, dtype=jnp.int32)[None, :] % NLON).astype(F32) * unit
     cos, sin = jnp.cos(fine), jnp.sin(fine)
-    repeat = TABLE_ROWS // rows
-    a = jnp.tile(jnp.concatenate([cos, -sin]), (repeat, 1))
-    b = jnp.tile(jnp.concatenate([sin, cos]), (repeat, 1))
-    row_spec = pl.BlockSpec((TABLE_ROWS, LANES), lambda i: (i, 0))
-    all_spec = pl.BlockSpec((TABLE_ROWS, NLON), lambda i: (0, 0))
-    out_spec = pl.BlockSpec((TABLE_ROWS, NLON), lambda i: (i, 0))
+    a = jnp.concatenate([cos, -sin])
+    b = jnp.concatenate([sin, cos])
+    rows = 2 * m_count
+    coarse_spec = pl.BlockSpec((owners, LANES), lambda i: (0, 0))
+    fine_spec = pl.BlockSpec((1, 1, NLON), lambda i: (i, 0, 0))
+    out_spec = pl.BlockSpec((owners, NLON), lambda i: (i, 0))
     shape = jax.ShapeDtypeStruct((owners * rows, NLON), BF)
     return pl.pallas_call(
         table_kernel,
-        grid=(owners * rows // TABLE_ROWS,),
-        in_specs=[row_spec] * 3 + [all_spec] * 2,
+        grid=(rows,),
+        in_specs=[coarse_spec] * 4 + [fine_spec] * 2,
         out_specs=[out_spec] * 2,
         out_shape=[shape] * 2,
         cost_estimate=pl.CostEstimate(flops=12 * TRUNC * NLON, bytes_accessed=8 * TRUNC * NLON, transcendentals=0),
         name="fourier_tables",
-    )(per_row(jnp.cos(coarse)), per_row(jnp.sin(coarse)), per_row(jnp.broadcast_to(sign, coarse.shape)), a, b)
-
-
-def swapped(x):
-    shape = x.shape
-    x = x.reshape(-1, 8, LANES)
-    row = lax.broadcasted_iota(jnp.int32, x.shape, 1)
-    block = lax.broadcasted_iota(jnp.int32, x.shape, 2) // 32
-    for bit in (2, 1):
-        span = 32 * bit
-        low, high = (row & bit) == 0, (block & bit) == 0
-        from_below = pltpu.roll(pltpu.roll(x, 8 - bit, 1), span, 2)
-        from_above = pltpu.roll(pltpu.roll(x, bit, 1), LANES - span, 2)
-        x = jnp.where(low == high, x, jnp.where(low, from_below, from_above))
-    return x.reshape(shape)
+    )(cos_c, sin_c, turn * cos_c, turn * sin_c, a[:, None], b[:, None])
+
+
+def exchanged(x, turned):
+    lanes = lane_ids(x[0].shape)
+    low, even = lanes < 64, (lanes & 32) == 0
+    pairs = [(jnp.where(low, x[i], turned[i + 2]), jnp.where(low, turned[i], x[i + 2])) for i in range(2)]
+    out = []
+    for first, second in zip(*pairs):
+        out.append(jnp.where(even, first, pltpu.roll(second, 32, 1)))
+        out.append(jnp.where(even, pltpu.roll(first, LANES - 32, 1), second))
+    return out
 
 
 def kept(m, shape, part_rows):
@@ -85,16 +80,22 @@
     return (k < TRUNC - m) & ((row < part_rows) | (m > 0)), k % 2 == 0
 
 
-def inverse_kernel(geometry, first_ref, spec_ref, leg_ref, out_ref, z_ref, q_ref):
+def inverse_kernel(geometry, first_ref, spec_ref, leg_ref, out_ref, z_ref, q_ref, x_ref, turned_ref):
     waves, levs, groups, bands, band_groups, m_count = geometry
     half_rows = leg_ref.shape[1]
     step = pl.program_id(0)
     spec = spec_ref[0].astype(F32)
     keep, even = kept(first_ref[0] + step, spec.shape, spec.shape[0] // 2)
     spec = jnp.where(keep, spec, 0.0)
-    stacked = jnp.concatenate([spec, jnp.where(even, spec, -spec)], axis=0).astype(BF)
+    other = jnp.where(even, spec, -spec)
+    stacked = jnp.concatenate([spec, other, other, spec], axis=0).astype(BF)
     values = lax.dot_general(leg_ref[0], stacked, (((1,), (1,)), ((), ())), preferred_element_type=F32)
-    z_ref[pl.ds(step * half_rows, half_rows), :] = swapped(values)
+    x_ref[...] = values[:, :LANES]
+    turned_ref[...] = values[:, LANES:]
+    quarter = half_rows // 4
+    lines = [pl.ds(q, quarter, stride=4) for q in range(4)]
+    for part, value in enumerate(exchanged([x_ref[i, :] for i in lines], [turned_ref[i, :] for i in lines])):
+        z_ref[pl.ds(step * half_rows + part * quarter, quarter), :] = value
 
     @pl.when(step == m_count - 1)
     def _():
@@ -108,17 +109,18 @@
                     at = band * band_groups + (lev * groups + g - HALO)
                     over = at >= bands * band_groups
                     line = jnp.where(over, 2 * bands * band_groups - 1 - at, jnp.maximum(at, 0))
-                    base = line * 4 + jnp.where(over, 1 - south, south) * 2
+                    base = line + jnp.where(over, 1 - south, south) * (half_rows // 2)
                     for c in range(2):
                         row = (g * 2 + c) * m_count
-                        q_ref[lev, row : row + m_count] = z_ref[pl.ds(base + c, m_count, stride=half_rows), :]
+                        start = base + c * (half_rows // 4)
+                        q_ref[lev, row : row + m_count] = z_ref[pl.ds(start, m_count, stride=half_rows), :]
                 out_ref[wave * levs + lev] = q_ref[lev].astype(BF)
             return carry
 
         lax.fori_loop(0, waves, of_wave, 0)
 
 
-def direct_kernel(geometry, first_ref, values_ref, weights_ref, leg_ref, out_ref, z_ref, q_ref):
+def direct_kernel(geometry, first_ref, values_ref, weights_ref, leg_ref, out_ref, z_ref, q_ref, x_ref):
     waves, levs, groups, bands, band_groups, m_count = geometry
     half_rows = leg_ref.shape[1]
     step = pl.program_id(0)
@@ -133,18 +135,21 @@
                 for g in range(groups):
                     inside = lev * groups + g - HALO
                     if 0 <= inside < band_groups:
-                        base = (band * band_groups + inside) * 4 + south * 2
+                        base = band * band_groups + inside + south * (half_rows // 2)
                         for c in range(2):
                             row = (g * 2 + c) * m_count
-                            z_ref[pl.ds(base + c, m_count, stride=half_rows), :] = q_ref[lev, row : row + m_count]
+                            start = base + c * (half_rows // 4)
+                            z_ref[pl.ds(start, m_count, stride=half_rows), :] = q_ref[lev, row : row + m_count]
             return carry
 
         lax.fori_loop(0, waves, of_wave, 0)
 
-    x = swapped(z_ref[pl.ds(step * half_rows, half_rows), :])
-    y = pltpu.roll(x, LANES // 2, 1)
-    north = lane_ids(x.shape) < LANES // 2
-    paired = (weights_ref[...] * jnp.where(north, x + y, y - x)).astype(BF)
+    quarter = half_rows // 4
+    x = [z_ref[pl.ds(step * half_rows + part * quarter, quarter), :] for part in range(4)]
+    x = [x[0] + x[2], x[1] + x[3], x[0] - x[2], x[1] - x[3]]
+    for q, value in enumerate(exchanged(x, [pltpu.roll(i, 64, 1) for i in x])):
+        x_ref[pl.ds(q, quarter, stride=4), :] = weights_ref[q] * value
+    paired = x_ref[...].astype(BF)
     folded = lax.dot_general(paired, leg_ref[0], (((0,), (0,)), ((), ())), preferred_element_type=F32)
     half = folded.shape[0] // 2
     keep, even = kept(first_ref[0] + step, (half, folded.shape[1]), half // 2)
@@ -152,7 +157,7 @@
     out_ref[0] = jnp.where(keep, chosen, 0.0).astype(BF)
 
 
-def legendre_call(kernel, name, first, operands, in_specs, out_spec, out_shape, geometry, legendre):
+def legendre_call(kernel, name, extra, first, operands, in_specs, out_spec, out_shape, geometry, legendre):
     m_count, half_rows, k_count = legendre.shape
     levs = geometry[1]
     return pl.pallas_call(
@@ -166,12 +171,56 @@
         scratch_shapes=[
             pltpu.VMEM((m_count * half_rows, LANES), F32),
             pltpu.VMEM((levs, PIECE_ROWS, LANES), F32),
-        ],
+        ]
+        + [pltpu.VMEM((half_rows, LANES), F32)] * extra,
         cost_estimate=pl.CostEstimate(
             flops=2 * legendre.size * LANES, bytes_accessed=2 * legendre.size + 5 * 10**6, transcendentals=0
         ),
         name=name,
     )(first.reshape(1), *operands, legendre)
+
+
+PARTS = 4
+
+
+def grid_kernel(owners, steps, table_ref, values_ref, out_ref, pack_ref):
+    step = pl.program_id(0)
+    groups = values_ref.shape[0] // LANES
+    rows = out_ref.shape[1]
+    result = lax.dot_general(table_ref[...], values_ref[...], (((1,), (1,)), ((), ())), preferred_element_type=F32)
+    for part in range(PARTS):
+        for g in range(groups):
+            start = g * (PARTS * steps) + step * PARTS + part
+            pack_ref[pl.ds(start, owners, stride=rows), :] = result[
+                part * owners : (part + 1) * owners, g * LANES : (g + 1) * LANES
+            ]
+
+    @pl.when(step == steps - 1)
+    def _():
+        blank = jnp.zeros((owners, LANES), F32)
+        for row in range(groups * (table_ref.shape[0] // owners) * steps, rows):
+            pack_ref[pl.ds(row, owners, stride=rows), :] = blank
+        out_ref[...] = pack_ref[...].reshape(out_ref.shape).astype(BF)
+
+
+def grid_to_pieces(table, values, owners):
+    rows = table.shape[0] // owners
+    block = PARTS * owners
+    return pl.pallas_call(
+        functools.partial(grid_kernel, owners, rows // PARTS),
+        grid=(rows // PARTS,),
+        in_specs=[
+            pl.BlockSpec((block, NLON), lambda i: (i, 0)),
+            pl.BlockSpec(values.shape, lambda i: (0, 0)),
+        ],
+        out_specs=pl.BlockSpec((owners, PIECE_ROWS, LANES), lambda i: (0, 0, 0)),
+        out_shape=jax.ShapeDtypeStruct((owners, PIECE_ROWS, LANES), BF),
+        scratch_shapes=[pltpu.VMEM((owners * PIECE_ROWS, LANES), F32)],
+        cost_estimate=pl.CostEstimate(
+            flops=2 * table.size * values.shape[0], bytes_accessed=2 * table.size + 5 * 10**6, transcendentals=0
+        ),
+        name="grid_to_pieces",
+    )(table, values)
 
 
 def lane_ids(shape):
@@ -263,7 +312,8 @@
         for at in range(2):
             one = both[:, at * LANES : (at + 1) * LANES]
             mix_ref[0, r - HALO + at] = one[:, :cols]
-            heating_ref[0, r + at : r + at + 1] = jnp.sum(heat * one, axis=0, keepdims=True)
+            warm = jnp.sum(heat * one, axis=0, keepdims=True)
+            heating_ref[0, r + at : r + at + 1] = jnp.where(lanes[:1] < cols, warm, 0.0)
 
 
 def shift(value, axis, by):
@@ -374,6 +424,7 @@
     pieces = legendre_call(
         inverse_kernel,
         "to_latitude",
+        2,
         first_m,
         [spectra.transpose(0, 2, 3, 1).reshape(m_count, width, k_count)],
         [spec_spec],
@@ -385,10 +436,9 @@
     spread = lax.all_to_all(pieces, both, split_axis=0, concat_axis=0, tiled=True)
     halos = tracer_halos(tracers)
     inverse, direct = fourier_tables(owners, m_count)
-    spread = spread[:, :used].reshape(owners, groups, 2 * m_count, LANES).transpose(0, 2, 1, 3)
-    spread = spread.reshape(2 * TRUNC, groups * LANES)
-
-    grid = lax.dot_general(spread, inverse, (((0,), (0,)), ((), ())), preferred_element_type=F32).astype(BF)
+    spread = spread[:, :used].transpose(1, 0, 2).reshape(groups, 2 * TRUNC, LANES)
+
+    grid = jnp.einsum("gkn,kj->gnj", spread, inverse, preferred_element_type=F32).astype(BF)
     grid = grid.reshape(groups, ratio, fields, NLON)
 
     lane = jnp.arange(LANES, dtype=jnp.int32)
@@ -410,8 +460,13 @@
     heating = heating.transpose(1, 0, 2)
     heating = jnp.where(south, jnp.flip(heating, axis=0), heating).reshape(levs, groups * levels, LANES)
     heating = lax.all_to_all(heating, "lev", split_axis=0, concat_axis=0, tiled=True)
-    heating = heating.reshape(levs, groups, levels, LANES)[..., :chem_cols].transpose(1, 2, 0, 3)
-    heating = jnp.repeat(heating.reshape(groups, 1, levels, levs * chem_cols), ratio, axis=3)
+    heating = heating.transpose(1, 0, 2).reshape(groups * levels, levs * LANES)
+    high = heating.astype(BF)
+    low = (heating - high.astype(F32)).astype(BF)
+    column = jnp.where(lane[None, :] < chem_cols, lane + chem_cols * jnp.arange(levs, dtype=jnp.int32)[:, None], -1)
+    copied = (column.reshape(levs * LANES)[:, None] == cell[None, :]).astype(BF)
+    heating = jnp.dot(jnp.concatenate([high, low]), copied, preferred_element_type=F32)
+    heating = (heating[: groups * levels] + heating[groups * levels :]).reshape(groups, 1, levels, NLON)
 
     physics = jnp.tanh(
         jnp.einsum("ef,gqfj->gqej", phys_matrix, grid.astype(F32), precision=lax.Precision.HIGHEST)
@@ -423,17 +478,16 @@
     ).astype(BF)
 
     tendency = tendency.reshape(groups * ratio * fields, NLON)
-    coeffs = lax.dot_general(direct, tendency, (((1,), (1,)), ((), ())), preferred_element_type=F32).astype(BF)
-    coeffs = coeffs.reshape(owners, 2 * m_count, groups, LANES).transpose(0, 2, 1, 3).reshape(owners, used, LANES)
-    coeffs = jnp.pad(coeffs, ((0, 0), (0, PIECE_ROWS - used), (0, 0)))
+    coeffs = grid_to_pieces(direct, tendency, owners)
     values = lax.all_to_all(coeffs, both, split_axis=0, concat_axis=0, tiled=True)
 
     result = legendre_call(
         direct_kernel,
         "to_spectral",
+        1,
         first_m,
-        [values, jnp.broadcast_to(gauss_weights[:, None], (half_rows, LANES))],
-        [piece_spec, pl.BlockSpec((half_rows, LANES), lambda m: (0, 0))],
+        [values, jnp.broadcast_to(gauss_weights.reshape(-1, 4).T[:, :, None], (4, half_rows // 4, LANES))],
+        [piece_spec, pl.BlockSpec((4, half_rows // 4, LANES), lambda m: (0, 0, 0))],
         spec_spec,
         jax.ShapeDtypeStruct((m_count, width, k_count), BF),
         geometry,

time: 226 us -> 205 us (0.907)
  blocking collectives: 40.2 us -> 0 us
  waiting for transfers between devices: 5.43 us -> 40.5 us
  local copies, waits for them, and re-layouts: 37.8 us -> 8.1 us
  Pallas kernels: 81 us -> 91.7 us
  starting transfers between devices: 26.1 us -> 36.4 us
  matrix products: 26.4 us -> 16.9 us
    all_to_all x1 -> x0, blocking collectives: 40.2 us -> none  [body(): lax.all_to_all(coeffs, both, split_axis=0, concat_axis=0, tiled=True)]
    all_to_all x0 -> x1, waiting for transfers between devices: none -> 29.9 us  [body(): lax.all_to_all(coeffs, both, split_axis=0, concat_axis=0, tiled=True)]
    reshape x5 -> x1, local copies, waits for them, and re-layouts: 11.4 us -> 0.11 us  [body(): gauss_weights.reshape(-1, 4).T[:, :, None]]
    pallas_call x1 -> x2, Pallas kernels: 18.9 us -> 29.8 us  [the longest x1 16.1 us: fourier_tables(): pl.pallas_call(table_kernel, grid=(rows,), in_specs=[coarse_spec] * 4 + [...]
    all_to_all x0 -> x1, starting transfers between devices: none -> 10.7 us  [body(): lax.all_to_all(coeffs, both, split_axis=0, concat_axis=0, tiled=True)]
    another operation x7 -> x0, local copies, waits for them, and re-layouts: 10 us -> none  [the longest x2 4.19 us: fourier_tables(): b = jnp.tile(jnp.concatenate([sin, cos]), (repeat, 1))]
    dot_general x2, matrix products: 19.9 us -> 10.5 us  [the longest x1 8.6 us: body(): jnp.einsum('gkn,kj->gnj', spread, inverse, preferred_element_type=F32)]
    broadcast_in_dim x5 -> x3, local copies, waits for them, and re-layouts: 8.62 us -> 2.75 us  [the longest x1 1.04 us: body(): jnp.broadcast_to(gauss_weights.reshape(-1, 4).T[:, :, None], (4, half_row...]
  transfers between devices with their start and end apart: 7 -> 8, of which waited for: 2 -> 5; matrix products, arithmetic and copies ran while one was open for 18% -> 11% of each run, Pallas kernels for 14% -> 14%
where the time goes in v1:
time: 205 us; the launch traced here: 202 us
  Pallas kernels  91.7 us (45%)
  waiting for transfers between devices  40.5 us (20%)
  starting transfers between devices  36.4 us (18%)
  matrix products  16.9 us (8%)
  local copies, waits for them, and re-layouts  8.1 us (4%)
  other arithmetic  7.79 us (4%)
    pallas_call x2, Pallas kernels, legendre_call(): pl.pallas_call(functools.partial(kernel, geometry), grid=(m_count,), in_s...  34.8 us
    all_to_all x1, waiting for transfers between devices, body(): lax.all_to_all(coeffs, both, split_axis=0, concat_axis=0, tiled=True)  29.9 us
    pallas_call x1, Pallas kernels, fourier_tables(): pl.pallas_call(table_kernel, grid=(rows,), in_specs=[coarse_spec] * 4 + [...  16.1 us
    pallas_call x1, Pallas kernels, chemistry(): pl.pallas_call(functools.partial(chemistry_kernel, total_rows), grid=(lev...  14.1 us
    pallas_call x1, Pallas kernels, grid_to_pieces(): pl.pallas_call(functools.partial(grid_kernel, owners, rows // PARTS), gri...  13.7 us
    all_to_all x1, starting transfers between devices, body(): lax.all_to_all(pieces, both, split_axis=0, concat_axis=0, tiled=True)  11.5 us
    all_to_all x1, starting transfers between devices, body(): lax.all_to_all(coeffs, both, split_axis=0, concat_axis=0, tiled=True)  10.7 us
    dot_general x1, matrix products, body(): jnp.einsum('gkn,kj->gnj', spread, inverse, preferred_element_type=F32)  8.6 us
  transfers between devices with their start and end apart: 8, of which 5 were waited for; matrix products, arithmetic and copies ran while one was open for 11% of the time, Pallas kernels for 14%

profile of v1, /device:TPU:1, one launch (start us, length us, event | category | flops | bytes accessed | tf_op | source)
XLA Modules:
  0.0 202.2 jit_solution(13351447642695298404)
XLA Ops:
  0.6 0.0 copy-start
  0.7 18.7 %to_latitude.1 = bf16[128,64,128]{2,1,0:T(8,128)(2,1)} custom-call(s32[1]{0:T(128)} %bitcast.first_ref, bf16[10,64,1280]{2,1,0:T(8,128)(2,1)} %bitcast.73, bf16[10,640,1280]{2,1,0:T(8,128)(2,1)} %leg_ref.3), custom_call_target="tpu_custom_call" | custom-call | flops 2097152000 | bytes 21384000 | tf_op jit(solution)/shard_map/to_latitude/pallas_call | solution.py:163
  19.3 11.5 %all-to-all-start = ((bf16[128,64,128]{2,1,0:T(8,128)(2,1)}), bf16[128,64,128]{2,1,0:T(8,128)(2,1)S(1)}, u32[]{:S(2)}, u32[]{:S(2)}) async-start(bf16[128,64,128]{2,1,0:T(8,128)(2,1)} %to_latitude.1), calls=%async_computation | async-start | bytes 4194304 | tf_op jit(solution)/shard_map/all_to_all | solution.py:436
  30.8 7.4 %edge_columns.1 = (f32[8,64,128]{2,1,0:T(8,128)}, f32[8,64,128]{2,1,0:T(8,128)}) custom-call(f32[8,20,64,80]{3,2,1,0:T(8,128)} %bitcast.63), custom_call_target="tpu_custom_call" | custom-call | flops 10000000 | bytes 7000000 | tf_op jit(solution)/shard_map/edge_columns/pallas_call | solution.py:331
  38.2 1.5 collective-permute-start
  39.7 2.3 %collective-permute-start.1 = (f32[8,64,128]{2,1,0:T(8,128)}, f32[8,64,128]{2,1,0:T(8,128)S(1)}, u32[]{:S(2)}, u32[]{:S(2)}) collective-permute-start(f32[8,64,128]{2,1,0:T(8,128)} %get-tuple-element.13), channel_id=1, source_target_pairs={{0,7},{1,0},{2,1},{3,2},{4,3},{5,4},{6,5},{7,6},{8,15},{9,8},{10,9... | collective-permute-start | bytes 786440 | tf_op jit(solution)/shard_map/ppermute | solution.py:321
  42.0 1.1 broadcast_multiply_fusion
  43.1 0.6 fusion.30
  43.7 0.7 fusion.23
  44.5 0.8 broadcast_in_dim.67.b_ref
  45.3 0.9 copy.11.a_ref
  46.2 16.1 %fourier_tables.1 = (bf16[2560,2560]{1,0:T(8,128)(2,1)}, bf16[2560,2560]{1,0:T(8,128)(2,1)}) custom-call(f32[128,128]{1,0:T(8,128)} %get-tuple-element.27.cos_ref, f32[128,128]{1,0:T(8,128)} %get-tuple-element.26.sin_ref, f32[128,128]{1,0:T(8,128)} %get-tuple-element.23.turned_cos_ref, f32[128,128]{1,0:T(8,128)} %get-tuple-element.22.turned_sin_ref, ...), custom_call_target="tpu_custom_call" | custom-call | flops 39321600 | bytes 26214400 | tf_op jit(solution)/shard_map/fourier_tables/pallas_call | solution.py:55
  62.3 0.1 fusion.42
  62.4 3.5 %collective-permute-done.west_ref = f32[8,64,128]{2,1,0:T(8,128)S(1)} collective-permute-done((f32[8,64,128]{2,1,0:T(8,128)}, f32[8,64,128]{2,1,0:T(8,128)S(1)}, u32[]{:S(2)}, u32[]{:S(2)}) %collective-permute-start) | collective-permute-done | bytes 262176 | tf_op jit(solution)/shard_map/ppermute | solution.py:321
  65.9 1.3 collective-permute-done.1.east_ref
  67.2 0.7 copy-done.4
  67.9 5.5 %edge_rows.1 = (f32[8,2,64,128]{3,2,1,0:T(8,128)}, f32[8,2,64,128]{3,2,1,0:T(8,128)}) custom-call(f32[8,20,64,80]{3,2,1,0:T(8,128)} %bitcast.64, f32[8,20,64,80]{3,2,1,0:T(8,128)} %bitcast.65, f32[8,64,128]{2,1,0:T(8,128)} %copy-done.3, f32[8,64,128]{2,1,0:T(8,128)} %copy-done.4), custom_call_target="tpu_custom_call" | custom-call | flops 1000000 | bytes 2000000 | tf_op jit(solution)/shard_map/edge_rows/pallas_call | solution.py:343
  73.4 3.2 %collective-permute-start.2 = (f32[8,2,64,128]{3,2,1,0:T(8,128)}, f32[8,2,64,128]{3,2,1,0:T(8,128)S(1)}, u32[]{:S(2)}, u32[]{:S(2)}) collective-permute-start(f32[8,2,64,128]{3,2,1,0:T(8,128)} %get-tuple-element.14), channel_id=1, source_target_pairs={{0,8},{8,16},{16,24},{24,32},{32,40},{40,48},{48,56},{56,64},{64,7... | collective-permute-start | bytes 1572872 | tf_op jit(solution)/shard_map/ppermute | solution.py:321
  76.7 0.2 slice_bitcast_fusion
  76.8 1.3 copy.12
  78.1 8.6 %fusion.13 = bf16[3,128,2560]{2,1,0:T(8,128)(2,1)S(1)} fusion(bf16[3,2560,128]{2,1,0:T(8,128)(2,1)S(1)} %bitcast.70, bf16[2560,2560]{1,0:T(8,128)(2,1)} %get-tuple-element.11), kind=kOutput, calls=%fused_computation.15 | convolution fusion | flops 5034147840 | bytes 17039360 | tf_op jit(solution)/shard_map/gkn,kj->gnj/dot_general | solution.py:441
  86.7 0.1 convert_reduce_fusion
  86.9 2.4 %fusion.16 = f32[8,48,128]{2,1,0:T(8,128)} fusion(bf16[48,2560,1]{1,0,2:T(8,128)(2,1)S(1)} %bitcast.77, s32[8,128]{1,0:T(8,128)S(1)} %get-tuple-element.24, s32[2560]{0:T(1024)S(1)} %add_select_fusion.2), kind=kOutput, calls=%fused_computation.19 | convolution fusion | flops 259522560 | bytes 456704 | tf_op jit(solution)/shard_map/gqfj,jx->gfx/dot_general | solution.py:451
  89.3 3.8 %all-to-all-start.1 = ((f32[8,48,128]{2,1,0:T(8,128)}), f32[8,48,128]{2,1,0:T(8,128)S(1)}, u32[]{:S(2)}, u32[]{:S(2)}) async-start(f32[8,48,128]{2,1,0:T(8,128)} %fusion.16), calls=%async_computation.1 | async-start | bytes 393216 | tf_op jit(solution)/shard_map/all_to_all | solution.py:453
  93.1 0.7 pad_maximum_fusion.2.react_ref
  93.8 4.8 %all-to-all-done.1 = f32[8,48,128]{2,1,0:T(8,128)S(1)} async-done(((f32[8,48,128]{2,1,0:T(8,128)}), f32[8,48,128]{2,1,0:T(8,128)S(1)}, u32[]{:S(2)}, u32[]{:S(2)}) %all-to-all-start.1) | async-done | bytes 196640 | tf_op jit(solution)/shard_map/all_to_all | solution.py:453
  98.6 0.1 copy.14
  98.7 0.8 select_bitcast_fusion.u_ref.v_ref
  99.5 0.8 broadcast_in_dim.72.heat_ref
  100.3 14.1 %chemistry.1 = (f32[8,20,64,80]{3,2,1,0:T(8,128)}, f32[8,24,128]{2,1,0:T(8,128)}) custom-call(s32[1]{0:T(128)} %bitcast.11.first_ref, f32[8,20,64,80]{3,2,1,0:T(8,128)} %bitcast.66, f32[8,2,64,128]{3,2,1,0:T(8,128)} %copy-done.5, f32[8,2,64,128]{3,2,1,0:T(8,128)} %collective-permute-done.3.south_ref, f32[8,64,128]{2,1,0:T(8,128)} %copy-done.3, ...), custom_call_target="tpu_custom_call" | custom-call | flops 1000000000 | bytes 16000000 | tf_op jit(solution)/shard_map/chemistry/pallas_call | solution.py:371
  114.5 0.9 rev.9
  115.4 0.9 broadcast_select_fusion
  116.3 0.7 copy.16
  116.9 3.4 %all-to-all-start.2 = ((f32[8,24,128]{2,1,0:T(8,128)}), f32[8,24,128]{2,1,0:T(8,128)S(1)}, u32[]{:S(2)}, u32[]{:S(2)}) async-start(f32[8,24,128]{2,1,0:T(8,128)} %bitcast.19), calls=%async_computation.2 | async-start | bytes 196608 | tf_op jit(solution)/shard_map/all_to_all | solution.py:462
  120.3 4.0 %fusion.49 = (bf16[3,4,32,2560]{3,2,1,0:T(8,128)(2,1)S(1)}, f32[3,4,32,2560]{3,2,1,0:T(8,128)}) fusion(f32[32]{0:T(128)S(1)} %copy-done.9, bf16[3,4,32,2560]{3,2,1,0:T(8,128)(2,1)S(1)} %bitcast.68, f32[32,32]{1,0:T(8,128)S(1)} %copy-done), kind=kOutput, calls=%fused_computation.82 | convolution fusion | flops 379453440 | bytes 7868544 | tf_op jit(solution)/shard_map/ef,gqfj->gqej/dot_general | solution.py:472
  124.3 0.1 slice.31
  124.5 0.9 all-to-all-done.2
  125.4 1.9 fusion.2
  127.3 1.3 fusion.17
  128.6 1.5 pad_maximum_fusion
  130.1 13.7 %grid_to_pieces.1 = bf16[128,64,128]{2,1,0:T(8,128)(2,1)} custom-call(bf16[2560,2560]{1,0:T(8,128)(2,1)} %get-tuple-element.10.table_ref, bf16[384,2560]{1,0:T(8,128)(2,1)} %bitcast.69), custom_call_target="tpu_custom_call" | custom-call | flops 5033164800 | bytes 18107200 | tf_op jit(solution)/shard_map/grid_to_pieces/pallas_call | solution.py:209
  143.8 10.7 %all-to-all-start.3 = ((bf16[128,64,128]{2,1,0:T(8,128)(2,1)}), bf16[128,64,128]{2,1,0:T(8,128)(2,1)S(1)}, u32[]{:S(2)}, u32[]{:S(2)}) async-start(bf16[128,64,128]{2,1,0:T(8,128)(2,1)} %grid_to_pieces.1), calls=%async_computation.3 | async-start | bytes 4194304 | tf_op jit(solution)/shard_map/all_to_all | solution.py:482
  154.5 0.1 reshape.191
  154.6 0.1 copy.18
  154.7 29.9 %all-to-all-done.3.values_ref = bf16[128,64,128]{2,1,0:T(8,128)(2,1)S(1)} async-done(((bf16[128,64,128]{2,1,0:T(8,128)(2,1)}), bf16[128,64,128]{2,1,0:T(8,128)(2,1)S(1)}, u32[]{:S(2)}, u32[]{:S(2)}) %all-to-all-start.3) | async-done | bytes 2097184 | tf_op jit(solution)/shard_map/all_to_all | solution.py:482
  184.6 1.0 broadcast_in_dim.74.weights_ref
  185.6 0.4 copy-done.2
  186.1 16.1 %to_spectral.1 = bf16[10,64,1280]{2,1,0:T(8,128)(2,1)} custom-call(s32[1]{0:T(128)} %bitcast.first_ref, bf16[128,64,128]{2,1,0:T(8,128)(2,1)} %copy-done.2, f32[4,160,128]{2,1,0:T(8,128)} %broadcast_in_dim.74.weights_ref, bf16[10,640,1280]{2,1,0:T(8,128)(2,1)} %leg_ref.3), custom_call_target="tpu_custom_call" | custom-call | flops 2097152000 | bytes 21384000 | tf_op jit(solution)/shard_map/to_spectral/pallas_call | solution.py:163
  (34 shorter events, 0.2 us)
Async XLA Ops:
  0.6 119.7 %copy-start = (f32[32,32]{1,0:T(8,128)S(1)}, f32[32,32]{1,0:T(8,128)}, u32[]{:S(2)}) copy-start(f32[32,32]{1,0:T(8,128)} %param.11) | copy-start | bytes 12292
  19.3 57.4 %all-to-all-start = ((bf16[128,64,128]{2,1,0:T(8,128)(2,1)}), bf16[128,64,128]{2,1,0:T(8,128)(2,1)S(1)}, u32[]{:S(2)}, u32[]{:S(2)}) async-start(bf16[128,64,128]{2,1,0:T(8,128)(2,1)} %to_latitude.1), calls=%async_computation | async-start | bytes 4194304 | tf_op jit(solution)/shard_map/all_to_all | solution.py:436
  38.2 27.7 %collective-permute-start = (f32[8,64,128]{2,1,0:T(8,128)}, f32[8,64,128]{2,1,0:T(8,128)S(1)}, u32[]{:S(2)}, u32[]{:S(2)}) collective-permute-start(f32[8,64,128]{2,1,0:T(8,128)} %get-tuple-element.12), channel_id=1, source_target_pairs={{0,1},{1,2},{2,3},{3,4},{4,5},{5,6},{6,7},{7,0},{8,9},{9,10},{10,1... | collective-permute-start | bytes 786440 | tf_op jit(solution)/shard_map/ppermute | solution.py:321
  39.7 27.5 %collective-permute-start.1 = (f32[8,64,128]{2,1,0:T(8,128)}, f32[8,64,128]{2,1,0:T(8,128)S(1)}, u32[]{:S(2)}, u32[]{:S(2)}) collective-permute-start(f32[8,64,128]{2,1,0:T(8,128)} %get-tuple-element.13), channel_id=1, source_target_pairs={{0,7},{1,0},{2,1},{3,2},{4,3},{5,4},{6,5},{7,6},{8,15},{9,8},{10,9... | collective-permute-start | bytes 786440 | tf_op jit(solution)/shard_map/ppermute | solution.py:321
  65.9 1.3 copy-start.3
  67.2 0.7 copy-start.4
  73.4 26.1 %collective-permute-start.2 = (f32[8,2,64,128]{3,2,1,0:T(8,128)}, f32[8,2,64,128]{3,2,1,0:T(8,128)S(1)}, u32[]{:S(2)}, u32[]{:S(2)}) collective-permute-start(f32[8,2,64,128]{3,2,1,0:T(8,128)} %get-tuple-element.14), channel_id=1, source_target_pairs={{0,8},{8,16},{16,24},{24,32},{32,40},{40,48},{48,56},{56,64},{64,7... | collective-permute-start | bytes 1572872 | tf_op jit(solution)/shard_map/ppermute | solution.py:321
  76.7 22.8 %collective-permute-start.3 = (f32[8,2,64,128]{3,2,1,0:T(8,128)}, f32[8,2,64,128]{3,2,1,0:T(8,128)}, u32[]{:S(2)}, u32[]{:S(2)}) collective-permute-start(f32[8,2,64,128]{3,2,1,0:T(8,128)} %get-tuple-element.15), channel_id=1, source_target_pairs={{0,120},{8,0},{16,8},{24,16},{32,24},{40,32},{48,40},{56,48},{64,5... | collective-permute-start | bytes 1572872 | tf_op jit(solution)/shard_map/ppermute | solution.py:321
  86.9 6.2 %copy-start.6 = (f32[64,64]{1,0:T(8,128)S(1)}, f32[64,64]{1,0:T(8,128)}, u32[]{:S(2)}) copy-start(f32[64,64]{1,0:T(8,128)} %param.14) | copy-start | bytes 49156
  86.9 12.6 %copy-start.8 = (f32[64]{0:T(128)S(1)}, f32[64]{0:T(128)}, u32[]{:S(2)}) copy-start(f32[64]{0:T(128)} %param.15) | copy-start | bytes 772
  89.3 9.3 %all-to-all-start.1 = ((f32[8,48,128]{2,1,0:T(8,128)}), f32[8,48,128]{2,1,0:T(8,128)S(1)}, u32[]{:S(2)}, u32[]{:S(2)}) async-start(f32[8,48,128]{2,1,0:T(8,128)} %fusion.16), calls=%async_computation.1 | async-start | bytes 393216 | tf_op jit(solution)/shard_map/all_to_all | solution.py:453
  99.5 0.8 copy-start.5
  100.3 20.0 %copy-start.9 = (f32[32]{0:T(128)S(1)}, f32[32]{0:T(128)}, u32[]{:S(2)}) copy-start(f32[32]{0:T(128)} %param.12) | copy-start | bytes 388
  116.9 8.4 %all-to-all-start.2 = ((f32[8,24,128]{2,1,0:T(8,128)}), f32[8,24,128]{2,1,0:T(8,128)S(1)}, u32[]{:S(2)}, u32[]{:S(2)}) async-start(f32[8,24,128]{2,1,0:T(8,128)} %bitcast.19), calls=%async_computation.2 | async-start | bytes 196608 | tf_op jit(solution)/shard_map/all_to_all | solution.py:462
  143.8 10.7 %copy-start.7 = (f32[640]{0:T(1024)S(1)}, f32[640]{0:T(1024)}, u32[]{:S(2)}) copy-start(f32[640]{0:T(1024)} %param.10) | copy-start | bytes 7684
  143.8 40.8 %all-to-all-start.3 = ((bf16[128,64,128]{2,1,0:T(8,128)(2,1)}), bf16[128,64,128]{2,1,0:T(8,128)(2,1)S(1)}, u32[]{:S(2)}, u32[]{:S(2)}) async-start(bf16[128,64,128]{2,1,0:T(8,128)(2,1)} %grid_to_pieces.1), calls=%async_computation.3 | async-start | bytes 4194304 | tf_op jit(solution)/shard_map/all_to_all | solution.py:482
  184.6 1.5 copy-start.2
  186.1 16.1 %copy-start.1 = (f32[32,32]{1,0:T(8,128)S(1)}, f32[32,32]{1,0:T(8,128)}, u32[]{:S(2)}) copy-start(f32[32,32]{1,0:T(8,128)} %param.11) | copy-start | bytes 12292

commit v2 on v1

--- a/solution.py
+++ b/solution.py
@@ -10,32 +10,32 @@
 
 TRUNC = 1280
 NLON = 2560
+HALF = NLON // 2
 SUBSTEPS = 2
 COURANT = 0.6
 LANES = 128
+FOLD = HALF + LANES
 PIECE_ROWS = 64
+UNIT = 8
 HALO = 2
 BF, F32 = jnp.bfloat16, jnp.float32
 
 
-def table_kernel(cos_ref, sin_ref, turned_cos_ref, turned_sin_ref, a_ref, b_ref, inverse_ref, direct_ref):
+def table_kernel(cos_ref, sin_ref, turned_cos_ref, turned_sin_ref, a_ref, b_ref, out_ref):
     step = pl.program_id(0)
-    scale = 1.0 / math.sqrt(NLON)
-    for block in range(NLON // LANES):
+    for block in range(FOLD // LANES):
         part = slice(block * LANES, (block + 1) * LANES)
         cos, sin = (turned_cos_ref, turned_sin_ref) if block % 2 else (cos_ref, sin_ref)
-        value = cos[...] * a_ref[0, :, part] - sin[...] * b_ref[0, :, part]
-        inverse_ref[:, part] = (value + value).astype(BF)
-        direct_ref[:, part] = (value * scale).astype(BF)
+        out_ref[:, part] = (cos[...] * a_ref[0, :, part] - sin[...] * b_ref[0, :, part]).astype(BF)
 
     @pl.when(step == 0)
     def _():
-        top = inverse_ref[:16, :].astype(F32)
+        top = out_ref[:16, :].astype(F32)
         first = lax.broadcasted_iota(jnp.int32, top.shape, 0) == 0
-        inverse_ref[:16, :] = jnp.where(first, 0.5 * top, top).astype(BF)
-
-
-def fourier_tables(owners, m_count):
+        out_ref[:16, :] = jnp.where(first, 0.5 * top, top).astype(BF)
+
+
+def fourier_table(owners, m_count):
     unit = 2.0 * math.pi / NLON
     owner = jnp.arange(owners, dtype=jnp.int32)[:, None]
     lane = jnp.arange(LANES, dtype=jnp.int32)[None, :]
@@ -43,23 +43,23 @@
     cos_c, sin_c = jnp.cos(coarse), jnp.sin(coarse)
     turn = jnp.where(owner % 2 == 1, -1.0, 1.0).astype(F32)
     inner = jnp.arange(m_count, dtype=jnp.int32)[:, None]
-    fine = (inner * jnp.arange(NLON, dtype=jnp.int32)[None, :] % NLON).astype(F32) * unit
+    fine = (inner * jnp.arange(FOLD, dtype=jnp.int32)[None, :] % NLON).astype(F32) * unit
     cos, sin = jnp.cos(fine), jnp.sin(fine)
-    a = jnp.concatenate([cos, -sin])
-    b = jnp.concatenate([sin, cos])
+    a = 2.0 * jnp.concatenate([cos, -sin])
+    b = 2.0 * jnp.concatenate([sin, cos])
     rows = 2 * m_count
     coarse_spec = pl.BlockSpec((owners, LANES), lambda i: (0, 0))
-    fine_spec = pl.BlockSpec((1, 1, NLON), lambda i: (i, 0, 0))
-    out_spec = pl.BlockSpec((owners, NLON), lambda i: (i, 0))
-    shape = jax.ShapeDtypeStruct((owners * rows, NLON), BF)
+    fine_spec = pl.BlockSpec((1, 1, FOLD), lambda i: (i, 0, 0))
+    out_spec = pl.BlockSpec((owners, FOLD), lambda i: (i, 0))
+    shape = jax.ShapeDtypeStruct((owners * rows, FOLD), BF)
     return pl.pallas_call(
         table_kernel,
         grid=(rows,),
         in_specs=[coarse_spec] * 4 + [fine_spec] * 2,
-        out_specs=[out_spec] * 2,
-        out_shape=[shape] * 2,
-        cost_estimate=pl.CostEstimate(flops=12 * TRUNC * NLON, bytes_accessed=8 * TRUNC * NLON, transcendentals=0),
-        name="fourier_tables",
+        out_specs=out_spec,
+        out_shape=shape,
+        cost_estimate=pl.CostEstimate(flops=6 * TRUNC * FOLD, bytes_accessed=4 * TRUNC * FOLD, transcendentals=0),
+        name="fourier_table",
     )(cos_c, sin_c, turn * cos_c, turn * sin_c, a[:, None], b[:, None])
 
 
@@ -106,40 +106,46 @@
             band = jnp.where(wave >= bands, waves - 1 - wave, wave)
             for lev in range(levs):
                 for g in range(groups):
-                    at = band * band_groups + (lev * groups + g - HALO)
+                    slot = lev * groups + g
+                    at = band * band_groups + jnp.where(south == 1, band_groups + HALO - 1 - slot, slot - HALO)
                     over = at >= bands * band_groups
                     line = jnp.where(over, 2 * bands * band_groups - 1 - at, jnp.maximum(at, 0))
                     base = line + jnp.where(over, 1 - south, south) * (half_rows // 2)
                     for c in range(2):
-                        row = (g * 2 + c) * m_count
-                        start = base + c * (half_rows // 4)
-                        q_ref[lev, row : row + m_count] = z_ref[pl.ds(start, m_count, stride=half_rows), :]
+                        for row, count, skip in moves(geometry, half_rows, slot, c):
+                            start = base + (c * (half_rows // 4) + skip)
+                            q_ref[lev, row : row + count] = z_ref[pl.ds(start, count, stride=half_rows), :]
                 out_ref[wave * levs + lev] = q_ref[lev].astype(BF)
             return carry
 
         lax.fori_loop(0, waves, of_wave, 0)
 
 
-def direct_kernel(geometry, first_ref, values_ref, weights_ref, leg_ref, out_ref, z_ref, q_ref, x_ref):
+def direct_kernel(geometry, first_ref, values_ref, weights_ref, leg_ref, out_ref, z_ref, q_ref, x_ref, w_ref):
     waves, levs, groups, bands, band_groups, m_count = geometry
     half_rows = leg_ref.shape[1]
     step = pl.program_id(0)
 
     @pl.when(step == 0)
     def _():
+        for q in range(4):
+            rows = pl.ds(q * (half_rows // 4), half_rows // 4)
+            w_ref[rows, :] = jnp.broadcast_to(weights_ref[:, q : q + 1], (half_rows // 4, LANES))
+
         def of_wave(wave, carry):
             south = (wave >= bands).astype(jnp.int32)
             band = jnp.where(wave >= bands, waves - 1 - wave, wave)
             for lev in range(levs):
                 q_ref[lev] = values_ref[wave * levs + lev].astype(F32)
                 for g in range(groups):
-                    inside = lev * groups + g - HALO
-                    if 0 <= inside < band_groups:
+                    slot = lev * groups + g
+                    if HALO <= slot < band_groups + HALO:
+                        inside = jnp.where(south == 1, band_groups + HALO - 1 - slot, slot - HALO)
                         base = band * band_groups + inside + south * (half_rows // 2)
                         for c in range(2):
-                            row = (g * 2 + c) * m_count
-                            start = base + c * (half_rows // 4)
-                            z_ref[pl.ds(start, m_count, stride=half_rows), :] = q_ref[lev, row : row + m_count]
+                            for row, count, skip in moves(geometry, half_rows, slot, c):
+                                start = base + (c * (half_rows // 4) + skip)
+                                z_ref[pl.ds(start, count, stride=half_rows), :] = q_ref[lev, row : row + count]
             return carry
 
         lax.fori_loop(0, waves, of_wave, 0)
@@ -148,13 +154,21 @@
     x = [z_ref[pl.ds(step * half_rows + part * quarter, quarter), :] for part in range(4)]
     x = [x[0] + x[2], x[1] + x[3], x[0] - x[2], x[1] - x[3]]
     for q, value in enumerate(exchanged(x, [pltpu.roll(i, 64, 1) for i in x])):
-        x_ref[pl.ds(q, quarter, stride=4), :] = weights_ref[q] * value
+        x_ref[pl.ds(q, quarter, stride=4), :] = w_ref[pl.ds(q * quarter, quarter), :] * value
     paired = x_ref[...].astype(BF)
     folded = lax.dot_general(paired, leg_ref[0], (((0,), (0,)), ((), ())), preferred_element_type=F32)
     half = folded.shape[0] // 2
     keep, even = kept(first_ref[0] + step, (half, folded.shape[1]), half // 2)
     chosen = jnp.where(even, folded[:half], folded[half:])
     out_ref[0] = jnp.where(keep, chosen, 0.0).astype(BF)
+
+
+def moves(geometry, half_rows, slot, c):
+    m_count = geometry[-1]
+    units = 2 * geometry[2]
+    unit = 2 * (slot % geometry[2]) + c
+    tail = m_count - UNIT
+    return (unit * UNIT, UNIT, 0), (units * UNIT + unit * tail, tail, UNIT * half_rows)
 
 
 def legendre_call(kernel, name, extra, first, operands, in_specs, out_spec, out_shape, geometry, legendre):
@@ -180,47 +194,92 @@
     )(first.reshape(1), *operands, legendre)
 
 
-PARTS = 4
-
-
-def grid_kernel(owners, steps, table_ref, values_ref, out_ref, pack_ref):
+PARTS = 5
+
+
+def grid_kernel(owners, steps, table_ref, *refs):
+    value_refs, warm_refs, (heat_ref, out_ref, pack_ref, fold_ref) = refs[:2], refs[2:4], refs[4:]
     step = pl.program_id(0)
-    groups = values_ref.shape[0] // LANES
+    lines = value_refs[0].shape[0]
+    groups = lines // LANES
     rows = out_ref.shape[1]
-    result = lax.dot_general(table_ref[...], values_ref[...], (((1,), (1,)), ((), ())), preferred_element_type=F32)
+    m_count = steps * PARTS // 2
+
+    @pl.when(step == 0)
+    def _():
+        scale = 0.5 / math.sqrt(NLON)
+        start = lane_ids((lines, LANES)) == 0
+        columns = lines // 32
+        levels = warm_refs[0].shape[0] // columns
+        below = heat_ref.shape[0] // 2
+
+        def tendency(side, block):
+            part = slice(block * LANES, (block + 1) * LANES)
+            there = slice(side * HALF + block * LANES, side * HALF + (block + 1) * LANES)
+            value = value_refs[side][:, part].astype(F32)
+            pieces = []
+            for at in range(columns):
+                cell = at // (columns // groups) * levels
+                heat = heat_ref[cell : cell + levels, there] + heat_ref[below + cell : below + cell + levels, there]
+                warm = warm_refs[side][at * levels : (at + 1) * levels, part] + heat
+                pieces += [value[at * 32 : at * 32 + 2 * levels], warm.astype(BF).astype(F32)]
+                pieces += [value[at * 32 + 3 * levels : (at + 1) * 32]]
+            return jnp.concatenate(pieces, axis=0)
+
+        for block in range(HALF // LANES):
+            west, east = tendency(0, block), tendency(1, block)
+            total = west + east
+            if block == 0:
+                total = jnp.where(start, west, total)
+                fold_ref[0, :, HALF:] = jnp.where(start, scale * east, 0.0).astype(BF)
+                fold_ref[1, :, HALF:] = jnp.zeros((lines, LANES), BF)
+            fold_ref[0, :, block * LANES : (block + 1) * LANES] = (scale * total).astype(BF)
+            fold_ref[1, :, block * LANES : (block + 1) * LANES] = (scale * (west - east)).astype(BF)
+
+    part_c = step // (steps // 2)
+    result = lax.dot_general(
+        table_ref[...], fold_ref[part_c], (((1,), (1,)), ((), ())), preferred_element_type=F32
+    )
+    first = (lax.broadcasted_iota(jnp.int32, (owners, LANES), 0) == 0) & (step == 0)
+    tail = m_count - UNIT
     for part in range(PARTS):
+        m = step % (steps // 2) * PARTS + part
         for g in range(groups):
-            start = g * (PARTS * steps) + step * PARTS + part
-            pack_ref[pl.ds(start, owners, stride=rows), :] = result[
-                part * owners : (part + 1) * owners, g * LANES : (g + 1) * LANES
-            ]
+            unit = 2 * g + part_c
+            start = jnp.where(m < UNIT, unit * UNIT + m, 2 * groups * UNIT + unit * tail + m - UNIT)
+            value = result[part * owners : (part + 1) * owners, g * LANES : (g + 1) * LANES]
+            if part == 0:
+                value = jnp.where(first, 2.0 * value, value)
+            pack_ref[pl.ds(start, owners, stride=rows), :] = value
 
     @pl.when(step == steps - 1)
     def _():
         blank = jnp.zeros((owners, LANES), F32)
-        for row in range(groups * (table_ref.shape[0] // owners) * steps, rows):
+        for row in range(groups * PARTS * steps, rows):
             pack_ref[pl.ds(row, owners, stride=rows), :] = blank
         out_ref[...] = pack_ref[...].reshape(out_ref.shape).astype(BF)
 
 
-def grid_to_pieces(table, values, owners):
-    rows = table.shape[0] // owners
-    block = PARTS * owners
+def grid_to_pieces(table, values, warm, heating, owners):
+    steps = table.shape[0] // owners // PARTS
     return pl.pallas_call(
-        functools.partial(grid_kernel, owners, rows // PARTS),
-        grid=(rows // PARTS,),
+        functools.partial(grid_kernel, owners, steps),
+        grid=(steps,),
         in_specs=[
-            pl.BlockSpec((block, NLON), lambda i: (i, 0)),
-            pl.BlockSpec(values.shape, lambda i: (0, 0)),
+            pl.BlockSpec((PARTS * owners, FOLD), lambda i: (i, 0)),
+            *[pl.BlockSpec(value.shape, lambda i: (0, 0)) for value in (*values, *warm, heating)],
         ],
         out_specs=pl.BlockSpec((owners, PIECE_ROWS, LANES), lambda i: (0, 0, 0)),
         out_shape=jax.ShapeDtypeStruct((owners, PIECE_ROWS, LANES), BF),
-        scratch_shapes=[pltpu.VMEM((owners * PIECE_ROWS, LANES), F32)],
+        scratch_shapes=[
+            pltpu.VMEM((owners * PIECE_ROWS, LANES), F32),
+            pltpu.VMEM((2, values[0].shape[0], FOLD), BF),
+        ],
         cost_estimate=pl.CostEstimate(
-            flops=2 * table.size * values.shape[0], bytes_accessed=2 * table.size + 5 * 10**6, transcendentals=0
+            flops=2 * table.size * values[0].shape[0], bytes_accessed=2 * table.size + 5 * 10**6, transcendentals=0
         ),
         name="grid_to_pieces",
-    )(table, values)
+    )(table, *values, *warm, heating)
 
 
 def lane_ids(shape):
@@ -233,28 +292,33 @@
     head = jnp.zeros((count, LANES), F32)
     tail = head
     pad[:, :, :cols] = tr_ref[0]
+    gap = LANES - HALO - cols
     for r in range(rows):
         line = pad[r]
-        here = (lanes >> 1) == r
-        head = jnp.where(here, pltpu.roll(line, 2 * r, 1), head)
-        tail = jnp.where(here, pltpu.roll(line, (2 * r - cols + 2) % LANES, 1), tail)
-    head_ref[0] = head
-    tail_ref[0] = tail
-
-
-def with_columns(line, r, west, east, cols, lanes):
-    line = jnp.where((lanes >> 1) == cols // 2, pltpu.roll(east, (cols - 2 * r) % LANES, 1), line)
-    return jnp.where((lanes >> 1) == LANES // 2 - 1, pltpu.roll(west, (LANES - 2 - 2 * r) % LANES, 1), line)
-
-
-def edge_rows_kernel(rows, first_ref, last_ref, west_ref, east_ref, top_ref, low_ref):
-    count, cols = first_ref.shape[2:]
+        head = jnp.where((lanes >> 1) == r, pltpu.roll(line, 2 * r, 1), head)
+        tail = jnp.where((lanes >> 1) == r + gap // 2, pltpu.roll(line, (2 * r + gap - cols + HALO) % LANES, 1), tail)
+    head_ref[0] = head.astype(BF)
+    tail_ref[0] = tail.astype(BF)
+
+
+def both_sides(west, east, cols, lanes):
+    return jnp.where(lanes < LANES - HALO - cols, east.astype(F32), west.astype(F32))
+
+
+def with_columns(line, r, sides, cols, lanes):
+    here = ((lanes >> 1) == cols // 2) | ((lanes >> 1) == LANES // 2 - 1)
+    return jnp.where(here, pltpu.roll(sides, (cols - 2 * r) % LANES, 1), line)
+
+
+def edge_rows_kernel(rows, first_ref, last_ref, west_ref, east_ref, top_ref, low_ref, line):
+    levels, _, count, cols = first_ref.shape
     lanes = lane_ids((count, LANES))
-    west, east = west_ref[0], east_ref[0]
-    for at in range(HALO):
-        for src, out, r in ((first_ref, top_ref, at), (last_ref, low_ref, rows - HALO + at)):
-            out[0, at, :, :cols] = src[0, at]
-            out[0, at] = with_columns(out[0, at], r, west, east, cols, lanes)
+    for level in range(levels):
+        sides = both_sides(west_ref[level], east_ref[level], cols, lanes)
+        for at in range(HALO):
+            for src, out, r in ((first_ref, top_ref, at), (last_ref, low_ref, rows - HALO + at)):
+                line[:, :cols] = src[level, at]
+                out[level, at] = with_columns(line[...], r, sides, cols, lanes).astype(BF)
 
 
 def chemistry_kernel(
@@ -264,13 +328,13 @@
     rows, tracers, cols = tr_ref.shape[1:]
     deep = rows + 2 * HALO
     lanes = lane_ids((tracers, LANES))
-    west, east = west_ref[0], east_ref[0]
+    sides = both_sides(west_ref[0], east_ref[0], cols, lanes)
     for at in range(HALO):
-        x_ref[at] = north_ref[0, at]
-        x_ref[rows + HALO + at] = south_ref[0, at]
+        x_ref[at] = north_ref[0, at].astype(F32)
+        x_ref[rows + HALO + at] = south_ref[0, at].astype(F32)
     x_ref[HALO : HALO + rows, :, :cols] = tr_ref[0]
     for r in range(rows):
-        x_ref[HALO + r] = with_columns(x_ref[HALO + r], r, west, east, cols, lanes)
+        x_ref[HALO + r] = with_columns(x_ref[HALO + r], r, sides, cols, lanes)
     u, v = u_ref[0], v_ref[0]
     face_u = 0.5 * (u + pltpu.roll(u, LANES - 1, 1))
     east_up, east_down = COURANT * jnp.maximum(face_u, 0.0), COURANT * jnp.minimum(face_u, 0.0)
@@ -325,9 +389,9 @@
     levels, rows, count, cols = tracers.shape
     tr_spec = pl.BlockSpec((1, rows, count, cols), lambda l: (l, 0, 0, 0))
     col_spec = pl.BlockSpec((1, count, LANES), lambda l: (l, 0, 0))
-    row_spec = pl.BlockSpec((1, HALO, count, LANES), lambda l: (l, 0, 0, 0))
-    col_shape = jax.ShapeDtypeStruct((levels, count, LANES), F32)
-    row_shape = jax.ShapeDtypeStruct((levels, HALO, count, LANES), F32)
+    col_shape = jax.ShapeDtypeStruct((levels, count, LANES), BF)
+    row_shape = jax.ShapeDtypeStruct((levels, HALO, count, LANES), BF)
+    some = levels // 2
     head, tail = pl.pallas_call(
         edge_columns_kernel,
         grid=(levels,),
@@ -342,14 +406,15 @@
     east = shift(head, "lev", -1)
     top, low = pl.pallas_call(
         functools.partial(edge_rows_kernel, rows),
-        grid=(levels,),
+        grid=(levels // some,),
         in_specs=[
-            pl.BlockSpec((1, HALO, count, cols), lambda l: (l, 0, 0, 0)),
-            pl.BlockSpec((1, HALO, count, cols), lambda l: (l, rows // HALO - 1, 0, 0)),
-            col_spec,
-            col_spec,
+            pl.BlockSpec((some, HALO, count, cols), lambda l: (l, 0, 0, 0)),
+            pl.BlockSpec((some, HALO, count, cols), lambda l: (l, rows // HALO - 1, 0, 0)),
+            pl.BlockSpec((some, count, LANES), lambda l: (l, 0, 0)),
+            pl.BlockSpec((some, count, LANES), lambda l: (l, 0, 0)),
         ],
-        out_specs=[row_spec] * 2,
+        out_specs=[pl.BlockSpec((some, HALO, count, LANES), lambda l: (l, 0, 0, 0))] * 2,
+        scratch_shapes=[pltpu.VMEM((count, LANES), F32)],
         out_shape=[row_shape] * 2,
         cost_estimate=pl.CostEstimate(flops=10**6, bytes_accessed=2 * 10**6, transcendentals=0),
         name="edge_rows",
@@ -409,7 +474,6 @@
     ratio = NLON // (chem_cols * levs)
     bands = waves // 2
     groups = (chem_rows + 2 * HALO) // levs
-    south = wave >= bands
     width = 2 * fields
 
     owners = waves * levs
@@ -435,30 +499,39 @@
     )
     spread = lax.all_to_all(pieces, both, split_axis=0, concat_axis=0, tiled=True)
     halos = tracer_halos(tracers)
-    inverse, direct = fourier_tables(owners, m_count)
-    spread = spread[:, :used].transpose(1, 0, 2).reshape(groups, 2 * TRUNC, LANES)
-
-    grid = jnp.einsum("gkn,kj->gnj", spread, inverse, preferred_element_type=F32).astype(BF)
-    grid = grid.reshape(groups, ratio, fields, NLON)
+    table = fourier_table(owners, m_count)
+    spread = spread[:, :used].transpose(1, 0, 2)
+    tiles = groups * 2 * UNIT
+    spread = jnp.concatenate(
+        [spread[:tiles].reshape(groups, 2, UNIT, owners, LANES), spread[tiles:].reshape(groups, 2, -1, owners, LANES)],
+        axis=2,
+    ).reshape(groups, 2, TRUNC, LANES)
+
+    sums = jnp.einsum("gckn,ckj->cgnj", spread, table.reshape(2, TRUNC, FOLD), preferred_element_type=F32)
+    cosine, sine, turn = sums[0, ..., :HALF], sums[1, ..., :HALF], sums[0, ..., HALF : HALF + 1]
+    turned = jnp.where(jnp.arange(HALF, dtype=jnp.int32) == 0, turn, cosine - sine)
+    halves = [value.astype(BF).reshape(groups, ratio, fields, HALF) for value in (cosine + sine, turned)]
 
     lane = jnp.arange(LANES, dtype=jnp.int32)
     column = jnp.where(lane < LANES - HALO, lane, lane - LANES)
     column = (column[None, :] + chem_cols * jnp.arange(levs, dtype=jnp.int32)[:, None]) % (chem_cols * levs)
     held = (lane < chem_cols + HALO) | (lane >= LANES - HALO)
     column = jnp.where(held[None, :], column, -1).reshape(levs * LANES)
-    cell = jnp.arange(NLON, dtype=jnp.int32) // ratio
+    order = jnp.arange(NLON, dtype=jnp.int32)
+    cell = jnp.where(order <= HALF, order, NLON + HALF - order) // ratio
     mean = jnp.where(cell[:, None] == column[None, :], 1.0 / ratio**2, 0.0).astype(BF)
-    winds = jnp.einsum("gqfj,jx->gfx", grid[:, :, : 2 * levels], mean, preferred_element_type=F32)
+    winds = sum(
+        jnp.einsum("gqfj,jx->gqfx", half[:, :, : 2 * levels], part, preferred_element_type=F32).sum(axis=1)
+        for half, part in zip(halves, (mean[:HALF], mean[HALF:]))
+    )
     winds = winds.reshape(groups * 2 * levels, levs, LANES).transpose(1, 0, 2)
     winds = lax.all_to_all(winds, "lev", split_axis=0, concat_axis=0, tiled=True)
-    winds = winds.reshape(levs * groups, 2 * levels, LANES)
-    winds = jnp.where(south, jnp.flip(winds, axis=0), winds).transpose(1, 0, 2)
+    winds = winds.reshape(levs * groups, 2 * levels, LANES).transpose(1, 0, 2)
 
     mixing, heating = chemistry(
         tracers, halos, winds, reaction, heat_coeff, wave * chem_rows, chem_rows * waves
     )
-    heating = heating.transpose(1, 0, 2)
-    heating = jnp.where(south, jnp.flip(heating, axis=0), heating).reshape(levs, groups * levels, LANES)
+    heating = heating.transpose(1, 0, 2).reshape(levs, groups * levels, LANES)
     heating = lax.all_to_all(heating, "lev", split_axis=0, concat_axis=0, tiled=True)
     heating = heating.transpose(1, 0, 2).reshape(groups * levels, levs * LANES)
     high = heating.astype(BF)
@@ -466,28 +539,26 @@
     column = jnp.where(lane[None, :] < chem_cols, lane + chem_cols * jnp.arange(levs, dtype=jnp.int32)[:, None], -1)
     copied = (column.reshape(levs * LANES)[:, None] == cell[None, :]).astype(BF)
     heating = jnp.dot(jnp.concatenate([high, low]), copied, preferred_element_type=F32)
-    heating = (heating[: groups * levels] + heating[groups * levels :]).reshape(groups, 1, levels, NLON)
-
-    physics = jnp.tanh(
-        jnp.einsum("ef,gqfj->gqej", phys_matrix, grid.astype(F32), precision=lax.Precision.HIGHEST)
-        + phys_bias[:, None]
-    )
-    tendency = jnp.concatenate(
-        [physics[:, :, : 2 * levels], physics[:, :, 2 * levels : 3 * levels] + heating, physics[:, :, 3 * levels :]],
-        axis=2,
-    ).astype(BF)
-
-    tendency = tendency.reshape(groups * ratio * fields, NLON)
-    coeffs = grid_to_pieces(direct, tendency, owners)
+
+    values, warm = [], []
+    for half in halves:
+        physics = jnp.tanh(
+            jnp.einsum("ef,gqfj->gqej", phys_matrix, half.astype(F32), precision=lax.Precision.HIGHEST)
+            + phys_bias[:, None]
+        )
+        values.append(physics.astype(BF).reshape(groups * ratio * fields, HALF))
+        warm.append(physics[:, :, 2 * levels : 3 * levels].reshape(groups * ratio * levels, HALF))
+
+    coeffs = grid_to_pieces(table, values, warm, heating, owners)
     values = lax.all_to_all(coeffs, both, split_axis=0, concat_axis=0, tiled=True)
 
     result = legendre_call(
         direct_kernel,
         "to_spectral",
-        1,
+        2,
         first_m,
-        [values, jnp.broadcast_to(gauss_weights.reshape(-1, 4).T[:, :, None], (4, half_rows // 4, LANES))],
-        [piece_spec, pl.BlockSpec((4, half_rows // 4, LANES), lambda m: (0, 0, 0))],
+        [values, gauss_weights.reshape(half_rows // 4, 4)],
+        [piece_spec, pl.BlockSpec((half_rows // 4, 4), lambda m: (0, 0))],
         spec_spec,
         jax.ShapeDtypeStruct((m_count, width, k_count), BF),
         geometry,

time: 205 us -> 191 us (0.932)
  Pallas kernels: 91.7 us -> 80.8 us
  waiting for transfers between devices: 40.5 us -> 33.9 us
  local copies, waits for them, and re-layouts: 8.1 us -> 12.5 us
    pallas_call x3, Pallas kernels: 35.3 us -> 26.9 us  [the longest x1 13.3 us: grid_to_pieces(): pl.pallas_call(functools.partial(grid_kernel, owners, steps), grid=(steps...]
    ppermute x4, waiting for transfers between devices: 4.81 us -> 1.11 us  [shift(): lax.ppermute(value, axis, [(i, (i + by) % count) for i in range(count)])]
    convert_element_type x0 -> x3, other arithmetic: none -> 3.63 us  [the longest x1 3.29 us: body(): jnp.where(cell[:, None] == column[None, :], 1.0 / ratio ** 2, 0.0)]
    slice x2 -> x6, local copies, waits for them, and re-layouts: 0.1 us -> 3.11 us  [the longest x2 2.65 us: body(): physics[:, :, 2 * levels:3 * levels].reshape(groups * ratio * levels, HALF)]
    unnamed x20 -> x25, local copies, waits for them, and re-layouts: 1.18 us -> 4.12 us
    broadcast_in_dim x3 -> x1, local copies, waits for them, and re-layouts: 2.75 us -> 0.09 us  [body(): jnp.where(jnp.arange(HALF, dtype=jnp.int32) == 0, turn, cosine - sine)]
    dot_general x3 -> x5, matrix products: 15 us -> 13.1 us  [the longest x2 5.28 us: body(): jnp.einsum('gqfj,jx->gqfx', half[:, :, :2 * levels], part, preferred_elem...]
  transfers between devices with their start and end apart: 8 -> 8, of which waited for: 5 -> 4; matrix products, arithmetic and copies ran while one was open for 11% -> 15% of each run, Pallas kernels for 14% -> 11%
where the time goes in v2:
time: 191 us; the launch traced here: 189 us
  Pallas kernels  80.8 us (42%)
  starting transfers between devices  36.7 us (19%)
  waiting for transfers between devices  33.9 us (18%)
  matrix products  15.8 us (8%)
  local copies, waits for them, and re-layouts  12.5 us (7%)
  other arithmetic  8.28 us (4%)
    pallas_call x2, Pallas kernels, legendre_call(): pl.pallas_call(functools.partial(kernel, geometry), grid=(m_count,), in_s...  34.9 us
    all_to_all x1, waiting for transfers between devices, body(): lax.all_to_all(coeffs, both, split_axis=0, concat_axis=0, tiled=True)  29.4 us
    pallas_call x1, Pallas kernels, grid_to_pieces(): pl.pallas_call(functools.partial(grid_kernel, owners, steps), grid=(steps...  13.3 us
    pallas_call x1, Pallas kernels, chemistry(): pl.pallas_call(functools.partial(chemistry_kernel, total_rows), grid=(lev...  12.4 us
    all_to_all x1, starting transfers between devices, body(): lax.all_to_all(pieces, both, split_axis=0, concat_axis=0, tiled=True)  11.5 us
    pallas_call x1, Pallas kernels, fourier_table(): pl.pallas_call(table_kernel, grid=(rows,), in_specs=[coarse_spec] * 4 + [...  11.5 us
    all_to_all x1, starting transfers between devices, body(): lax.all_to_all(coeffs, both, split_axis=0, concat_axis=0, tiled=True)  11.1 us
    ppermute x4, starting transfers between devices, shift(): lax.ppermute(value, axis, [(i, (i + by) % count) for i in range(count)])  7.21 us
  transfers between devices with their start and end apart: 8, of which 4 were waited for; matrix products, arithmetic and copies ran while one was open for 15% of the time, Pallas kernels for 11%

profile of v2, /device:TPU:1, one launch (start us, length us, event | category | flops | bytes accessed | tf_op | source)
XLA Modules:
  0.0 189.0 jit_solution(11565508472709815873)
XLA Ops:
  0.7 18.4 %to_latitude.1 = bf16[128,64,128]{2,1,0:T(8,128)(2,1)} custom-call(s32[1]{0:T(128)} %bitcast.first_ref, bf16[10,64,1280]{2,1,0:T(8,128)(2,1)} %bitcast.118, bf16[10,640,1280]{2,1,0:T(8,128)(2,1)} %leg_ref.3), custom_call_target="tpu_custom_call" | custom-call | flops 2097152000 | bytes 21384000 | tf_op jit(solution)/shard_map/to_latitude/pallas_call | solution.py:177
  19.1 11.5 %all-to-all-start = ((bf16[128,64,128]{2,1,0:T(8,128)(2,1)}), bf16[128,64,128]{2,1,0:T(8,128)(2,1)S(1)}, u32[]{:S(2)}, u32[]{:S(2)}) async-start(bf16[128,64,128]{2,1,0:T(8,128)(2,1)} %to_latitude.1), calls=%async_computation | async-start | bytes 4194304 | tf_op jit(solution)/shard_map/all_to_all | solution.py:500
  30.6 6.7 %edge_columns.1 = (bf16[8,64,128]{2,1,0:T(8,128)(2,1)}, bf16[8,64,128]{2,1,0:T(8,128)(2,1)}) custom-call(f32[8,20,64,80]{3,2,1,0:T(8,128)} %bitcast.100), custom_call_target="tpu_custom_call" | custom-call | flops 10000000 | bytes 7000000 | tf_op jit(solution)/shard_map/edge_columns/pallas_call | solution.py:395
  37.3 1.5 collective-permute-start
  38.8 2.3 %collective-permute-start.1 = (bf16[8,64,128]{2,1,0:T(8,128)(2,1)}, bf16[8,64,128]{2,1,0:T(8,128)(2,1)S(1)}, u32[]{:S(2)}, u32[]{:S(2)}) collective-permute-start(bf16[8,64,128]{2,1,0:T(8,128)(2,1)} %get-tuple-element.9), channel_id=1, source_target_pairs={{0,7},{1,0},{2,1},{3,2},{4,3},{5,4},{6,5},{7,6},{8,15},{9,8},{10,9... | collective-permute-start | bytes 393224 | tf_op jit(solution)/shard_map/ppermute | solution.py:385
  41.1 0.4 fusion.26
  41.5 0.4 cosine_bitcast_fusion
  42.0 0.8 maximum_multiply_fusion.a_ref
  43.0 1.0 broadcast_multiply_fusion
  44.0 0.8 copy_multiply_fusion.b_ref
  44.8 3.3 %select_convert_fusion = bf16[2560,1024]{1,0:T(8,128)(2,1)} fusion(s32[1024]{0:T(1024)S(1)} %fusion.40, s32[2560]{0:T(1024)S(1)} %add_select_fusion.2), kind=kLoop, calls=%fused_computation | loop fusion | flops 7864320 | bytes 5257216 | tf_op jit(solution)/shard_map/convert_element_type | solution.py:522
  48.1 11.5 %fourier_table.1.table_ref = bf16[2560,1408]{1,0:T(8,128)(2,1)} custom-call(f32[128,128]{1,0:T(8,128)} %get-tuple-element.19.cos_ref, f32[128,128]{1,0:T(8,128)} %get-tuple-element.18.sin_ref, f32[128,128]{1,0:T(8,128)} %get-tuple-element.17.turned_cos_ref, f32[128,128]{1,0:T(8,128)} %get-tuple-element.16.turned_sin_ref, ...), custom_call_target="tpu_custom_call" | custom-call | flops 10813440 | bytes 7208960 | tf_op jit(solution)/shard_map/fourier_table/pallas_call | solution.py:55
  59.6 0.7 pad_maximum_fusion.2.react_ref
  60.3 1.1 collective-permute-done.1.east_ref
  61.4 0.6 copy-done.3
  62.0 2.1 %edge_rows.1 = (bf16[8,2,64,128]{3,2,1,0:T(8,128)(2,1)}, bf16[8,2,64,128]{3,2,1,0:T(8,128)(2,1)}) custom-call(f32[8,20,64,80]{3,2,1,0:T(8,128)} %bitcast.101, f32[8,20,64,80]{3,2,1,0:T(8,128)} %bitcast.102, bf16[8,64,128]{2,1,0:T(8,128)(2,1)} %copy-done.2, bf16[8,64,128]{2,1,0:T(8,128)(2,1)} %copy-done.3), custom_call_target="tpu_custom_call" | custom-call | flops 1000000 | bytes 2000000 | tf_op jit(solution)/shard_map/edge_rows/pallas_call | solution.py:407
  64.1 3.4 %collective-permute-start.2 = (bf16[8,2,64,128]{3,2,1,0:T(8,128)(2,1)}, bf16[8,2,64,128]{3,2,1,0:T(8,128)(2,1)S(1)}, u32[]{:S(2)}, u32[]{:S(2)}) collective-permute-start(bf16[8,2,64,128]{3,2,1,0:T(8,128)(2,1)} %get-tuple-element.10), channel_id=1, source_target_pairs={{0,8},{8,16},{16,24},{24,32},{32,40},{40,48},{48,56},{56,64},{64,7... | collective-permute-start | bytes 786440 | tf_op jit(solution)/shard_map/ppermute | solution.py:385
  67.5 0.2 slice_bitcast_fusion.4
  68.1 0.4 copy.33
  68.5 0.2 pad_maximum_fusion
  68.7 1.1 slice-done
  69.7 1.0 slice-done.1
  70.7 3.3 %fusion.10 = f32[2,3,128,1408]{3,2,1,0:T(8,128)S(1)} fusion(bf16[2,1280,1408,1]{2,1,3,0:T(8,128)(2,1)S(1)} %bitcast.106, bf16[3,2,1280,128]{3,2,1,0:T(8,128)(2,1)S(1)} %bitcast.107), kind=kOutput, calls=%fused_computation.17 | convolution fusion | flops 2768240640 | bytes 13500416 | tf_op jit(solution)/shard_map/gckn,ckj->cgnj/dot_general | solution.py:510
  74.0 0.2 add_convert_fusion
  74.2 0.2 slice_subtract_fusion
  74.6 2.6 %fusion.12 = f32[3,16,1024]{2,1,0:T(8,128)S(1)} fusion(bf16[2560,1024]{1,0:T(8,128)(2,1)} %select_convert_fusion, bf16[3,4,32,1280]{3,2,1,0:T(8,128)(2,1)S(1)} %bitcast.110), kind=kOutput, calls=%fused_computation.22 | convolution fusion | flops 503463936 | bytes 3309568 | tf_op jit(solution)/shard_map/gqfj,jx->gqfx/dot_general | solution.py:524
  77.3 0.2 select_convert_fusion.1
  77.5 2.6 %fusion.13 = f32[3,16,1024]{2,1,0:T(8,128)S(1)} fusion(bf16[2560,1024]{1,0:T(8,128)(2,1)} %select_convert_fusion, bf16[3,4,32,1280]{3,2,1,0:T(8,128)(2,1)S(1)} %select_convert_fusion.1), kind=kOutput, calls=%fused_computation.23 | convolution fusion | flops 503463936 | bytes 3309568 | tf_op jit(solution)/shard_map/gqfj,jx->gqfx/dot_general | solution.py:524
  80.2 0.7 copy.35
  80.9 3.6 %all-to-all-start.1 = ((f32[8,48,128]{2,1,0:T(8,128)}), f32[8,48,128]{2,1,0:T(8,128)S(1)}, u32[]{:S(2)}, u32[]{:S(2)}) async-start(f32[8,48,128]{2,1,0:T(8,128)} %copy.35), calls=%async_computation.1 | async-start | bytes 393216 | tf_op jit(solution)/shard_map/all_to_all | solution.py:528
  84.5 2.6 %fusion.43 = (bf16[3,4,32,1280]{3,2,1,0:T(8,128)(2,1)}, f32[3,4,32,1280]{3,2,1,0:T(8,128)}) fusion(f32[32]{0:T(128)S(1)} %copy-done.8, bf16[3,4,32,1280]{3,2,1,0:T(8,128)(2,1)S(1)} %bitcast.111, f32[32,32]{1,0:T(8,128)S(1)} %copy-done), kind=kOutput, calls=%fused_computation.88 | convolution fusion | flops 189726720 | bytes 3936384 | tf_op jit(solution)/shard_map/ef,gqfj->gqej/dot_general | solution.py:546
  87.1 2.9 %all-to-all-done.1 = f32[8,48,128]{2,1,0:T(8,128)S(1)} async-done(((f32[8,48,128]{2,1,0:T(8,128)}), f32[8,48,128]{2,1,0:T(8,128)S(1)}, u32[]{:S(2)}, u32[]{:S(2)}) %all-to-all-start.1) | async-done | bytes 196640 | tf_op jit(solution)/shard_map/all_to_all | solution.py:528
  90.0 0.7 copy.55
  90.8 0.8 broadcast_in_dim.86.heat_ref
  91.6 12.4 %chemistry.1 = (f32[8,20,64,80]{3,2,1,0:T(8,128)}, f32[8,24,128]{2,1,0:T(8,128)}) custom-call(s32[1]{0:T(128)} %bitcast.23.first_ref, f32[8,20,64,80]{3,2,1,0:T(8,128)} %bitcast.103, bf16[8,2,64,128]{3,2,1,0:T(8,128)(2,1)} %copy-done.4, bf16[8,2,64,128]{3,2,1,0:T(8,128)(2,1)} %copy-done.5, bf16[8,64,128]{2,1,0:T(8,128)(2,1)} %copy-done.2, ...), custom_call_target="tpu_custom_call" | custom-call | flops 1000000000 | bytes 16000000 | tf_op jit(solution)/shard_map/chemistry/pallas_call | solution.py:436
  104.0 1.5 copy.37
  105.5 3.4 %all-to-all-start.2 = ((f32[8,24,128]{2,1,0:T(8,128)}), f32[8,24,128]{2,1,0:T(8,128)S(1)}, u32[]{:S(2)}, u32[]{:S(2)}) async-start(f32[8,24,128]{2,1,0:T(8,128)} %bitcast.35), calls=%async_computation.2 | async-start | bytes 196608 | tf_op jit(solution)/shard_map/all_to_all | solution.py:535
  108.9 1.9 %fusion.44 = (bf16[3,4,32,1280]{3,2,1,0:T(8,128)(2,1)}, f32[3,4,32,1280]{3,2,1,0:T(8,128)S(1)}) fusion(f32[32]{0:T(128)S(1)} %copy-done.8, bf16[3,4,32,1280]{3,2,1,0:T(8,128)(2,1)S(1)} %select_convert_fusion.1, f32[32,32]{1,0:T(8,128)S(1)} %copy-done), kind=kOutput, calls=%fused_computation.89 | convolution fusion | flops 189726720 | bytes 3936384 | tf_op jit(solution)/shard_map/ef,gqfj->gqej/dot_general | solution.py:546
  110.8 1.8 slice.54
  112.7 0.8 slice.55
  113.5 0.5 all-to-all-done.2
  114.0 2.7 %fusion.refs_4_ = f32[48,2560]{1,0:T(8,128)} fusion(s32[2560]{0:T(1024)S(1)} %add_select_fusion.2, s32[1024]{0:T(1024)S(1)} %select_bitcast_fusion, bf16[24,1024]{1,0:T(8,128)(2,1)S(1)} %fusion.16, bf16[24,1024]{1,0:T(8,128)(2,1)S(1)} %bitcast_convert_fusion), kind=kOutput, calls=%fused_computation.1 | convolution fusion | flops 254476288 | bytes 604160 | tf_op jit(solution)/shard_map/dot_general | solution.py:541
  116.7 13.3 %grid_to_pieces.1 = bf16[128,64,128]{2,1,0:T(8,128)(2,1)} custom-call(bf16[2560,1408]{1,0:T(8,128)(2,1)} %fourier_table.1.table_ref, bf16[384,1280]{1,0:T(8,128)(2,1)} %bitcast.112, bf16[384,1280]{1,0:T(8,128)(2,1)} %bitcast.113, f32[96,1280]{1,0:T(8,128)} %bitcast.114, f32[96,1280]{1,0:T(8,128)} %bitcast.115, f32[48,2560]{1,0:T(8,128)} %fusion.refs_4_), custom_call_target="tpu_custom_call" | custom-call | flops 2768240640 | bytes 12208960 | tf_op jit(solution)/shard_map/grid_to_pieces/pallas_call | solution.py:265
  130.0 11.1 %all-to-all-start.3 = ((bf16[128,64,128]{2,1,0:T(8,128)(2,1)}), bf16[128,64,128]{2,1,0:T(8,128)(2,1)S(1)}, u32[]{:S(2)}, u32[]{:S(2)}) async-start(bf16[128,64,128]{2,1,0:T(8,128)(2,1)} %grid_to_pieces.1), calls=%async_computation.3 | async-start | bytes 4194304 | tf_op jit(solution)/shard_map/all_to_all | solution.py:553
  141.0 0.8 reshape.284.weights_ref
  141.8 29.4 %all-to-all-done.3.values_ref = bf16[128,64,128]{2,1,0:T(8,128)(2,1)S(1)} async-done(((bf16[128,64,128]{2,1,0:T(8,128)(2,1)}), bf16[128,64,128]{2,1,0:T(8,128)(2,1)S(1)}, u32[]{:S(2)}, u32[]{:S(2)}) %all-to-all-start.3) | async-done | bytes 2097184 | tf_op jit(solution)/shard_map/all_to_all | solution.py:553
  171.2 1.3 copy-done.1
  172.5 16.5 %to_spectral.1 = bf16[10,64,1280]{2,1,0:T(8,128)(2,1)} custom-call(s32[1]{0:T(128)} %bitcast.first_ref, bf16[128,64,128]{2,1,0:T(8,128)(2,1)} %copy-done.1, f32[160,4]{1,0:T(8,128)} %reshape.284.weights_ref, bf16[10,640,1280]{2,1,0:T(8,128)(2,1)} %leg_ref.3), custom_call_target="tpu_custom_call" | custom-call | flops 2097152000 | bytes 21384000 | tf_op jit(solution)/shard_map/to_spectral/pallas_call | solution.py:177
  (49 shorter events, 1.0 us)
Async XLA Ops:
  0.6 83.9 %copy-start = (f32[32,32]{1,0:T(8,128)S(1)}, f32[32,32]{1,0:T(8,128)}, u32[]{:S(2)}) copy-start(f32[32,32]{1,0:T(8,128)} %param.11) | copy-start | bytes 12292
  19.1 48.5 %all-to-all-start = ((bf16[128,64,128]{2,1,0:T(8,128)(2,1)}), bf16[128,64,128]{2,1,0:T(8,128)(2,1)S(1)}, u32[]{:S(2)}, u32[]{:S(2)}) async-start(bf16[128,64,128]{2,1,0:T(8,128)(2,1)} %to_latitude.1), calls=%async_computation | async-start | bytes 4194304 | tf_op jit(solution)/shard_map/all_to_all | solution.py:500
  30.6 11.5 %copy-start.6 = (f32[64,64]{1,0:T(8,128)S(1)}, f32[64,64]{1,0:T(8,128)}, u32[]{:S(2)}) copy-start(f32[64,64]{1,0:T(8,128)} %param.14) | copy-start | bytes 49156
  37.3 23.0 %collective-permute-start = (bf16[8,64,128]{2,1,0:T(8,128)(2,1)}, bf16[8,64,128]{2,1,0:T(8,128)(2,1)S(1)}, u32[]{:S(2)}, u32[]{:S(2)}) collective-permute-start(bf16[8,64,128]{2,1,0:T(8,128)(2,1)} %get-tuple-element.8), channel_id=1, source_target_pairs={{0,1},{1,2},{2,3},{3,4},{4,5},{5,6},{6,7},{7,0},{8,9},{9,10},{10,1... | collective-permute-start | bytes 393224 | tf_op jit(solution)/shard_map/ppermute | solution.py:385
  38.8 22.6 %collective-permute-start.1 = (bf16[8,64,128]{2,1,0:T(8,128)(2,1)}, bf16[8,64,128]{2,1,0:T(8,128)(2,1)S(1)}, u32[]{:S(2)}, u32[]{:S(2)}) collective-permute-start(bf16[8,64,128]{2,1,0:T(8,128)(2,1)} %get-tuple-element.9), channel_id=1, source_target_pairs={{0,7},{1,0},{2,1},{3,2},{4,3},{5,4},{6,5},{7,6},{8,15},{9,8},{10,9... | collective-permute-start | bytes 393224 | tf_op jit(solution)/shard_map/ppermute | solution.py:385
  60.3 1.1 copy-start.2
  61.4 0.6 copy-start.3
  64.1 26.6 %collective-permute-start.2 = (bf16[8,2,64,128]{3,2,1,0:T(8,128)(2,1)}, bf16[8,2,64,128]{3,2,1,0:T(8,128)(2,1)S(1)}, u32[]{:S(2)}, u32[]{:S(2)}) collective-permute-start(bf16[8,2,64,128]{3,2,1,0:T(8,128)(2,1)} %get-tuple-element.10), channel_id=1, source_target_pairs={{0,8},{8,16},{16,24},{24,32},{32,40},{40,48},{48,56},{56,64},{64,7... | collective-permute-start | bytes 786440 | tf_op jit(solution)/shard_map/ppermute | solution.py:385
  67.5 23.2 %collective-permute-start.3 = (bf16[8,2,64,128]{3,2,1,0:T(8,128)(2,1)}, bf16[8,2,64,128]{3,2,1,0:T(8,128)(2,1)S(1)}, u32[]{:S(2)}, u32[]{:S(2)}) collective-permute-start(bf16[8,2,64,128]{3,2,1,0:T(8,128)(2,1)} %get-tuple-element.11), channel_id=1, source_target_pairs={{0,120},{8,0},{16,8},{24,16},{32,24},{40,32},{48,40},{56,48},{64,5... | collective-permute-start | bytes 786440 | tf_op jit(solution)/shard_map/ppermute | solution.py:385
  67.5 2.2 %slice-start = ((s8[7208960]{0:T(1024)(128)(4,1)}), s8[4194304]{0:T(1024)(128)(4,1)S(1)}, s32[]{:S(2)}) async-start(s8[7208960]{0:T(1024)(128)(4,1)} %bitcast.104), calls=%async_computation.4 | async-start | bytes 8388608
  67.8 2.9 %slice-start.1 = ((s8[7208960]{0:T(1024)(128)(4,1)}), s8[3014656]{0:T(1024)(128)(4,1)S(1)}, s32[]{:S(2)}) async-start(s8[7208960]{0:T(1024)(128)(4,1)} %bitcast.104), calls=%async_computation.5 | async-start | bytes 6029312
  77.5 7.1 %copy-start.8 = (f32[32]{0:T(128)S(1)}, f32[32]{0:T(128)}, u32[]{:S(2)}) copy-start(f32[32]{0:T(128)} %param.12) | copy-start | bytes 388
  80.9 9.1 %all-to-all-start.1 = ((f32[8,48,128]{2,1,0:T(8,128)}), f32[8,48,128]{2,1,0:T(8,128)S(1)}, u32[]{:S(2)}, u32[]{:S(2)}) async-start(f32[8,48,128]{2,1,0:T(8,128)} %copy.35), calls=%async_computation.1 | async-start | bytes 393216 | tf_op jit(solution)/shard_map/all_to_all | solution.py:528
  84.5 6.3 %copy-start.9 = (f32[64]{0:T(128)S(1)}, f32[64]{0:T(128)}, u32[]{:S(2)}) copy-start(f32[64]{0:T(128)} %param.15) | copy-start | bytes 772
  90.8 0.8 copy-start.4
  90.8 0.8 copy-start.5
  105.5 8.4 %all-to-all-start.2 = ((f32[8,24,128]{2,1,0:T(8,128)}), f32[8,24,128]{2,1,0:T(8,128)S(1)}, u32[]{:S(2)}, u32[]{:S(2)}) async-start(f32[8,24,128]{2,1,0:T(8,128)} %bitcast.35), calls=%async_computation.2 | async-start | bytes 196608 | tf_op jit(solution)/shard_map/all_to_all | solution.py:535
  130.0 11.1 %copy-start.7 = (f32[640]{0:T(1024)S(1)}, f32[640]{0:T(1024)}, u32[]{:S(2)}) copy-start(f32[640]{0:T(1024)} %param.10) | copy-start | bytes 7684
  130.0 41.2 %all-to-all-start.3 = ((bf16[128,64,128]{2,1,0:T(8,128)(2,1)}), bf16[128,64,128]{2,1,0:T(8,128)(2,1)S(1)}, u32[]{:S(2)}, u32[]{:S(2)}) async-start(bf16[128,64,128]{2,1,0:T(8,128)(2,1)} %grid_to_pieces.1), calls=%async_computation.3 | async-start | bytes 4194304 | tf_op jit(solution)/shard_map/all_to_all | solution.py:553
  171.2 1.3 copy-start.1

commit v3 on v2

--- a/solution.py
+++ b/solution.py
@@ -23,10 +23,13 @@
 
 def table_kernel(cos_ref, sin_ref, turned_cos_ref, turned_sin_ref, a_ref, b_ref, out_ref):
     step = pl.program_id(0)
-    for block in range(FOLD // LANES):
-        part = slice(block * LANES, (block + 1) * LANES)
-        cos, sin = (turned_cos_ref, turned_sin_ref) if block % 2 else (cos_ref, sin_ref)
-        out_ref[:, part] = (cos[...] * a_ref[0, :, part] - sin[...] * b_ref[0, :, part]).astype(BF)
+    owners = cos_ref.shape[0]
+    for row in range(a_ref.shape[0]):
+        for block in range(FOLD // LANES):
+            part = slice(block * LANES, (block + 1) * LANES)
+            cos, sin = (turned_cos_ref, turned_sin_ref) if block % 2 else (cos_ref, sin_ref)
+            value = cos[...] * a_ref[row, :, part] - sin[...] * b_ref[row, :, part]
+            out_ref[row * owners : (row + 1) * owners, part] = value.astype(BF)
 
     @pl.when(step == 0)
     def _():
@@ -49,12 +52,12 @@
     b = 2.0 * jnp.concatenate([sin, cos])
     rows = 2 * m_count
     coarse_spec = pl.BlockSpec((owners, LANES), lambda i: (0, 0))
-    fine_spec = pl.BlockSpec((1, 1, FOLD), lambda i: (i, 0, 0))
-    out_spec = pl.BlockSpec((owners, FOLD), lambda i: (i, 0))
+    fine_spec = pl.BlockSpec((PARTS, 1, FOLD), lambda i: (i, 0, 0))
+    out_spec = pl.BlockSpec((PARTS * owners, FOLD), lambda i: (i, 0))
     shape = jax.ShapeDtypeStruct((owners * rows, FOLD), BF)
     return pl.pallas_call(
         table_kernel,
-        grid=(rows,),
+        grid=(rows // PARTS,),
         in_specs=[coarse_spec] * 4 + [fine_spec] * 2,
         out_specs=out_spec,
         out_shape=shape,
@@ -287,18 +290,21 @@
 
 
 def edge_columns_kernel(tr_ref, head_ref, tail_ref, pad):
-    rows, count, cols = tr_ref.shape[1:]
+    levels, rows, count, cols = tr_ref.shape
     lanes = lane_ids((count, LANES))
-    head = jnp.zeros((count, LANES), F32)
-    tail = head
-    pad[:, :, :cols] = tr_ref[0]
     gap = LANES - HALO - cols
-    for r in range(rows):
-        line = pad[r]
-        head = jnp.where((lanes >> 1) == r, pltpu.roll(line, 2 * r, 1), head)
-        tail = jnp.where((lanes >> 1) == r + gap // 2, pltpu.roll(line, (2 * r + gap - cols + HALO) % LANES, 1), tail)
-    head_ref[0] = head.astype(BF)
-    tail_ref[0] = tail.astype(BF)
+    for level in range(levels):
+        head = jnp.zeros((count, LANES), F32)
+        tail = head
+        pad[level, :, :, :cols] = tr_ref[level]
+        for r in range(rows):
+            line = pad[level, r]
+            head = jnp.where((lanes >> 1) == r, pltpu.roll(line, 2 * r, 1), head)
+            tail = jnp.where(
+                (lanes >> 1) == r + gap // 2, pltpu.roll(line, (2 * r + gap - cols + HALO) % LANES, 1), tail
+            )
+        head_ref[level] = head.astype(BF)
+        tail_ref[level] = tail.astype(BF)
 
 
 def both_sides(west, east, cols, lanes):
@@ -369,7 +375,7 @@
         both = step(x_ref, r)
         y_ref[r] = both[:, :LANES]
         y_ref[r + 1] = both[:, LANES:]
-    heat = heat_ref[...]
+    heat = jnp.broadcast_to(heat_ref[...], (tracers, LANES))
     heating_ref[0] = jnp.zeros_like(heating_ref[0])
     for r in range(HALO, rows + HALO, 2):
         both = step(y_ref, r)
@@ -385,26 +391,26 @@
     return lax.ppermute(value, axis, [(i, (i + by) % count) for i in range(count)])
 
 
-def tracer_halos(tracers):
+def edge_columns(tracers):
     levels, rows, count, cols = tracers.shape
-    tr_spec = pl.BlockSpec((1, rows, count, cols), lambda l: (l, 0, 0, 0))
-    col_spec = pl.BlockSpec((1, count, LANES), lambda l: (l, 0, 0))
-    col_shape = jax.ShapeDtypeStruct((levels, count, LANES), BF)
-    row_shape = jax.ShapeDtypeStruct((levels, HALO, count, LANES), BF)
-    some = levels // 2
-    head, tail = pl.pallas_call(
+    pair = levels // 4
+    return pl.pallas_call(
         edge_columns_kernel,
-        grid=(levels,),
-        in_specs=[tr_spec],
-        out_specs=[col_spec] * 2,
-        out_shape=[col_shape] * 2,
-        scratch_shapes=[pltpu.VMEM((rows, count, LANES), F32)],
+        grid=(levels // pair,),
+        in_specs=[pl.BlockSpec((pair, rows, count, cols), lambda l: (l, 0, 0, 0))],
+        out_specs=[pl.BlockSpec((pair, count, LANES), lambda l: (l, 0, 0))] * 2,
+        out_shape=[jax.ShapeDtypeStruct((levels, count, LANES), BF)] * 2,
+        scratch_shapes=[pltpu.VMEM((pair, rows, count, LANES), F32)],
         cost_estimate=pl.CostEstimate(flops=10**7, bytes_accessed=7 * 10**6, transcendentals=0),
         name="edge_columns",
     )(tracers)
-    west = shift(tail, "lev", 1)
-    east = shift(head, "lev", -1)
-    top, low = pl.pallas_call(
+
+
+def edge_rows(tracers, west, east):
+    levels, rows, count, cols = tracers.shape
+    row_shape = jax.ShapeDtypeStruct((levels, HALO, count, LANES), BF)
+    some = levels // 2
+    return pl.pallas_call(
         functools.partial(edge_rows_kernel, rows),
         grid=(levels // some,),
         in_specs=[
@@ -419,7 +425,6 @@
         cost_estimate=pl.CostEstimate(flops=10**6, bytes_accessed=2 * 10**6, transcendentals=0),
         name="edge_rows",
     )(tracers, tracers, west, east)
-    return shift(low, "wave", 1), shift(top, "wave", -1), west, east
 
 
 def chemistry(tracers, halos, winds, reaction, heat_coeff, row_first, total_rows):
@@ -428,7 +433,7 @@
     high = reaction.astype(BF)
     low = (reaction - high.astype(F32)).astype(BF)
     react = jnp.concatenate([high, low, high], axis=1)
-    heat = jnp.broadcast_to(heat_coeff[:, None], (count, LANES))
+    heat = heat_coeff[:, None]
     tr_spec = pl.BlockSpec((1, rows, count, cols), lambda l: (l, 0, 0, 0))
     col_spec = pl.BlockSpec((1, count, LANES), lambda l: (l, 0, 0))
     row_spec = pl.BlockSpec((1, HALO, count, LANES), lambda l: (l, 0, 0, 0))
@@ -498,7 +503,8 @@
         legendre,
     )
     spread = lax.all_to_all(pieces, both, split_axis=0, concat_axis=0, tiled=True)
-    halos = tracer_halos(tracers)
+    head, tail = edge_columns(tracers)
+    west, east = shift(tail, "lev", 1), shift(head, "lev", -1)
     table = fourier_table(owners, m_count)
     spread = spread[:, :used].transpose(1, 0, 2)
     tiles = groups * 2 * UNIT
@@ -517,14 +523,18 @@
     column = (column[None, :] + chem_cols * jnp.arange(levs, dtype=jnp.int32)[:, None]) % (chem_cols * levs)
     held = (lane < chem_cols + HALO) | (lane >= LANES - HALO)
     column = jnp.where(held[None, :], column, -1).reshape(levs * LANES)
-    order = jnp.arange(NLON, dtype=jnp.int32)
-    cell = jnp.where(order <= HALF, order, NLON + HALF - order) // ratio
-    mean = jnp.where(cell[:, None] == column[None, :], 1.0 / ratio**2, 0.0).astype(BF)
+    order = jnp.arange(HALF, dtype=jnp.int32)
+    cells = [order // ratio, jnp.where(order == 0, HALF, NLON - order) // ratio]
+    means = [jnp.where(cell[:, None] == column[None, :], 1.0 / ratio**2, 0.0).astype(BF) for cell in cells]
+    cell = jnp.concatenate(cells)
     winds = sum(
         jnp.einsum("gqfj,jx->gqfx", half[:, :, : 2 * levels], part, preferred_element_type=F32).sum(axis=1)
-        for half, part in zip(halves, (mean[:HALF], mean[HALF:]))
+        for half, part in zip(halves, means)
     )
     winds = winds.reshape(groups * 2 * levels, levs, LANES).transpose(1, 0, 2)
+    winds, west, east = lax.optimization_barrier((winds, west, east))
+    top, low = edge_rows(tracers, west, east)
+    halos = (shift(low, "wave", 1), shift(top, "wave", -1), west, east)
     winds = lax.all_to_all(winds, "lev", split_axis=0, concat_axis=0, tiled=True)
     winds = winds.reshape(levs * groups, 2 * levels, LANES).transpose(1, 0, 2)
 

time: 191 us -> 185 us (0.969)
  waiting for transfers between devices: 33.9 us -> 44.4 us
  Pallas kernels: 80.8 us -> 72.6 us
  matrix products: 15.8 us -> 12.4 us
  other arithmetic: 8.28 us -> 4.99 us
  starting transfers between devices: 36.7 us -> 34.6 us
    all_to_all x1, waiting for transfers between devices: 0.01 us -> 11.5 us  [body(): lax.all_to_all(pieces, both, split_axis=0, concat_axis=0, tiled=True)]
    pallas_call x3, Pallas kernels: 20.3 us -> 12.1 us  [the longest x1 5.24 us: fourier_table(): pl.pallas_call(table_kernel, grid=(rows // PARTS,), in_specs=[coarse_spec...]
    dot_general x2, matrix products: 5.28 us -> 1.91 us  [body(): jnp.einsum('gqfj,jx->gqfx', half[:, :, :2 * levels], part, preferred_elem...]
    convert_element_type x1 -> x0, other arithmetic: 3.29 us -> none  [body(): jnp.where(cell[:, None] == column[None, :], 1.0 / ratio ** 2, 0.0)]
  transfers between devices with their start and end apart: 8 -> 8, of which waited for: 4 -> 4; matrix products, arithmetic and copies ran while one was open for 15% -> 12% of each run, Pallas kernels for 11% -> 5%
where the time goes in v3:
time: 185 us; the launch traced here: 183 us
  Pallas kernels  72.6 us (39%)
  waiting for transfers between devices  44.4 us (24%)
  starting transfers between devices  34.6 us (19%)
  local copies, waits for them, and re-layouts  13.3 us (7%)
  matrix products  12.4 us (7%)
  other arithmetic  4.99 us (3%)
    pallas_call x2, Pallas kernels, legendre_call(): pl.pallas_call(functools.partial(kernel, geometry), grid=(m_count,), in_s...  34.8 us
    all_to_all x1, waiting for transfers between devices, body(): lax.all_to_all(coeffs, both, split_axis=0, concat_axis=0, tiled=True)  29.5 us
    pallas_call x1, Pallas kernels, grid_to_pieces(): pl.pallas_call(functools.partial(grid_kernel, owners, steps), grid=(steps...  13.3 us
    pallas_call x1, Pallas kernels, chemistry(): pl.pallas_call(functools.partial(chemistry_kernel, total_rows), grid=(lev...  12.4 us
    all_to_all x1, starting transfers between devices, body(): lax.all_to_all(pieces, both, split_axis=0, concat_axis=0, tiled=True)  11.5 us
    all_to_all x1, waiting for transfers between devices, body(): lax.all_to_all(pieces, both, split_axis=0, concat_axis=0, tiled=True)  11.5 us
    all_to_all x1, starting transfers between devices, body(): lax.all_to_all(coeffs, both, split_axis=0, concat_axis=0, tiled=True)  10.2 us
    ppermute x4, starting transfers between devices, shift(): lax.ppermute(value, axis, [(i, (i + by) % count) for i in range(count)])  5.46 us
  transfers between devices with their start and end apart: 8, of which 4 were waited for; matrix products, arithmetic and copies ran while one was open for 12% of the time, Pallas kernels for 5%

profile of v3, /device:TPU:1, one launch (start us, length us, event | category | flops | bytes accessed | tf_op | source)
XLA Modules:
  0.0 183.2 jit_solution(8707825931684040765)
XLA Ops:
  0.7 18.3 %to_latitude.1 = bf16[128,64,128]{2,1,0:T(8,128)(2,1)} custom-call(s32[1]{0:T(128)} %bitcast.first_ref, bf16[10,64,1280]{2,1,0:T(8,128)(2,1)} %bitcast.119, bf16[10,640,1280]{2,1,0:T(8,128)(2,1)} %leg_ref.3), custom_call_target="tpu_custom_call" | custom-call | flops 2097152000 | bytes 21384000 | tf_op jit(solution)/shard_map/to_latitude/pallas_call | solution.py:180
  19.0 11.5 %all-to-all-start = ((bf16[128,64,128]{2,1,0:T(8,128)(2,1)}), bf16[128,64,128]{2,1,0:T(8,128)(2,1)S(1)}, u32[]{:S(2)}, u32[]{:S(2)}) async-start(bf16[128,64,128]{2,1,0:T(8,128)(2,1)} %to_latitude.1), calls=%async_computation | async-start | bytes 4194304 | tf_op jit(solution)/shard_map/all_to_all | solution.py:505
  30.5 4.8 %edge_columns.1 = (bf16[8,64,128]{2,1,0:T(8,128)(2,1)}, bf16[8,64,128]{2,1,0:T(8,128)(2,1)}) custom-call(f32[8,20,64,80]{3,2,1,0:T(8,128)} %bitcast.101), custom_call_target="tpu_custom_call" | custom-call | flops 10000000 | bytes 7000000 | tf_op jit(solution)/shard_map/edge_columns/pallas_call | solution.py:397
  35.3 1.5 collective-permute-start
  36.8 2.3 %collective-permute-start.1 = (bf16[8,64,128]{2,1,0:T(8,128)(2,1)}, bf16[8,64,128]{2,1,0:T(8,128)(2,1)S(1)}, u32[]{:S(2)}, u32[]{:S(2)}) collective-permute-start(bf16[8,64,128]{2,1,0:T(8,128)(2,1)} %get-tuple-element.12), channel_id=1, source_target_pairs={{0,7},{1,0},{2,1},{3,2},{4,3},{5,4},{6,5},{7,6},{8,15},{9,8},{10,9... | collective-permute-start | bytes 393224 | tf_op jit(solution)/shard_map/ppermute | solution.py:391
  39.1 0.4 fusion.38
  39.4 0.4 cosine_bitcast_fusion
  40.0 1.1 broadcast_multiply_fusion
  41.0 0.8 maximum_multiply_fusion.a_ref
  41.8 0.7 copy.40.heat_ref
  42.5 0.8 copy_multiply_fusion.b_ref
  43.2 5.2 %fourier_table.1.table_ref = bf16[2560,1408]{1,0:T(8,128)(2,1)} custom-call(f32[128,128]{1,0:T(8,128)} %get-tuple-element.25.cos_ref, f32[128,128]{1,0:T(8,128)} %get-tuple-element.24.sin_ref, f32[128,128]{1,0:T(8,128)} %get-tuple-element.23.turned_cos_ref, f32[128,128]{1,0:T(8,128)} %get-tuple-element.22.turned_sin_ref, ...), custom_call_target="tpu_custom_call" | custom-call | flops 10813440 | bytes 7208960 | tf_op jit(solution)/shard_map/fourier_table/pallas_call | solution.py:58
  48.6 0.7 pad_maximum_fusion.2.react_ref
  49.4 11.5 %all-to-all-done = bf16[128,64,128]{2,1,0:T(8,128)(2,1)S(1)} async-done(((bf16[128,64,128]{2,1,0:T(8,128)(2,1)}), bf16[128,64,128]{2,1,0:T(8,128)(2,1)S(1)}, u32[]{:S(2)}, u32[]{:S(2)}) %all-to-all-start) | async-done | bytes 2097184 | tf_op jit(solution)/shard_map/all_to_all | solution.py:505
  60.9 0.2 slice_bitcast_fusion
  61.4 0.4 copy.36
  61.8 0.2 pad_maximum_fusion
  62.0 1.1 slice-done
  63.1 1.0 slice-done.1
  64.1 3.3 %fusion.18 = f32[2,3,128,1408]{3,2,1,0:T(8,128)S(1)} fusion(bf16[2,1280,1408,1]{2,1,3,0:T(8,128)(2,1)S(1)} %bitcast.107, bf16[3,2,1280,128]{3,2,1,0:T(8,128)(2,1)S(1)} %bitcast.108), kind=kOutput, calls=%fused_computation.22 | convolution fusion | flops 2768240640 | bytes 13500416 | tf_op jit(solution)/shard_map/gckn,ckj->cgnj/dot_general | solution.py:516
  67.4 0.2 add_convert_fusion
  67.6 0.2 slice_subtract_fusion
  68.0 1.0 fusion.20
  69.1 0.9 fusion.23
  70.2 0.6 copy-done.2
  70.9 2.1 %edge_rows.1 = (bf16[8,2,64,128]{3,2,1,0:T(8,128)(2,1)}, bf16[8,2,64,128]{3,2,1,0:T(8,128)(2,1)}) custom-call(f32[8,20,64,80]{3,2,1,0:T(8,128)} %bitcast.102, f32[8,20,64,80]{3,2,1,0:T(8,128)} %bitcast.103, bf16[8,64,128]{2,1,0:T(8,128)(2,1)} %copy-done.2, bf16[8,64,128]{2,1,0:T(8,128)(2,1)} %copy-done.3), custom_call_target="tpu_custom_call" | custom-call | flops 1000000 | bytes 2000000 | tf_op jit(solution)/shard_map/edge_rows/pallas_call | solution.py:413
  73.0 1.1 collective-permute-start.2
  74.1 0.6 collective-permute-start.3
  74.7 0.7 copy.38
  75.4 3.4 %all-to-all-start.1 = ((f32[8,48,128]{2,1,0:T(8,128)}), f32[8,48,128]{2,1,0:T(8,128)S(1)}, u32[]{:S(2)}, u32[]{:S(2)}) async-start(f32[8,48,128]{2,1,0:T(8,128)} %copy.38), calls=%async_computation.1 | async-start | bytes 393216 | tf_op jit(solution)/shard_map/all_to_all | solution.py:538
  78.8 2.6 %fusion.62 = (bf16[3,4,32,1280]{3,2,1,0:T(8,128)(2,1)}, f32[3,4,32,1280]{3,2,1,0:T(8,128)}) fusion(f32[32]{0:T(128)S(1)} %copy-done.8, bf16[3,4,32,1280]{3,2,1,0:T(8,128)(2,1)S(1)} %bitcast.112, f32[32,32]{1,0:T(8,128)S(1)} %copy-done), kind=kOutput, calls=%fused_computation.105 | convolution fusion | flops 189726720 | bytes 3936384 | tf_op jit(solution)/shard_map/ef,gqfj->gqej/dot_general | solution.py:556
  81.4 2.9 %all-to-all-done.1 = f32[8,48,128]{2,1,0:T(8,128)S(1)} async-done(((f32[8,48,128]{2,1,0:T(8,128)}), f32[8,48,128]{2,1,0:T(8,128)S(1)}, u32[]{:S(2)}, u32[]{:S(2)}) %all-to-all-start.1) | async-done | bytes 196640 | tf_op jit(solution)/shard_map/all_to_all | solution.py:538
  84.2 0.7 copy.59
  85.0 0.7 copy-done.4
  85.8 12.4 %chemistry.1 = (f32[8,20,64,80]{3,2,1,0:T(8,128)}, f32[8,24,128]{2,1,0:T(8,128)}) custom-call(s32[1]{0:T(128)} %bitcast.23.first_ref, f32[8,20,64,80]{3,2,1,0:T(8,128)} %bitcast.104, bf16[8,2,64,128]{3,2,1,0:T(8,128)(2,1)} %copy-done.4, bf16[8,2,64,128]{3,2,1,0:T(8,128)(2,1)} %copy-done.5, bf16[8,64,128]{2,1,0:T(8,128)(2,1)} %copy-done.2, ...), custom_call_target="tpu_custom_call" | custom-call | flops 1000000000 | bytes 16000000 | tf_op jit(solution)/shard_map/chemistry/pallas_call | solution.py:441
  98.2 1.6 copy.41
  99.7 4.1 %all-to-all-start.2 = ((f32[8,24,128]{2,1,0:T(8,128)}), f32[8,24,128]{2,1,0:T(8,128)S(1)}, u32[]{:S(2)}, u32[]{:S(2)}) async-start(f32[8,24,128]{2,1,0:T(8,128)} %bitcast.36), calls=%async_computation.2 | async-start | bytes 196608 | tf_op jit(solution)/shard_map/all_to_all | solution.py:545
  103.8 1.9 %fusion.63 = (bf16[3,4,32,1280]{3,2,1,0:T(8,128)(2,1)}, f32[3,4,32,1280]{3,2,1,0:T(8,128)S(1)}) fusion(f32[32]{0:T(128)S(1)} %copy-done.8, bf16[3,4,32,1280]{3,2,1,0:T(8,128)(2,1)S(1)} %select_convert_fusion.2, f32[32,32]{1,0:T(8,128)S(1)} %copy-done), kind=kOutput, calls=%fused_computation.106 | convolution fusion | flops 189726720 | bytes 3936384 | tf_op jit(solution)/shard_map/ef,gqfj->gqej/dot_general | solution.py:556
  105.8 1.9 %slice.46 = f32[3,4,8,1280]{3,2,1,0:T(8,128)} slice(f32[3,4,32,1280]{3,2,1,0:T(8,128)} %get-tuple-element.27), slice={[0:3], [0:4], [16:24], [0:1280]} | slice | bytes 983040 | tf_op jit(solution)/shard_map/slice | solution.py:560
  107.6 0.8 slice.47
  108.4 0.5 all-to-all-done.2
  109.0 2.7 %fusion.refs_4_ = f32[48,2560]{1,0:T(8,128)} fusion(s32[2560]{0:T(1024)S(1)} %pad_add_fusion, s32[1024]{0:T(1024)S(1)} %select_bitcast_fusion, bf16[24,1024]{1,0:T(8,128)(2,1)S(1)} %fusion.28, bf16[24,1024]{1,0:T(8,128)(2,1)S(1)} %bitcast_convert_fusion), kind=kOutput, calls=%fused_computation | convolution fusion | flops 254476288 | bytes 604160 | tf_op jit(solution)/shard_map/dot_general | solution.py:551
  111.7 13.3 %grid_to_pieces.1 = bf16[128,64,128]{2,1,0:T(8,128)(2,1)} custom-call(bf16[2560,1408]{1,0:T(8,128)(2,1)} %fourier_table.1.table_ref, bf16[384,1280]{1,0:T(8,128)(2,1)} %bitcast.113, bf16[384,1280]{1,0:T(8,128)(2,1)} %bitcast.114, f32[96,1280]{1,0:T(8,128)} %bitcast.115, f32[96,1280]{1,0:T(8,128)} %bitcast.116, f32[48,2560]{1,0:T(8,128)} %fusion.refs_4_), custom_call_target="tpu_custom_call" | custom-call | flops 2768240640 | bytes 12208960 | tf_op jit(solution)/shard_map/grid_to_pieces/pallas_call | solution.py:268
  125.0 10.2 %all-to-all-start.3 = ((bf16[128,64,128]{2,1,0:T(8,128)(2,1)}), bf16[128,64,128]{2,1,0:T(8,128)(2,1)S(1)}, u32[]{:S(2)}, u32[]{:S(2)}) async-start(bf16[128,64,128]{2,1,0:T(8,128)(2,1)} %grid_to_pieces.1), calls=%async_computation.3 | async-start | bytes 4194304 | tf_op jit(solution)/shard_map/all_to_all | solution.py:563
  135.2 0.7 reshape.275.weights_ref
  136.0 29.5 %all-to-all-done.3.values_ref = bf16[128,64,128]{2,1,0:T(8,128)(2,1)S(1)} async-done(((bf16[128,64,128]{2,1,0:T(8,128)(2,1)}), bf16[128,64,128]{2,1,0:T(8,128)(2,1)S(1)}, u32[]{:S(2)}, u32[]{:S(2)}) %all-to-all-start.3) | async-done | bytes 2097184 | tf_op jit(solution)/shard_map/all_to_all | solution.py:563
  165.5 1.3 copy-done.1
  166.8 16.5 %to_spectral.1 = bf16[10,64,1280]{2,1,0:T(8,128)(2,1)} custom-call(s32[1]{0:T(128)} %bitcast.first_ref, bf16[128,64,128]{2,1,0:T(8,128)(2,1)} %copy-done.1, f32[160,4]{1,0:T(8,128)} %reshape.275.weights_ref, bf16[10,640,1280]{2,1,0:T(8,128)(2,1)} %leg_ref.3), custom_call_target="tpu_custom_call" | custom-call | flops 2097152000 | bytes 21384000 | tf_op jit(solution)/shard_map/to_spectral/pallas_call | solution.py:180
  (49 shorter events, 1.3 us)
Async XLA Ops:
  0.6 78.2 %copy-start = (f32[32,32]{1,0:T(8,128)S(1)}, f32[32,32]{1,0:T(8,128)}, u32[]{:S(2)}) copy-start(f32[32,32]{1,0:T(8,128)} %param.11) | copy-start | bytes 12292
  19.0 41.9 %all-to-all-start = ((bf16[128,64,128]{2,1,0:T(8,128)(2,1)}), bf16[128,64,128]{2,1,0:T(8,128)(2,1)S(1)}, u32[]{:S(2)}, u32[]{:S(2)}) async-start(bf16[128,64,128]{2,1,0:T(8,128)(2,1)} %to_latitude.1), calls=%async_computation | async-start | bytes 4194304 | tf_op jit(solution)/shard_map/all_to_all | solution.py:505
  30.5 11.3 %copy-start.9 = (f32[64]{0:T(128)S(1)}, f32[64]{0:T(128)}, u32[]{:S(2)}) copy-start(f32[64]{0:T(128)} %param.15) | copy-start | bytes 772
  35.3 34.9 %collective-permute-start = (bf16[8,64,128]{2,1,0:T(8,128)(2,1)}, bf16[8,64,128]{2,1,0:T(8,128)(2,1)S(1)}, u32[]{:S(2)}, u32[]{:S(2)}) collective-permute-start(bf16[8,64,128]{2,1,0:T(8,128)(2,1)} %get-tuple-element.11), channel_id=1, source_target_pairs={{0,1},{1,2},{2,3},{3,4},{4,5},{5,6},{6,7},{7,0},{8,9},{9,10},{10,1... | collective-permute-start | bytes 393224 | tf_op jit(solution)/shard_map/ppermute | solution.py:391
  36.8 33.4 %collective-permute-start.1 = (bf16[8,64,128]{2,1,0:T(8,128)(2,1)}, bf16[8,64,128]{2,1,0:T(8,128)(2,1)S(1)}, u32[]{:S(2)}, u32[]{:S(2)}) collective-permute-start(bf16[8,64,128]{2,1,0:T(8,128)(2,1)} %get-tuple-element.12), channel_id=1, source_target_pairs={{0,7},{1,0},{2,1},{3,2},{4,3},{5,4},{6,5},{7,6},{8,15},{9,8},{10,9... | collective-permute-start | bytes 393224 | tf_op jit(solution)/shard_map/ppermute | solution.py:391
  43.2 5.3 %copy-start.6 = (f32[64,64]{1,0:T(8,128)S(1)}, f32[64,64]{1,0:T(8,128)}, u32[]{:S(2)}) copy-start(f32[64,64]{1,0:T(8,128)} %param.14) | copy-start | bytes 49156
  60.9 2.2 %slice-start = ((s8[7208960]{0:T(1024)(128)(4,1)}), s8[4194304]{0:T(1024)(128)(4,1)S(1)}, s32[]{:S(2)}) async-start(s8[7208960]{0:T(1024)(128)(4,1)} %bitcast.105), calls=%async_computation.4 | async-start | bytes 8388608
  61.1 2.9 %slice-start.1 = ((s8[7208960]{0:T(1024)(128)(4,1)}), s8[3014656]{0:T(1024)(128)(4,1)S(1)}, s32[]{:S(2)}) async-start(s8[7208960]{0:T(1024)(128)(4,1)} %bitcast.105), calls=%async_computation.5 | async-start | bytes 6029312
  70.2 0.7 copy-start.2
  70.2 0.7 copy-start.3
  70.9 7.9 %copy-start.8 = (f32[32]{0:T(128)S(1)}, f32[32]{0:T(128)}, u32[]{:S(2)}) copy-start(f32[32]{0:T(128)} %param.12) | copy-start | bytes 388
  73.0 12.0 %collective-permute-start.2 = (bf16[8,2,64,128]{3,2,1,0:T(8,128)(2,1)}, bf16[8,2,64,128]{3,2,1,0:T(8,128)(2,1)S(1)}, u32[]{:S(2)}, u32[]{:S(2)}) collective-permute-start(bf16[8,2,64,128]{3,2,1,0:T(8,128)(2,1)} %get-tuple-element.15), channel_id=1, source_target_pairs={{0,8},{8,16},{16,24},{24,32},{32,40},{40,48},{48,56},{56,64},{64,7... | collective-permute-start | bytes 786440 | tf_op jit(solution)/shard_map/ppermute | solution.py:391
  74.1 10.9 %collective-permute-start.3 = (bf16[8,2,64,128]{3,2,1,0:T(8,128)(2,1)}, bf16[8,2,64,128]{3,2,1,0:T(8,128)(2,1)S(1)}, u32[]{:S(2)}, u32[]{:S(2)}) collective-permute-start(bf16[8,2,64,128]{3,2,1,0:T(8,128)(2,1)} %get-tuple-element.16), channel_id=1, source_target_pairs={{0,120},{8,0},{16,8},{24,16},{32,24},{40,32},{48,40},{56,48},{64,5... | collective-permute-start | bytes 786440 | tf_op jit(solution)/shard_map/ppermute | solution.py:391
  75.4 8.9 %all-to-all-start.1 = ((f32[8,48,128]{2,1,0:T(8,128)}), f32[8,48,128]{2,1,0:T(8,128)S(1)}, u32[]{:S(2)}, u32[]{:S(2)}) async-start(f32[8,48,128]{2,1,0:T(8,128)} %copy.38), calls=%async_computation.1 | async-start | bytes 393216 | tf_op jit(solution)/shard_map/all_to_all | solution.py:538
  85.0 0.7 copy-start.4
  85.0 0.8 copy-start.5
  99.7 9.3 %all-to-all-start.2 = ((f32[8,24,128]{2,1,0:T(8,128)}), f32[8,24,128]{2,1,0:T(8,128)S(1)}, u32[]{:S(2)}, u32[]{:S(2)}) async-start(f32[8,24,128]{2,1,0:T(8,128)} %bitcast.36), calls=%async_computation.2 | async-start | bytes 196608 | tf_op jit(solution)/shard_map/all_to_all | solution.py:545
  125.0 10.2 %copy-start.7 = (f32[640]{0:T(1024)S(1)}, f32[640]{0:T(1024)}, u32[]{:S(2)}) copy-start(f32[640]{0:T(1024)} %param.10) | copy-start | bytes 7684
  125.0 40.4 %all-to-all-start.3 = ((bf16[128,64,128]{2,1,0:T(8,128)(2,1)}), bf16[128,64,128]{2,1,0:T(8,128)(2,1)S(1)}, u32[]{:S(2)}, u32[]{:S(2)}) async-start(bf16[128,64,128]{2,1,0:T(8,128)(2,1)} %grid_to_pieces.1), calls=%async_computation.3 | async-start | bytes 4194304 | tf_op jit(solution)/shard_map/all_to_all | solution.py:563
  165.5 1.3 copy-start.1

commit v4 on v3

--- a/solution.py
+++ b/solution.py
@@ -16,6 +16,7 @@
 LANES = 128
 FOLD = HALF + LANES
 PIECE_ROWS = 64
+DEPTH = 3
 UNIT = 8
 HALO = 2
 BF, F32 = jnp.bfloat16, jnp.float32
@@ -83,16 +84,34 @@
     return (k < TRUNC - m) & ((row < part_rows) | (m > 0)), k % 2 == 0
 
 
-def inverse_kernel(geometry, first_ref, spec_ref, leg_ref, out_ref, z_ref, q_ref, x_ref, turned_ref):
+def table_copy(leg_ref, table_ref, sem, m):
+    slot = m % DEPTH
+    return pltpu.make_async_copy(leg_ref.at[m], table_ref.at[slot], sem.at[slot])
+
+
+def start_copies(leg_ref, table_ref, sem, step, count):
+    @pl.when(step == 0)
+    def _():
+        for m in range(DEPTH - 1):
+            table_copy(leg_ref, table_ref, sem, m).start()
+
+    @pl.when(step + DEPTH - 1 < count)
+    def _():
+        table_copy(leg_ref, table_ref, sem, step + DEPTH - 1).start()
+
+
+def inverse_kernel(geometry, first_ref, spec_ref, leg_ref, out_ref, z_ref, q_ref, x_ref, turned_ref, table_ref, sem):
     waves, levs, groups, bands, band_groups, m_count = geometry
     half_rows = leg_ref.shape[1]
     step = pl.program_id(0)
+    start_copies(leg_ref, table_ref, sem, step, m_count)
     spec = spec_ref[0].astype(F32)
     keep, even = kept(first_ref[0] + step, spec.shape, spec.shape[0] // 2)
     spec = jnp.where(keep, spec, 0.0)
     other = jnp.where(even, spec, -spec)
     stacked = jnp.concatenate([spec, other, other, spec], axis=0).astype(BF)
-    values = lax.dot_general(leg_ref[0], stacked, (((1,), (1,)), ((), ())), preferred_element_type=F32)
+    table_copy(leg_ref, table_ref, sem, step).wait()
+    values = lax.dot_general(table_ref[step % DEPTH], stacked, (((1,), (1,)), ((), ())), preferred_element_type=F32)
     x_ref[...] = values[:, :LANES]
     turned_ref[...] = values[:, LANES:]
     quarter = half_rows // 4
@@ -124,10 +143,11 @@
         lax.fori_loop(0, waves, of_wave, 0)
 
 
-def direct_kernel(geometry, first_ref, values_ref, weights_ref, leg_ref, out_ref, z_ref, q_ref, x_ref, w_ref):
+def direct_kernel(geometry, first_ref, values_ref, weights_ref, leg_ref, out_ref, z_ref, q_ref, x_ref, w_ref, table_ref, sem):
     waves, levs, groups, bands, band_groups, m_count = geometry
     half_rows = leg_ref.shape[1]
     step = pl.program_id(0)
+    start_copies(leg_ref, table_ref, sem, step, m_count)
 
     @pl.when(step == 0)
     def _():
@@ -159,7 +179,8 @@
     for q, value in enumerate(exchanged(x, [pltpu.roll(i, 64, 1) for i in x])):
         x_ref[pl.ds(q, quarter, stride=4), :] = w_ref[pl.ds(q * quarter, quarter), :] * value
     paired = x_ref[...].astype(BF)
-    folded = lax.dot_general(paired, leg_ref[0], (((0,), (0,)), ((), ())), preferred_element_type=F32)
+    table_copy(leg_ref, table_ref, sem, step).wait()
+    folded = lax.dot_general(paired, table_ref[step % DEPTH], (((0,), (0,)), ((), ())), preferred_element_type=F32)
     half = folded.shape[0] // 2
     keep, even = kept(first_ref[0] + step, (half, folded.shape[1]), half // 2)
     chosen = jnp.where(even, folded[:half], folded[half:])
@@ -182,14 +203,15 @@
         grid=(m_count,),
         in_specs=[pl.BlockSpec(memory_space=pltpu.SMEM)]
         + in_specs
-        + [pl.BlockSpec((1, half_rows, k_count), lambda m: (m, 0, 0))],
+        + [pl.BlockSpec(memory_space=pl.ANY)],
         out_specs=out_spec,
         out_shape=out_shape,
         scratch_shapes=[
             pltpu.VMEM((m_count * half_rows, LANES), F32),
             pltpu.VMEM((levs, PIECE_ROWS, LANES), F32),
         ]
-        + [pltpu.VMEM((half_rows, LANES), F32)] * extra,
+        + [pltpu.VMEM((half_rows, LANES), F32)] * extra
+        + [pltpu.VMEM((DEPTH, half_rows, k_count), BF), pltpu.SemaphoreType.DMA((DEPTH,))],
         cost_estimate=pl.CostEstimate(
             flops=2 * legendre.size * LANES, bytes_accessed=2 * legendre.size + 5 * 10**6, transcendentals=0
         ),

time: 185 us -> 180 us (0.973)
  Pallas kernels: 72.6 us -> 68.4 us
    pallas_call x2, Pallas kernels: 34.8 us -> 30.6 us  [legendre_call(): pl.pallas_call(functools.partial(kernel, geometry), grid=(m_count,), in_s...]
  transfers between devices with their start and end apart: 8 -> 8, of which waited for: 4 -> 4; matrix products, arithmetic and copies ran while one was open for 12% -> 12% of each run, Pallas kernels for 5% -> 6%
where the time goes in v4:
time: 180 us; the launch traced here: 179 us
  Pallas kernels  68.4 us (38%)
  waiting for transfers between devices  44.4 us (25%)
  starting transfers between devices  34.6 us (19%)
  local copies, waits for them, and re-layouts  13.3 us (7%)
  matrix products  12.4 us (7%)
  other arithmetic  4.99 us (3%)
    pallas_call x2, Pallas kernels, legendre_call(): pl.pallas_call(functools.partial(kernel, geometry), grid=(m_count,), in_s...  30.6 us
    all_to_all x1, waiting for transfers between devices, body(): lax.all_to_all(coeffs, both, split_axis=0, concat_axis=0, tiled=True)  29.5 us
    pallas_call x1, Pallas kernels, grid_to_pieces(): pl.pallas_call(functools.partial(grid_kernel, owners, steps), grid=(steps...  13.3 us
    pallas_call x1, Pallas kernels, chemistry(): pl.pallas_call(functools.partial(chemistry_kernel, total_rows), grid=(lev...  12.4 us
    all_to_all x1, starting transfers between devices, body(): lax.all_to_all(pieces, both, split_axis=0, concat_axis=0, tiled=True)  11.5 us
    all_to_all x1, waiting for transfers between devices, body(): lax.all_to_all(pieces, both, split_axis=0, concat_axis=0, tiled=True)  11.5 us
    all_to_all x1, starting transfers between devices, body(): lax.all_to_all(coeffs, both, split_axis=0, concat_axis=0, tiled=True)  10.2 us
    ppermute x4, starting transfers between devices, shift(): lax.ppermute(value, axis, [(i, (i + by) % count) for i in range(count)])  5.46 us
  transfers between devices with their start and end apart: 8, of which 4 were waited for; matrix products, arithmetic and copies ran while one was open for 12% of the time, Pallas kernels for 6%

profile of v4, /device:TPU:1, one launch (start us, length us, event | category | flops | bytes accessed | tf_op | source)
XLA Modules:
  0.0 179.2 jit_solution(15310912335758227239)
XLA Ops:
  0.7 17.4 %to_latitude.1 = bf16[128,64,128]{2,1,0:T(8,128)(2,1)} custom-call(s32[1]{0:T(128)} %bitcast.first_ref, bf16[10,64,1280]{2,1,0:T(8,128)(2,1)} %bitcast.119, bf16[10,640,1280]{2,1,0:T(8,128)(2,1)} %leg_ref.3), custom_call_target="tpu_custom_call" | custom-call | flops 2097152000 | bytes 21384000 | tf_op jit(solution)/shard_map/to_latitude/pallas_call | solution.py:201
  18.0 11.5 %all-to-all-start = ((bf16[128,64,128]{2,1,0:T(8,128)(2,1)}), bf16[128,64,128]{2,1,0:T(8,128)(2,1)S(1)}, u32[]{:S(2)}, u32[]{:S(2)}) async-start(bf16[128,64,128]{2,1,0:T(8,128)(2,1)} %to_latitude.1), calls=%async_computation | async-start | bytes 4194304 | tf_op jit(solution)/shard_map/all_to_all | solution.py:527
  29.5 4.8 %edge_columns.1 = (bf16[8,64,128]{2,1,0:T(8,128)(2,1)}, bf16[8,64,128]{2,1,0:T(8,128)(2,1)}) custom-call(f32[8,20,64,80]{3,2,1,0:T(8,128)} %bitcast.101), custom_call_target="tpu_custom_call" | custom-call | flops 10000000 | bytes 7000000 | tf_op jit(solution)/shard_map/edge_columns/pallas_call | solution.py:419
  34.3 1.5 collective-permute-start
  35.8 2.3 %collective-permute-start.1 = (bf16[8,64,128]{2,1,0:T(8,128)(2,1)}, bf16[8,64,128]{2,1,0:T(8,128)(2,1)S(1)}, u32[]{:S(2)}, u32[]{:S(2)}) collective-permute-start(bf16[8,64,128]{2,1,0:T(8,128)(2,1)} %get-tuple-element.12), channel_id=1, source_target_pairs={{0,7},{1,0},{2,1},{3,2},{4,3},{5,4},{6,5},{7,6},{8,15},{9,8},{10,9... | collective-permute-start | bytes 393224 | tf_op jit(solution)/shard_map/ppermute | solution.py:413
  38.1 0.4 fusion.38
  38.5 0.4 cosine_bitcast_fusion
  39.0 1.1 broadcast_multiply_fusion
  40.1 0.8 maximum_multiply_fusion.a_ref
  40.8 0.7 copy.40.heat_ref
  41.5 0.8 copy_multiply_fusion.b_ref
  42.3 5.2 %fourier_table.1.table_ref = bf16[2560,1408]{1,0:T(8,128)(2,1)} custom-call(f32[128,128]{1,0:T(8,128)} %get-tuple-element.25.cos_ref, f32[128,128]{1,0:T(8,128)} %get-tuple-element.24.sin_ref, f32[128,128]{1,0:T(8,128)} %get-tuple-element.23.turned_cos_ref, f32[128,128]{1,0:T(8,128)} %get-tuple-element.22.turned_sin_ref, ...), custom_call_target="tpu_custom_call" | custom-call | flops 10813440 | bytes 7208960 | tf_op jit(solution)/shard_map/fourier_table/pallas_call | solution.py:59
  47.6 0.7 pad_maximum_fusion.2.react_ref
  48.5 11.5 %all-to-all-done = bf16[128,64,128]{2,1,0:T(8,128)(2,1)S(1)} async-done(((bf16[128,64,128]{2,1,0:T(8,128)(2,1)}), bf16[128,64,128]{2,1,0:T(8,128)(2,1)S(1)}, u32[]{:S(2)}, u32[]{:S(2)}) %all-to-all-start) | async-done | bytes 2097184 | tf_op jit(solution)/shard_map/all_to_all | solution.py:527
  59.9 0.2 slice_bitcast_fusion
  60.4 0.4 copy.36
  60.9 0.2 pad_maximum_fusion
  61.0 1.1 slice-done
  62.1 1.0 slice-done.1
  63.1 3.3 %fusion.18 = f32[2,3,128,1408]{3,2,1,0:T(8,128)S(1)} fusion(bf16[2,1280,1408,1]{2,1,3,0:T(8,128)(2,1)S(1)} %bitcast.107, bf16[3,2,1280,128]{3,2,1,0:T(8,128)(2,1)S(1)} %bitcast.108), kind=kOutput, calls=%fused_computation.22 | convolution fusion | flops 2768240640 | bytes 13500416 | tf_op jit(solution)/shard_map/gckn,ckj->cgnj/dot_general | solution.py:538
  66.4 0.2 add_convert_fusion
  66.6 0.2 slice_subtract_fusion
  67.0 1.0 fusion.20
  68.1 0.9 fusion.23
  69.2 0.6 copy-done.2
  69.9 2.1 %edge_rows.1 = (bf16[8,2,64,128]{3,2,1,0:T(8,128)(2,1)}, bf16[8,2,64,128]{3,2,1,0:T(8,128)(2,1)}) custom-call(f32[8,20,64,80]{3,2,1,0:T(8,128)} %bitcast.102, f32[8,20,64,80]{3,2,1,0:T(8,128)} %bitcast.103, bf16[8,64,128]{2,1,0:T(8,128)(2,1)} %copy-done.2, bf16[8,64,128]{2,1,0:T(8,128)(2,1)} %copy-done.3), custom_call_target="tpu_custom_call" | custom-call | flops 1000000 | bytes 2000000 | tf_op jit(solution)/shard_map/edge_rows/pallas_call | solution.py:435
  72.0 1.1 collective-permute-start.2
  73.1 0.6 collective-permute-start.3
  73.7 0.7 copy.38
  74.4 3.4 %all-to-all-start.1 = ((f32[8,48,128]{2,1,0:T(8,128)}), f32[8,48,128]{2,1,0:T(8,128)S(1)}, u32[]{:S(2)}, u32[]{:S(2)}) async-start(f32[8,48,128]{2,1,0:T(8,128)} %copy.38), calls=%async_computation.1 | async-start | bytes 393216 | tf_op jit(solution)/shard_map/all_to_all | solution.py:560
  77.8 2.6 %fusion.62 = (bf16[3,4,32,1280]{3,2,1,0:T(8,128)(2,1)}, f32[3,4,32,1280]{3,2,1,0:T(8,128)}) fusion(f32[32]{0:T(128)S(1)} %copy-done.8, bf16[3,4,32,1280]{3,2,1,0:T(8,128)(2,1)S(1)} %bitcast.112, f32[32,32]{1,0:T(8,128)S(1)} %copy-done), kind=kOutput, calls=%fused_computation.105 | convolution fusion | flops 189726720 | bytes 3936384 | tf_op jit(solution)/shard_map/ef,gqfj->gqej/dot_general | solution.py:578
  80.4 2.9 %all-to-all-done.1 = f32[8,48,128]{2,1,0:T(8,128)S(1)} async-done(((f32[8,48,128]{2,1,0:T(8,128)}), f32[8,48,128]{2,1,0:T(8,128)S(1)}, u32[]{:S(2)}, u32[]{:S(2)}) %all-to-all-start.1) | async-done | bytes 196640 | tf_op jit(solution)/shard_map/all_to_all | solution.py:560
  83.3 0.7 copy.59
  84.0 0.7 copy-done.4
  84.8 12.4 %chemistry.1 = (f32[8,20,64,80]{3,2,1,0:T(8,128)}, f32[8,24,128]{2,1,0:T(8,128)}) custom-call(s32[1]{0:T(128)} %bitcast.23.first_ref, f32[8,20,64,80]{3,2,1,0:T(8,128)} %bitcast.104, bf16[8,2,64,128]{3,2,1,0:T(8,128)(2,1)} %copy-done.4, bf16[8,2,64,128]{3,2,1,0:T(8,128)(2,1)} %copy-done.5, bf16[8,64,128]{2,1,0:T(8,128)(2,1)} %copy-done.2, ...), custom_call_target="tpu_custom_call" | custom-call | flops 1000000000 | bytes 16000000 | tf_op jit(solution)/shard_map/chemistry/pallas_call | solution.py:463
  97.2 1.6 copy.41
  98.7 4.1 %all-to-all-start.2 = ((f32[8,24,128]{2,1,0:T(8,128)}), f32[8,24,128]{2,1,0:T(8,128)S(1)}, u32[]{:S(2)}, u32[]{:S(2)}) async-start(f32[8,24,128]{2,1,0:T(8,128)} %bitcast.36), calls=%async_computation.2 | async-start | bytes 196608 | tf_op jit(solution)/shard_map/all_to_all | solution.py:567
  102.9 1.9 %fusion.63 = (bf16[3,4,32,1280]{3,2,1,0:T(8,128)(2,1)}, f32[3,4,32,1280]{3,2,1,0:T(8,128)S(1)}) fusion(f32[32]{0:T(128)S(1)} %copy-done.8, bf16[3,4,32,1280]{3,2,1,0:T(8,128)(2,1)S(1)} %select_convert_fusion.2, f32[32,32]{1,0:T(8,128)S(1)} %copy-done), kind=kOutput, calls=%fused_computation.106 | convolution fusion | flops 189726720 | bytes 3936384 | tf_op jit(solution)/shard_map/ef,gqfj->gqej/dot_general | solution.py:578
  104.8 1.9 %slice.46 = f32[3,4,8,1280]{3,2,1,0:T(8,128)} slice(f32[3,4,32,1280]{3,2,1,0:T(8,128)} %get-tuple-element.27), slice={[0:3], [0:4], [16:24], [0:1280]} | slice | bytes 983040 | tf_op jit(solution)/shard_map/slice | solution.py:582
  106.7 0.8 slice.47
  107.5 0.5 all-to-all-done.2
  108.0 2.7 %fusion.refs_4_ = f32[48,2560]{1,0:T(8,128)} fusion(s32[2560]{0:T(1024)S(1)} %pad_add_fusion, s32[1024]{0:T(1024)S(1)} %select_bitcast_fusion, bf16[24,1024]{1,0:T(8,128)(2,1)S(1)} %fusion.28, bf16[24,1024]{1,0:T(8,128)(2,1)S(1)} %bitcast_convert_fusion), kind=kOutput, calls=%fused_computation | convolution fusion | flops 254476288 | bytes 604160 | tf_op jit(solution)/shard_map/dot_general | solution.py:573
  110.7 13.3 %grid_to_pieces.1 = bf16[128,64,128]{2,1,0:T(8,128)(2,1)} custom-call(bf16[2560,1408]{1,0:T(8,128)(2,1)} %fourier_table.1.table_ref, bf16[384,1280]{1,0:T(8,128)(2,1)} %bitcast.113, bf16[384,1280]{1,0:T(8,128)(2,1)} %bitcast.114, f32[96,1280]{1,0:T(8,128)} %bitcast.115, f32[96,1280]{1,0:T(8,128)} %bitcast.116, f32[48,2560]{1,0:T(8,128)} %fusion.refs_4_), custom_call_target="tpu_custom_call" | custom-call | flops 2768240640 | bytes 12208960 | tf_op jit(solution)/shard_map/grid_to_pieces/pallas_call | solution.py:290
  124.0 10.2 %all-to-all-start.3 = ((bf16[128,64,128]{2,1,0:T(8,128)(2,1)}), bf16[128,64,128]{2,1,0:T(8,128)(2,1)S(1)}, u32[]{:S(2)}, u32[]{:S(2)}) async-start(bf16[128,64,128]{2,1,0:T(8,128)(2,1)} %grid_to_pieces.1), calls=%async_computation.3 | async-start | bytes 4194304 | tf_op jit(solution)/shard_map/all_to_all | solution.py:585
  134.2 0.7 reshape.275.weights_ref
  135.0 29.5 %all-to-all-done.3.values_ref = bf16[128,64,128]{2,1,0:T(8,128)(2,1)S(1)} async-done(((bf16[128,64,128]{2,1,0:T(8,128)(2,1)}), bf16[128,64,128]{2,1,0:T(8,128)(2,1)S(1)}, u32[]{:S(2)}, u32[]{:S(2)}) %all-to-all-start.3) | async-done | bytes 2097184 | tf_op jit(solution)/shard_map/all_to_all | solution.py:585
  164.5 1.3 copy-done.1
  165.8 13.2 %to_spectral.1 = bf16[10,64,1280]{2,1,0:T(8,128)(2,1)} custom-call(s32[1]{0:T(128)} %bitcast.first_ref, bf16[128,64,128]{2,1,0:T(8,128)(2,1)} %copy-done.1, f32[160,4]{1,0:T(8,128)} %reshape.275.weights_ref, bf16[10,640,1280]{2,1,0:T(8,128)(2,1)} %leg_ref.3), custom_call_target="tpu_custom_call" | custom-call | flops 2097152000 | bytes 21384000 | tf_op jit(solution)/shard_map/to_spectral/pallas_call | solution.py:201
  (49 shorter events, 1.3 us)
Async XLA Ops:
  0.6 77.2 %copy-start = (f32[32,32]{1,0:T(8,128)S(1)}, f32[32,32]{1,0:T(8,128)}, u32[]{:S(2)}) copy-start(f32[32,32]{1,0:T(8,128)} %param.11) | copy-start | bytes 12292
  18.0 41.9 %all-to-all-start = ((bf16[128,64,128]{2,1,0:T(8,128)(2,1)}), bf16[128,64,128]{2,1,0:T(8,128)(2,1)S(1)}, u32[]{:S(2)}, u32[]{:S(2)}) async-start(bf16[128,64,128]{2,1,0:T(8,128)(2,1)} %to_latitude.1), calls=%async_computation | async-start | bytes 4194304 | tf_op jit(solution)/shard_map/all_to_all | solution.py:527
  29.5 11.3 %copy-start.9 = (f32[64]{0:T(128)S(1)}, f32[64]{0:T(128)}, u32[]{:S(2)}) copy-start(f32[64]{0:T(128)} %param.15) | copy-start | bytes 772
  34.3 34.9 %collective-permute-start = (bf16[8,64,128]{2,1,0:T(8,128)(2,1)}, bf16[8,64,128]{2,1,0:T(8,128)(2,1)S(1)}, u32[]{:S(2)}, u32[]{:S(2)}) collective-permute-start(bf16[8,64,128]{2,1,0:T(8,128)(2,1)} %get-tuple-element.11), channel_id=1, source_target_pairs={{0,1},{1,2},{2,3},{3,4},{4,5},{5,6},{6,7},{7,0},{8,9},{9,10},{10,1... | collective-permute-start | bytes 393224 | tf_op jit(solution)/shard_map/ppermute | solution.py:413
  35.8 33.4 %collective-permute-start.1 = (bf16[8,64,128]{2,1,0:T(8,128)(2,1)}, bf16[8,64,128]{2,1,0:T(8,128)(2,1)S(1)}, u32[]{:S(2)}, u32[]{:S(2)}) collective-permute-start(bf16[8,64,128]{2,1,0:T(8,128)(2,1)} %get-tuple-element.12), channel_id=1, source_target_pairs={{0,7},{1,0},{2,1},{3,2},{4,3},{5,4},{6,5},{7,6},{8,15},{9,8},{10,9... | collective-permute-start | bytes 393224 | tf_op jit(solution)/shard_map/ppermute | solution.py:413
  42.3 5.3 %copy-start.6 = (f32[64,64]{1,0:T(8,128)S(1)}, f32[64,64]{1,0:T(8,128)}, u32[]{:S(2)}) copy-start(f32[64,64]{1,0:T(8,128)} %param.14) | copy-start | bytes 49156
  59.9 2.2 %slice-start = ((s8[7208960]{0:T(1024)(128)(4,1)}), s8[4194304]{0:T(1024)(128)(4,1)S(1)}, s32[]{:S(2)}) async-start(s8[7208960]{0:T(1024)(128)(4,1)} %bitcast.105), calls=%async_computation.4 | async-start | bytes 8388608
  60.2 2.9 %slice-start.1 = ((s8[7208960]{0:T(1024)(128)(4,1)}), s8[3014656]{0:T(1024)(128)(4,1)S(1)}, s32[]{:S(2)}) async-start(s8[7208960]{0:T(1024)(128)(4,1)} %bitcast.105), calls=%async_computation.5 | async-start | bytes 6029312
  69.2 0.7 copy-start.2
  69.2 0.7 copy-start.3
  69.9 7.9 %copy-start.8 = (f32[32]{0:T(128)S(1)}, f32[32]{0:T(128)}, u32[]{:S(2)}) copy-start(f32[32]{0:T(128)} %param.12) | copy-start | bytes 388
  72.0 12.0 %collective-permute-start.2 = (bf16[8,2,64,128]{3,2,1,0:T(8,128)(2,1)}, bf16[8,2,64,128]{3,2,1,0:T(8,128)(2,1)S(1)}, u32[]{:S(2)}, u32[]{:S(2)}) collective-permute-start(bf16[8,2,64,128]{3,2,1,0:T(8,128)(2,1)} %get-tuple-element.15), channel_id=1, source_target_pairs={{0,8},{8,16},{16,24},{24,32},{32,40},{40,48},{48,56},{56,64},{64,7... | collective-permute-start | bytes 786440 | tf_op jit(solution)/shard_map/ppermute | solution.py:413
  73.1 10.9 %collective-permute-start.3 = (bf16[8,2,64,128]{3,2,1,0:T(8,128)(2,1)}, bf16[8,2,64,128]{3,2,1,0:T(8,128)(2,1)S(1)}, u32[]{:S(2)}, u32[]{:S(2)}) collective-permute-start(bf16[8,2,64,128]{3,2,1,0:T(8,128)(2,1)} %get-tuple-element.16), channel_id=1, source_target_pairs={{0,120},{8,0},{16,8},{24,16},{32,24},{40,32},{48,40},{56,48},{64,5... | collective-permute-start | bytes 786440 | tf_op jit(solution)/shard_map/ppermute | solution.py:413
  74.4 8.9 %all-to-all-start.1 = ((f32[8,48,128]{2,1,0:T(8,128)}), f32[8,48,128]{2,1,0:T(8,128)S(1)}, u32[]{:S(2)}, u32[]{:S(2)}) async-start(f32[8,48,128]{2,1,0:T(8,128)} %copy.38), calls=%async_computation.1 | async-start | bytes 393216 | tf_op jit(solution)/shard_map/all_to_all | solution.py:560
  84.0 0.7 copy-start.4
  84.0 0.8 copy-start.5
  98.7 9.3 %all-to-all-start.2 = ((f32[8,24,128]{2,1,0:T(8,128)}), f32[8,24,128]{2,1,0:T(8,128)S(1)}, u32[]{:S(2)}, u32[]{:S(2)}) async-start(f32[8,24,128]{2,1,0:T(8,128)} %bitcast.36), calls=%async_computation.2 | async-start | bytes 196608 | tf_op jit(solution)/shard_map/all_to_all | solution.py:567
  124.0 10.2 %copy-start.7 = (f32[640]{0:T(1024)S(1)}, f32[640]{0:T(1024)}, u32[]{:S(2)}) copy-start(f32[640]{0:T(1024)} %param.10) | copy-start | bytes 7684
  124.0 40.4 %all-to-all-start.3 = ((bf16[128,64,128]{2,1,0:T(8,128)(2,1)}), bf16[128,64,128]{2,1,0:T(8,128)(2,1)S(1)}, u32[]{:S(2)}, u32[]{:S(2)}) async-start(bf16[128,64,128]{2,1,0:T(8,128)(2,1)} %grid_to_pieces.1), calls=%async_computation.3 | async-start | bytes 4194304 | tf_op jit(solution)/shard_map/all_to_all | solution.py:585
  164.5 1.3 copy-start.1

commit v5 on v4

--- a/solution.py
+++ b/solution.py
@@ -16,7 +16,7 @@
 LANES = 128
 FOLD = HALF + LANES
 PIECE_ROWS = 64
-DEPTH = 3
+DEPTH = 4
 UNIT = 8
 HALO = 2
 BF, F32 = jnp.bfloat16, jnp.float32

time: 180 us -> 180 us (level)
  no operation moved by 1% of the time
where the time goes in v5:
time: 180 us; the launch traced here: 179 us
  Pallas kernels  68.4 us (38%)
  waiting for transfers between devices  44.4 us (25%)
  starting transfers between devices  34.7 us (19%)
  local copies, waits for them, and re-layouts  13.3 us (7%)
  matrix products  12.4 us (7%)
  other arithmetic  4.99 us (3%)
    pallas_call x2, Pallas kernels, legendre_call(): pl.pallas_call(functools.partial(kernel, geometry), grid=(m_count,), in_s...  30.6 us
    all_to_all x1, waiting for transfers between devices, body(): lax.all_to_all(coeffs, both, split_axis=0, concat_axis=0, tiled=True)  29.5 us
    pallas_call x1, Pallas kernels, grid_to_pieces(): pl.pallas_call(functools.partial(grid_kernel, owners, steps), grid=(steps...  13.3 us
    pallas_call x1, Pallas kernels, chemistry(): pl.pallas_call(functools.partial(chemistry_kernel, total_rows), grid=(lev...  12.4 us
    all_to_all x1, starting transfers between devices, body(): lax.all_to_all(pieces, both, split_axis=0, concat_axis=0, tiled=True)  11.5 us
    all_to_all x1, waiting for transfers between devices, body(): lax.all_to_all(pieces, both, split_axis=0, concat_axis=0, tiled=True)  11.5 us
    all_to_all x1, starting transfers between devices, body(): lax.all_to_all(coeffs, both, split_axis=0, concat_axis=0, tiled=True)  10.2 us
    ppermute x4, starting transfers between devices, shift(): lax.ppermute(value, axis, [(i, (i + by) % count) for i in range(count)])  5.46 us
  transfers between devices with their start and end apart: 8, of which 4 were waited for; matrix products, arithmetic and copies ran while one was open for 12% of the time, Pallas kernels for 6%

profile of v5, /device:TPU:1, one launch (start us, length us, event | category | flops | bytes accessed | tf_op | source)
XLA Modules:
  0.0 179.3 jit_solution(11011874562776006578)
XLA Ops:
  0.7 17.4 %to_latitude.1 = bf16[128,64,128]{2,1,0:T(8,128)(2,1)} custom-call(s32[1]{0:T(128)} %bitcast.first_ref, bf16[10,64,1280]{2,1,0:T(8,128)(2,1)} %bitcast.119, bf16[10,640,1280]{2,1,0:T(8,128)(2,1)} %leg_ref.3), custom_call_target="tpu_custom_call" | custom-call | flops 2097152000 | bytes 21384000 | tf_op jit(solution)/shard_map/to_latitude/pallas_call | solution.py:201
  18.1 11.5 %all-to-all-start = ((bf16[128,64,128]{2,1,0:T(8,128)(2,1)}), bf16[128,64,128]{2,1,0:T(8,128)(2,1)S(1)}, u32[]{:S(2)}, u32[]{:S(2)}) async-start(bf16[128,64,128]{2,1,0:T(8,128)(2,1)} %to_latitude.1), calls=%async_computation | async-start | bytes 4194304 | tf_op jit(solution)/shard_map/all_to_all | solution.py:527
  29.6 4.8 %edge_columns.1 = (bf16[8,64,128]{2,1,0:T(8,128)(2,1)}, bf16[8,64,128]{2,1,0:T(8,128)(2,1)}) custom-call(f32[8,20,64,80]{3,2,1,0:T(8,128)} %bitcast.101), custom_call_target="tpu_custom_call" | custom-call | flops 10000000 | bytes 7000000 | tf_op jit(solution)/shard_map/edge_columns/pallas_call | solution.py:419
  34.4 1.5 collective-permute-start
  35.9 2.3 %collective-permute-start.1 = (bf16[8,64,128]{2,1,0:T(8,128)(2,1)}, bf16[8,64,128]{2,1,0:T(8,128)(2,1)S(1)}, u32[]{:S(2)}, u32[]{:S(2)}) collective-permute-start(bf16[8,64,128]{2,1,0:T(8,128)(2,1)} %get-tuple-element.12), channel_id=1, source_target_pairs={{0,7},{1,0},{2,1},{3,2},{4,3},{5,4},{6,5},{7,6},{8,15},{9,8},{10,9... | collective-permute-start | bytes 393224 | tf_op jit(solution)/shard_map/ppermute | solution.py:413
  38.2 0.4 fusion.38
  38.6 0.4 cosine_bitcast_fusion
  39.1 1.1 broadcast_multiply_fusion
  40.2 0.8 maximum_multiply_fusion.a_ref
  40.9 0.7 copy.40.heat_ref
  41.6 0.8 copy_multiply_fusion.b_ref
  42.4 5.2 %fourier_table.1.table_ref = bf16[2560,1408]{1,0:T(8,128)(2,1)} custom-call(f32[128,128]{1,0:T(8,128)} %get-tuple-element.25.cos_ref, f32[128,128]{1,0:T(8,128)} %get-tuple-element.24.sin_ref, f32[128,128]{1,0:T(8,128)} %get-tuple-element.23.turned_cos_ref, f32[128,128]{1,0:T(8,128)} %get-tuple-element.22.turned_sin_ref, ...), custom_call_target="tpu_custom_call" | custom-call | flops 10813440 | bytes 7208960 | tf_op jit(solution)/shard_map/fourier_table/pallas_call | solution.py:59
  47.7 0.7 pad_maximum_fusion.2.react_ref
  48.6 11.5 %all-to-all-done = bf16[128,64,128]{2,1,0:T(8,128)(2,1)S(1)} async-done(((bf16[128,64,128]{2,1,0:T(8,128)(2,1)}), bf16[128,64,128]{2,1,0:T(8,128)(2,1)S(1)}, u32[]{:S(2)}, u32[]{:S(2)}) %all-to-all-start) | async-done | bytes 2097184 | tf_op jit(solution)/shard_map/all_to_all | solution.py:527
  60.0 0.2 slice_bitcast_fusion
  60.5 0.4 copy.36
  61.0 0.2 pad_maximum_fusion
  61.2 1.1 slice-done
  62.2 1.0 slice-done.1
  63.2 3.3 %fusion.18 = f32[2,3,128,1408]{3,2,1,0:T(8,128)S(1)} fusion(bf16[2,1280,1408,1]{2,1,3,0:T(8,128)(2,1)S(1)} %bitcast.107, bf16[3,2,1280,128]{3,2,1,0:T(8,128)(2,1)S(1)} %bitcast.108), kind=kOutput, calls=%fused_computation.22 | convolution fusion | flops 2768240640 | bytes 13500416 | tf_op jit(solution)/shard_map/gckn,ckj->cgnj/dot_general | solution.py:538
  66.5 0.2 add_convert_fusion
  66.7 0.2 slice_subtract_fusion
  67.1 1.0 fusion.20
  68.3 0.9 fusion.23
  69.4 0.6 copy-done.2
  70.0 2.1 %edge_rows.1 = (bf16[8,2,64,128]{3,2,1,0:T(8,128)(2,1)}, bf16[8,2,64,128]{3,2,1,0:T(8,128)(2,1)}) custom-call(f32[8,20,64,80]{3,2,1,0:T(8,128)} %bitcast.102, f32[8,20,64,80]{3,2,1,0:T(8,128)} %bitcast.103, bf16[8,64,128]{2,1,0:T(8,128)(2,1)} %copy-done.2, bf16[8,64,128]{2,1,0:T(8,128)(2,1)} %copy-done.3), custom_call_target="tpu_custom_call" | custom-call | flops 1000000 | bytes 2000000 | tf_op jit(solution)/shard_map/edge_rows/pallas_call | solution.py:435
  72.1 1.1 collective-permute-start.2
  73.2 0.6 collective-permute-start.3
  73.8 0.7 copy.38
  74.5 3.4 %all-to-all-start.1 = ((f32[8,48,128]{2,1,0:T(8,128)}), f32[8,48,128]{2,1,0:T(8,128)S(1)}, u32[]{:S(2)}, u32[]{:S(2)}) async-start(f32[8,48,128]{2,1,0:T(8,128)} %copy.38), calls=%async_computation.1 | async-start | bytes 393216 | tf_op jit(solution)/shard_map/all_to_all | solution.py:560
  77.9 2.6 %fusion.62 = (bf16[3,4,32,1280]{3,2,1,0:T(8,128)(2,1)}, f32[3,4,32,1280]{3,2,1,0:T(8,128)}) fusion(f32[32]{0:T(128)S(1)} %copy-done.8, bf16[3,4,32,1280]{3,2,1,0:T(8,128)(2,1)S(1)} %bitcast.112, f32[32,32]{1,0:T(8,128)S(1)} %copy-done), kind=kOutput, calls=%fused_computation.105 | convolution fusion | flops 189726720 | bytes 3936384 | tf_op jit(solution)/shard_map/ef,gqfj->gqej/dot_general | solution.py:578
  80.5 2.9 %all-to-all-done.1 = f32[8,48,128]{2,1,0:T(8,128)S(1)} async-done(((f32[8,48,128]{2,1,0:T(8,128)}), f32[8,48,128]{2,1,0:T(8,128)S(1)}, u32[]{:S(2)}, u32[]{:S(2)}) %all-to-all-start.1) | async-done | bytes 196640 | tf_op jit(solution)/shard_map/all_to_all | solution.py:560
  83.4 0.7 copy.59
  84.1 0.7 copy-done.4
  84.9 12.4 %chemistry.1 = (f32[8,20,64,80]{3,2,1,0:T(8,128)}, f32[8,24,128]{2,1,0:T(8,128)}) custom-call(s32[1]{0:T(128)} %bitcast.23.first_ref, f32[8,20,64,80]{3,2,1,0:T(8,128)} %bitcast.104, bf16[8,2,64,128]{3,2,1,0:T(8,128)(2,1)} %copy-done.4, bf16[8,2,64,128]{3,2,1,0:T(8,128)(2,1)} %copy-done.5, bf16[8,64,128]{2,1,0:T(8,128)(2,1)} %copy-done.2, ...), custom_call_target="tpu_custom_call" | custom-call | flops 1000000000 | bytes 16000000 | tf_op jit(solution)/shard_map/chemistry/pallas_call | solution.py:463
  97.3 1.6 copy.41
  98.8 4.1 %all-to-all-start.2 = ((f32[8,24,128]{2,1,0:T(8,128)}), f32[8,24,128]{2,1,0:T(8,128)S(1)}, u32[]{:S(2)}, u32[]{:S(2)}) async-start(f32[8,24,128]{2,1,0:T(8,128)} %bitcast.36), calls=%async_computation.2 | async-start | bytes 196608 | tf_op jit(solution)/shard_map/all_to_all | solution.py:567
  103.0 1.9 %fusion.63 = (bf16[3,4,32,1280]{3,2,1,0:T(8,128)(2,1)}, f32[3,4,32,1280]{3,2,1,0:T(8,128)S(1)}) fusion(f32[32]{0:T(128)S(1)} %copy-done.8, bf16[3,4,32,1280]{3,2,1,0:T(8,128)(2,1)S(1)} %select_convert_fusion.2, f32[32,32]{1,0:T(8,128)S(1)} %copy-done), kind=kOutput, calls=%fused_computation.106 | convolution fusion | flops 189726720 | bytes 3936384 | tf_op jit(solution)/shard_map/ef,gqfj->gqej/dot_general | solution.py:578
  104.9 1.9 %slice.46 = f32[3,4,8,1280]{3,2,1,0:T(8,128)} slice(f32[3,4,32,1280]{3,2,1,0:T(8,128)} %get-tuple-element.27), slice={[0:3], [0:4], [16:24], [0:1280]} | slice | bytes 983040 | tf_op jit(solution)/shard_map/slice | solution.py:582
  106.8 0.8 slice.47
  107.6 0.5 all-to-all-done.2
  108.2 2.7 %fusion.refs_4_ = f32[48,2560]{1,0:T(8,128)} fusion(s32[2560]{0:T(1024)S(1)} %pad_add_fusion, s32[1024]{0:T(1024)S(1)} %select_bitcast_fusion, bf16[24,1024]{1,0:T(8,128)(2,1)S(1)} %fusion.28, bf16[24,1024]{1,0:T(8,128)(2,1)S(1)} %bitcast_convert_fusion), kind=kOutput, calls=%fused_computation | convolution fusion | flops 254476288 | bytes 604160 | tf_op jit(solution)/shard_map/dot_general | solution.py:573
  110.9 13.3 %grid_to_pieces.1 = bf16[128,64,128]{2,1,0:T(8,128)(2,1)} custom-call(bf16[2560,1408]{1,0:T(8,128)(2,1)} %fourier_table.1.table_ref, bf16[384,1280]{1,0:T(8,128)(2,1)} %bitcast.113, bf16[384,1280]{1,0:T(8,128)(2,1)} %bitcast.114, f32[96,1280]{1,0:T(8,128)} %bitcast.115, f32[96,1280]{1,0:T(8,128)} %bitcast.116, f32[48,2560]{1,0:T(8,128)} %fusion.refs_4_), custom_call_target="tpu_custom_call" | custom-call | flops 2768240640 | bytes 12208960 | tf_op jit(solution)/shard_map/grid_to_pieces/pallas_call | solution.py:290
  124.2 10.2 %all-to-all-start.3 = ((bf16[128,64,128]{2,1,0:T(8,128)(2,1)}), bf16[128,64,128]{2,1,0:T(8,128)(2,1)S(1)}, u32[]{:S(2)}, u32[]{:S(2)}) async-start(bf16[128,64,128]{2,1,0:T(8,128)(2,1)} %grid_to_pieces.1), calls=%async_computation.3 | async-start | bytes 4194304 | tf_op jit(solution)/shard_map/all_to_all | solution.py:585
  134.3 0.7 reshape.275.weights_ref
  135.1 29.5 %all-to-all-done.3.values_ref = bf16[128,64,128]{2,1,0:T(8,128)(2,1)S(1)} async-done(((bf16[128,64,128]{2,1,0:T(8,128)(2,1)}), bf16[128,64,128]{2,1,0:T(8,128)(2,1)S(1)}, u32[]{:S(2)}, u32[]{:S(2)}) %all-to-all-start.3) | async-done | bytes 2097184 | tf_op jit(solution)/shard_map/all_to_all | solution.py:585
  164.6 1.3 copy-done.1
  165.9 13.2 %to_spectral.1 = bf16[10,64,1280]{2,1,0:T(8,128)(2,1)} custom-call(s32[1]{0:T(128)} %bitcast.first_ref, bf16[128,64,128]{2,1,0:T(8,128)(2,1)} %copy-done.1, f32[160,4]{1,0:T(8,128)} %reshape.275.weights_ref, bf16[10,640,1280]{2,1,0:T(8,128)(2,1)} %leg_ref.3), custom_call_target="tpu_custom_call" | custom-call | flops 2097152000 | bytes 21384000 | tf_op jit(solution)/shard_map/to_spectral/pallas_call | solution.py:201
  (49 shorter events, 1.3 us)
Async XLA Ops:
  0.6 77.3 %copy-start = (f32[32,32]{1,0:T(8,128)S(1)}, f32[32,32]{1,0:T(8,128)}, u32[]{:S(2)}) copy-start(f32[32,32]{1,0:T(8,128)} %param.11) | copy-start | bytes 12292
  18.1 41.9 %all-to-all-start = ((bf16[128,64,128]{2,1,0:T(8,128)(2,1)}), bf16[128,64,128]{2,1,0:T(8,128)(2,1)S(1)}, u32[]{:S(2)}, u32[]{:S(2)}) async-start(bf16[128,64,128]{2,1,0:T(8,128)(2,1)} %to_latitude.1), calls=%async_computation | async-start | bytes 4194304 | tf_op jit(solution)/shard_map/all_to_all | solution.py:527
  29.6 11.3 %copy-start.9 = (f32[64]{0:T(128)S(1)}, f32[64]{0:T(128)}, u32[]{:S(2)}) copy-start(f32[64]{0:T(128)} %param.15) | copy-start | bytes 772
  34.4 34.9 %collective-permute-start = (bf16[8,64,128]{2,1,0:T(8,128)(2,1)}, bf16[8,64,128]{2,1,0:T(8,128)(2,1)S(1)}, u32[]{:S(2)}, u32[]{:S(2)}) collective-permute-start(bf16[8,64,128]{2,1,0:T(8,128)(2,1)} %get-tuple-element.11), channel_id=1, source_target_pairs={{0,1},{1,2},{2,3},{3,4},{4,5},{5,6},{6,7},{7,0},{8,9},{9,10},{10,1... | collective-permute-start | bytes 393224 | tf_op jit(solution)/shard_map/ppermute | solution.py:413
  35.9 33.4 %collective-permute-start.1 = (bf16[8,64,128]{2,1,0:T(8,128)(2,1)}, bf16[8,64,128]{2,1,0:T(8,128)(2,1)S(1)}, u32[]{:S(2)}, u32[]{:S(2)}) collective-permute-start(bf16[8,64,128]{2,1,0:T(8,128)(2,1)} %get-tuple-element.12), channel_id=1, source_target_pairs={{0,7},{1,0},{2,1},{3,2},{4,3},{5,4},{6,5},{7,6},{8,15},{9,8},{10,9... | collective-permute-start | bytes 393224 | tf_op jit(solution)/shard_map/ppermute | solution.py:413
  42.4 5.3 %copy-start.6 = (f32[64,64]{1,0:T(8,128)S(1)}, f32[64,64]{1,0:T(8,128)}, u32[]{:S(2)}) copy-start(f32[64,64]{1,0:T(8,128)} %param.14) | copy-start | bytes 49156
  60.0 2.2 %slice-start = ((s8[7208960]{0:T(1024)(128)(4,1)}), s8[4194304]{0:T(1024)(128)(4,1)S(1)}, s32[]{:S(2)}) async-start(s8[7208960]{0:T(1024)(128)(4,1)} %bitcast.105), calls=%async_computation.4 | async-start | bytes 8388608
  60.3 2.9 %slice-start.1 = ((s8[7208960]{0:T(1024)(128)(4,1)}), s8[3014656]{0:T(1024)(128)(4,1)S(1)}, s32[]{:S(2)}) async-start(s8[7208960]{0:T(1024)(128)(4,1)} %bitcast.105), calls=%async_computation.5 | async-start | bytes 6029312
  69.3 0.7 copy-start.2
  69.3 0.7 copy-start.3
  70.0 7.9 %copy-start.8 = (f32[32]{0:T(128)S(1)}, f32[32]{0:T(128)}, u32[]{:S(2)}) copy-start(f32[32]{0:T(128)} %param.12) | copy-start | bytes 388
  72.1 12.0 %collective-permute-start.2 = (bf16[8,2,64,128]{3,2,1,0:T(8,128)(2,1)}, bf16[8,2,64,128]{3,2,1,0:T(8,128)(2,1)S(1)}, u32[]{:S(2)}, u32[]{:S(2)}) collective-permute-start(bf16[8,2,64,128]{3,2,1,0:T(8,128)(2,1)} %get-tuple-element.15), channel_id=1, source_target_pairs={{0,8},{8,16},{16,24},{24,32},{32,40},{40,48},{48,56},{56,64},{64,7... | collective-permute-start | bytes 786440 | tf_op jit(solution)/shard_map/ppermute | solution.py:413
  73.2 10.9 %collective-permute-start.3 = (bf16[8,2,64,128]{3,2,1,0:T(8,128)(2,1)}, bf16[8,2,64,128]{3,2,1,0:T(8,128)(2,1)S(1)}, u32[]{:S(2)}, u32[]{:S(2)}) collective-permute-start(bf16[8,2,64,128]{3,2,1,0:T(8,128)(2,1)} %get-tuple-element.16), channel_id=1, source_target_pairs={{0,120},{8,0},{16,8},{24,16},{32,24},{40,32},{48,40},{56,48},{64,5... | collective-permute-start | bytes 786440 | tf_op jit(solution)/shard_map/ppermute | solution.py:413
  74.5 8.9 %all-to-all-start.1 = ((f32[8,48,128]{2,1,0:T(8,128)}), f32[8,48,128]{2,1,0:T(8,128)S(1)}, u32[]{:S(2)}, u32[]{:S(2)}) async-start(f32[8,48,128]{2,1,0:T(8,128)} %copy.38), calls=%async_computation.1 | async-start | bytes 393216 | tf_op jit(solution)/shard_map/all_to_all | solution.py:560
  84.1 0.7 copy-start.4
  84.1 0.8 copy-start.5
  98.8 9.3 %all-to-all-start.2 = ((f32[8,24,128]{2,1,0:T(8,128)}), f32[8,24,128]{2,1,0:T(8,128)S(1)}, u32[]{:S(2)}, u32[]{:S(2)}) async-start(f32[8,24,128]{2,1,0:T(8,128)} %bitcast.36), calls=%async_computation.2 | async-start | bytes 196608 | tf_op jit(solution)/shard_map/all_to_all | solution.py:567
  124.2 10.2 %copy-start.7 = (f32[640]{0:T(1024)S(1)}, f32[640]{0:T(1024)}, u32[]{:S(2)}) copy-start(f32[640]{0:T(1024)} %param.10) | copy-start | bytes 7684
  124.2 40.4 %all-to-all-start.3 = ((bf16[128,64,128]{2,1,0:T(8,128)(2,1)}), bf16[128,64,128]{2,1,0:T(8,128)(2,1)S(1)}, u32[]{:S(2)}, u32[]{:S(2)}) async-start(bf16[128,64,128]{2,1,0:T(8,128)(2,1)} %grid_to_pieces.1), calls=%async_computation.3 | async-start | bytes 4194304 | tf_op jit(solution)/shard_map/all_to_all | solution.py:585
  164.6 1.3 copy-start.1
